TPU v7x, 128 devices: a whole 4x4x4 slice. The times are simulated.
128 devices in a mesh: row: 8 (over x_hi, z), col: 16 (over y, x_lo, core).
Axes of the slice: x: 4 (x_hi: 2, x_lo: 2; x = x_hi * 2 + x_lo), y: 4, z: 4, core: 2. Of those that a mesh axis runs over, the one named last changes fastest.
Arguments:
- query_vectors: bfloat16 [4096, 16, 128], P('col', 'row'), may hold values from -68 to 68
- key_vectors: bfloat16 [4096, 16, 128], P('col', 'row'), may hold values from -6 to 6
- value_vectors: bfloat16 [4096, 16, 128], P('col', 'row'), may hold values from -6 to 6
- gate_logits: bfloat16 [4096, 16, 128], P('col', 'row'), may hold values from -6 to 6
- cotangent: bfloat16 [4096, 16, 128], P('col', 'row'), may hold values from -6 to 6
- pair_bias: bfloat16 [32, 4, 128, 16, 128], P('col'), may hold values from -6 to 6
- block_table: int32 [32, 16], P('col'), may hold values from 0 to 31, as said below
- valid_counts: int32 [32], P('col'), may hold values from 1 to 16
Outputs:
- query_grad: bfloat16 [4096, 16, 128], P('col', 'row')
- key_grad: bfloat16 [4096, 16, 128], P('col', 'row')
- value_grad: bfloat16 [4096, 16, 128], P('col', 'row')
- gate_grad: bfloat16 [4096, 16, 128], P('col', 'row')
- bias_grad: bfloat16 [32, 4, 128, 16, 128], P('col', None, None, 'row')
Inputs may be any that keep to these rules, and one draw needn't show every extreme that they name: `block_table`: each row holds 16 distinct block numbers; its first entry is the row's own block number.
All inputs are finite; a program needn't handle non-finite values.
Results may differ from a plain program's by a relative error of at most 0.03.
Values may be sent and summed in bfloat16 or wider, within the bound.
No kernel may reach another device: no remote copies, remote signals or barrier semaphores. Data moves between devices by JAX's collectives and lax.ppermute only.
A program may use at most 128 MiB of HBM per device.

v0:
```python
import math

import jax
import jax.numpy as jnp
from jax import lax
from jax.experimental import pallas as pl
from jax.experimental.pallas import tpu as pltpu
from jax.sharding import PartitionSpec as P


DH,BS,TAB=32,128,16
G=4
SCALE=DH**-0.5
LOG2E=math.log2(math.e)
F32=jnp.float32
BF=jnp.bfloat16
NT=(((1,),(1,)),((),()))
NN=(((1,),(0,)),((),()))


def dot(a,b,dims): return lax.dot_general(a,b,dims,preferred_element_type=F32)


def loop2(pairs,f):
    def two(k,c):
        f(2*k,0); f(2*k+1,0)
        return c
    lax.fori_loop(0,pairs//2,two,0)
    @pl.when(pairs%2==1)
    def _(): f(pairs-1,0)


def attend_kernel(first, *refs):
    idx,cnt,chk,q,gate,cot,bias=refs[:7]
    pieces=refs[7:15]
    k=15
    prev=None
    if not first: prev=refs[15:19]; k=19
    dq,gg,bg=refs[k:k+3]
    terms=refs[k+3:k+7]
    s_ref,e_ref,m_ref,l_ref,o_ref,off_ref,qm,qt,dom,domt,acc,kv,sem=refs[k+7:]
    for m in range(8):
        pltpu.make_async_copy(pieces[m],kv.at[pl.ds(4*m,4)],sem.at[m]).start()
    lane=lax.broadcasted_iota(jnp.int32,(BS,BS),1)//DH
    acc[...]=jnp.zeros(acc.shape,F32)
    for m in range(8):
        pltpu.make_async_copy(pieces[m],kv.at[pl.ds(4*m,4)],sem.at[m]).wait()
    def block(j,carry):
        n=cnt[j]
        pairs=(n+1)//2
        qj=q[j]
        for g in range(G):
            r=slice(g*BS,(g+1)*BS)
            v=jnp.where(lane==g,qj,jnp.zeros_like(qj))
            qm[r,:]=v
            qt[:,r]=v.T
        m_ref[...]=jnp.full(m_ref.shape,-jnp.inf,F32)
        l_ref[...]=jnp.zeros(l_ref.shape,F32)
        o_ref[...]=jnp.zeros(o_ref.shape,F32)
        def both(p,w):
            return jnp.concatenate([kv[idx[j,2*p],w],kv[idx[j,2*p+1],w]],0)
        def score(p,c):
            k2=both(p,0)
            S=dot(qm[...],k2,NT)*(SCALE*LOG2E)
            for h in range(2):
                b0=bias[j,h,2*p].astype(F32)*LOG2E
                b1=bias[j,h,2*p+1].astype(F32)*LOG2E
                b1=jnp.where(2*p+1<n,b1,-1e30)
                for i in range(2):
                    g=2*i+h
                    r=slice(g*BS,(g+1)*BS)
                    s=S[r,:]
                    s0=s[:,:BS]+b0; s1=s[:,BS:]+b1
                    s_ref[p,r,:BS]=s0
                    s_ref[p,r,BS:]=s1
                    m_ref[r,:]=jnp.maximum(m_ref[r,:],jnp.maximum(s0,s1))
            return c
        loop2(pairs,score)
        m_ref[...]=jnp.broadcast_to(jnp.max(m_ref[...],axis=1,keepdims=True),m_ref.shape)
        def attend(p,c):
            v2=both(p,1)
            for g in range(G):
                r=slice(g*BS,(g+1)*BS)
                m=m_ref[r,:]
                e0=jnp.exp2(s_ref[p,r,:BS]-m); e1=jnp.exp2(s_ref[p,r,BS:]-m)
                l_ref[r,:]+=e0+e1
                e=jnp.concatenate([e0.astype(BF),e1.astype(BF)],1)
                e_ref[p,r,:]=e
            o_ref[...]+=dot(e_ref[p],v2,NN)
            return c
        loop2(pairs,attend)
        att=jnp.zeros((BS,BS),F32); inv=[]
        for g in range(G):
            r=slice(g*BS,(g+1)*BS)
            inv.append(1.0/jnp.sum(l_ref[r,:],axis=1,keepdims=True))
            att=jnp.where(lane==g,o_ref[r,:]*inv[g],att)
        c=cot[j].astype(F32)
        opened=1.0/(1.0+jnp.exp(-gate[j].astype(F32)))
        gg[j]=(c*att*opened*(1.0-opened)).astype(BF)
        core=(c*opened).astype(BF).astype(F32)
        for g in range(G):
            r=slice(g*BS,(g+1)*BS)
            d=jnp.where(lane==g,core*inv[g],0.0).astype(BF)
            dom[r,:]=d
            domt[:,r]=d.T
            off_ref[r,:]=jnp.broadcast_to(jnp.sum(d.astype(F32)*att,axis=1,keepdims=True),(BS,BS))
        o_ref[...]=jnp.zeros(o_ref.shape,F32)
        def backward(p,c):
            a0=idx[j,2*p]; a1=idx[j,2*p+1]
            ch=chk[p]
            k2=both(p,0); v2=both(p,1)
            halves=[]; total=[None,None]
            WG=dot(dom[...],v2,NT)
            for g in range(G):
                r=slice(g*BS,(g+1)*BS); h=g%2
                off=off_ref[r,:]
                wg=WG[r,:]
                ds=e_ref[p,r,:].astype(F32)*(wg-jnp.concatenate([off,off],1))
                if g<2: total[h]=ds
                else:
                    b=(total[h]+ds).astype(BF)
                    bg[ch,j,h,0]=b[:,:BS]; bg[ch,j,h,1]=b[:,BS:]
                half=ds.astype(BF)
                halves.append(half)
            hs=jnp.concatenate(halves,0)
            o_ref[...]+=dot(hs,k2,NN)
            dk=dot(qt[...],hs,NN)
            dv=dot(domt[...],e_ref[p],NN)
            acc[a0,0]+=dk[:,:BS]; acc[a1,0]+=dk[:,BS:]
            acc[a0,1]+=dv[:,:BS]; acc[a1,1]+=dv[:,BS:]
            return c
        loop2(pairs,backward)
        def clear(p,c):
            z=jnp.zeros((2,2,BS,BS),BF)
            bg[chk[p],j]=z
            return c
        lax.fori_loop(pairs,8,clear,0)
        x=jnp.zeros((BS,BS),F32)
        for g in range(G):
            x=jnp.where(lane==g,o_ref[g*BS:(g+1)*BS,:],x)
        dq[j]=(x*SCALE).astype(BF)
        return carry
    lax.fori_loop(0,2,block,0)
    for dy in range(4):
        def store(b,c):
            a=acc[8*dy+b]
            if not first: a=a+prev[dy][b].astype(F32)
            terms[dy][b]=a.astype(BF)
            return c
        lax.fori_loop(0,8,store,0)


def attend_blocks(idx,cnt,chk,q,gate,cot,bias,pieces,prev):
    first=prev is None
    SM=pl.BlockSpec(memory_space=pltpu.SMEM)
    VM=pl.BlockSpec(memory_space=pltpu.VMEM)
    AN=pl.BlockSpec(memory_space=pl.ANY)
    args=[idx,cnt,chk,q,gate,cot,bias,*pieces]
    specs=[SM]*3+[VM]*4+[AN]*8
    if not first:
        args+=prev
        specs+=[VM]*4

    def kernel(*refs):
        attend_kernel(first,*refs)

    shapes=((2,BS,BS),(2,BS,BS),(8,2,2,2,BS,BS))+((8,2,BS,BS),)*4
    return pl.pallas_call(
        kernel,
        out_shape=tuple(jax.ShapeDtypeStruct(s,BF) for s in shapes),
        in_specs=specs,
        out_specs=(VM,)*7,
        scratch_shapes=[pltpu.VMEM((8,G*BS,2*BS),F32),pltpu.VMEM((8,G*BS,2*BS),BF)]
        +[pltpu.VMEM((G*BS,BS),F32)]*4
        +[pltpu.VMEM((G*BS,BS),BF),pltpu.VMEM((BS,G*BS),BF)]*2
        +[pltpu.VMEM((32,2,BS,BS),F32),pltpu.VMEM((32,2,BS,BS),BF),pltpu.SemaphoreType.DMA((8,))],
        compiler_params=pltpu.CompilerParams(vmem_limit_bytes=20<<20),
        cost_estimate=pl.CostEstimate(flops=10_000_000_000,bytes_accessed=24<<20,transcendentals=4<<20),
        name="attend_blocks",
    )(*args)


def join_kernel(p,xs,cs,xc,sel,k_out,v_out):
    for w,out in ((0,k_out),(1,v_out)):
        for b in range(2):
            own=p[b,w].astype(F32)+xs[b,w].astype(F32)
            far=cs[b,w].astype(F32)+xc[b,w].astype(F32)
            if w==0:
                own=own*SCALE
                far=far*SCALE
            both=jnp.concatenate([own.astype(BF).T,far.astype(BF).T],1)
            full=dot(both,sel[...],NT).astype(BF)
            out[0,b*BS:(b+1)*BS,:]=full[:,:BS]
            out[1,b*BS:(b+1)*BS,:]=full[:,BS:]


def unite_kernel(q,g,back,sel,q_out,g_out):
    for w,mine,out in ((0,q,q_out),(1,g,g_out)):
        for b in range(2):
            both=jnp.concatenate([mine[b],back[w,b]],1)
            full=dot(both,sel[...],NT).astype(BF)
            out[0,b*BS:(b+1)*BS,:]=full[:,:BS]
            out[1,b*BS:(b+1)*BS,:]=full[:,BS:]


def small_call(kernel,*args):
    VM=pl.BlockSpec(memory_space=pltpu.VMEM)
    return pl.pallas_call(
        kernel,
        out_shape=(jax.ShapeDtypeStruct((2,2*BS,BS),BF),)*2,
        in_specs=[VM]*len(args),
        out_specs=(VM,)*2,
        compiler_params=pltpu.CompilerParams(vmem_limit_bytes=8<<20),
        cost_estimate=pl.CostEstimate(flops=1<<28,bytes_accessed=1<<20,transcendentals=0),
    )(*args)


def to_col(x,dy,dx,dc):
    pairs=[]
    for s in range(16):
        sy,sx,sc=s//4,(s//2)%2,s%2
        pairs.append((s,((sy+dy)%4)*4+(sx^dx)*2+(sc^dc)))
    return lax.ppermute(x,"col",pairs)


def to_row(x,dx,dz):
    pairs=[(s,((s//4)^dx)*4+(s%4+dz)%4) for s in range(8)]
    return lax.ppermute(x,"row",pairs)


def swap(x):
    return to_col(x,0,0,1)


def plus(*terms):
    total=terms[0].astype(F32)
    for t in terms[1:]:
        total=total+t.astype(F32)
    return total


def body(
    query_vectors,
    key_vectors,
    value_vectors,
    gate_logits,
    cotangent,
    pair_bias,
    block_table,
    valid_counts,
):
    col=lax.axis_index("col")
    row=lax.axis_index("row")
    y,xl,core=col//4,(col//2)%2,col%2
    xh,z=row//4,row%4

    src=lax.broadcasted_iota(jnp.int32,(256,256),0)
    dst=lax.broadcasted_iota(jnp.int32,(256,256),1)
    want=((dst%BS)//64)*BS+((dst//BS)^core)*64+dst%64
    sel=lax.optimization_barrier((src==want).astype(BF))

    def split(x):
        both=lax.dot_general(x.reshape(2*BS,2*BS),sel,NN,preferred_element_type=F32).astype(BF)
        return both[:,:BS].reshape(2,BS,BS),both[:,BS:].reshape(2,BS,BS)

    k_mine,k_send=split(key_vectors)
    v_mine,v_send=split(value_vectors)
    shard=jnp.concatenate([jnp.stack([k_mine,v_mine],1),swap(jnp.stack([k_send,v_send],1))],0)
    shard,pair_bias=lax.optimization_barrier((shard,pair_bias))
    pieces=[]
    for dy in range(4):
        for dx in range(2):
            pieces.append(to_col(shard,(4-dy)%4,dx,0) if dy+dx else shard)

    table=jnp.concatenate([block_table,valid_counts[:,None]],1)
    tables=[table,swap(table)]

    def places(t):
        ids=t[:,:TAB]
        owner=ids//2
        chip=((owner//4-y)%4)*2+(((owner//2)%2)^xl)
        return chip*4+((owner%2)^core)*2+ids%2

    dest=jnp.arange(8,dtype=jnp.int32)
    far=(dest//4)^xh
    turn=(dest%4-z)%4

    bias=pair_bias.transpose(0,1,3,2,4)
    bias_mine=lax.dynamic_slice_in_dim(bias,2*core,2,1)
    bias_other=swap(lax.dynamic_slice_in_dim(bias,2-2*core,2,1))
    parts=[split(x) for x in (query_vectors,gate_logits,cotangent)]
    mine=[p[0] for p in parts]
    other=swap(jnp.stack([p[1] for p in parts],0))

    ready=(places(tables[0]),tables[0][:,TAB],places(tables[1]),tables[1][:,TAB],mine,other,bias_mine,bias_other,pieces)
    idx0,cnt0,idx1,cnt1,mine,other,bias_mine,bias_other,pieces=lax.optimization_barrier(ready)
    dq0,gg0,bg0,*terms=attend_blocks(idx0,cnt0,turn*2+far,*mine,bias_mine,pieces,None)
    bg0=bg0.reshape(4,2,2,2,2,BS,BS)
    bg0_in=[]
    for dz in range(1,4):
        bg0_in.append(to_row(bg0[dz],0,dz))
    dq1,gg1,bg1,*terms=attend_blocks(
        idx1,cnt1,far*4+turn,other[0],other[1],other[2],bias_other,pieces,terms
    )
    bg1=bg1.reshape(2,4,2,2,2,BS,BS)

    terms=[t.reshape(2,4,2,BS,BS) for t in terms]
    part=plus(terms[0],*[to_col(terms[dy],dy,0,0) for dy in range(1,4)]).astype(BF)
    bg1=plus(bg1[0],to_row(bg1[1],1,0)).astype(BF)
    bg0=plus(bg0[0],*bg0_in).astype(BF)
    bias1_in=[to_row(bg1[dz],0,dz) for dz in range(1,4)]
    bias0=plus(bg0[0],to_row(bg0[1],1,0)).astype(BF)
    bias1=plus(bg1[0],*bias1_in).astype(BF)
    bias_back=swap(bias1)

    q_back=swap(jnp.stack([dq1,gg1],0))
    query_grad,gate_grad=small_call(unite_kernel,dq0,gg0,q_back,sel)
    key_grad,value_grad=small_call(
        join_kernel,
        part[0,:2],
        to_col(part[1,:2],0,1,0),
        swap(part[0,2:]),
        to_col(part[1,2:],0,1,1),
        sel,
    )

    a=jnp.where(core==0,bias0,bias_back)
    b=jnp.where(core==0,bias_back,bias0)
    bias_grad=jnp.concatenate([a,b],1).transpose(0,1,3,2,4)

    def rows(x):
        return x.transpose(1,0,2)

    return rows(query_grad),rows(key_grad),rows(value_grad),rows(gate_grad),bias_grad


def solution(mesh):
    return jax.shard_map(
        body,
        mesh=mesh,
        in_specs=(
            P("col","row",None),
            P("col","row",None),
            P("col","row",None),
            P("col","row",None),
            P("col","row",None),
            P("col",None,None,None,None),
            P("col",None),
            P("col"),
        ),
        out_specs=(
            P("col","row",None),
            P("col","row",None),
            P("col","row",None),
            P("col","row",None),
            P("col",None,None,"row",None),
        ),
        check_vma=False,
    )
```

profile of v0, /device:TPU:0, one launch (start us, length us, event | category | flops | bytes accessed | tf_op | source)
XLA Modules:
  0.0 127.8 jit_solution(4255769951239666182)
XLA Ops:
  0.8 1.1 fusion.3
  1.9 1.1 fusion.4
  5.1 3.4 %copy.22 = bf16[2,4,128,16,128]{4,2,3,1,0:T(8,128)(2,1)S(1)} copy(bf16[2,4,128,16,128]{4,3,2,1,0:T(8,128)(2,1)} %param.13) | data formatting | bytes 8388608 | tf_op jit(solution)/shard_map/optimization_barrier | solution.py:269
  8.5 1.7 %dynamic-slice_bitcast_fusion = (bf16[2,2,16,128,128]{4,3,2,1,0:T(8,128)(2,1)}, bf16[2,2,16,128,128]{4,3,2,1,0:T(8,128)(2,1)S(1)}) fusion(bf16[2,4,128,16,128]{4,2,3,1,0:T(8,128)(2,1)S(1)} %copy.22, s32[]{:T(128)S(6)} %select_n.153, s32[]{:T(128)S(6)} %select_n.152), kind=kLoop, calls=%fused_computation.1 | loop fusion | bytes 8388616 | tf_op jit(solution)/shard_map/dynamic_slice | solution.py:290
  11.6 2.6 %collective-permute-start.10 = (bf16[4,2,128,128]{3,2,1,0:T(8,128)(2,1)S(1)}, bf16[4,2,128,128]{3,2,1,0:T(8,128)(2,1)S(1)}, u32[]{:S(2)}, u32[]{:S(2)}) collective-permute-start(bf16[4,2,128,128]{3,2,1,0:T(8,128)(2,1)S(1)} %pad_maximum_fusion.refs_7_), channel_id=1, source_target_pairs={{0,6},{1,7},{2,4},{3,5},{4,10},{5,11},{6,8},{7,9},{8,14},{9,15},{1... | collective-permute-start | bytes 786440 | tf_op jit(solution)/shard_map/ppermute | solution.py:223
  14.7 1.5 %collective-permute-start.5 = (bf16[4,2,128,128]{3,2,1,0:T(8,128)(2,1)S(1)}, bf16[4,2,128,128]{3,2,1,0:T(8,128)(2,1)S(1)}, u32[]{:S(2)}, u32[]{:S(2)}) collective-permute-start(bf16[4,2,128,128]{3,2,1,0:T(8,128)(2,1)S(1)} %pad_maximum_fusion.refs_7_), channel_id=1, source_target_pairs={{0,12},{1,13},{2,14},{3,15},{4,0},{5,1},{6,2},{7,3},{8,4},{9,5},{1... | collective-permute-start | bytes 786440 | tf_op jit(solution)/shard_map/ppermute | solution.py:223
  16.5 1.6 %collective-permute-done.1 = bf16[3,2,128,128]{3,2,1,0:T(8,128)(2,1)S(1)} collective-permute-done((bf16[3,2,128,128]{3,2,1,0:T(8,128)(2,1)}, bf16[3,2,128,128]{3,2,1,0:T(8,128)(2,1)S(1)}, u32[]{:S(2)}, u32[]{:S(2)}) %collective-permute-start.1) | collective-permute-done | bytes 196640 | tf_op jit(solution)/shard_map/ppermute | solution.py:223
  18.1 2.8 %collective-permute-start.6 = (bf16[4,2,128,128]{3,2,1,0:T(8,128)(2,1)S(1)}, bf16[4,2,128,128]{3,2,1,0:T(8,128)(2,1)S(1)}, u32[]{:S(2)}, u32[]{:S(2)}) collective-permute-start(bf16[4,2,128,128]{3,2,1,0:T(8,128)(2,1)S(1)} %pad_maximum_fusion.refs_7_), channel_id=1, source_target_pairs={{0,14},{1,15},{2,12},{3,13},{4,2},{5,3},{6,0},{7,1},{8,6},{9,7},{1... | collective-permute-start | bytes 786440 | tf_op jit(solution)/shard_map/ppermute | solution.py:223
  20.9 2.0 %collective-permute-done.10.refs_14_ = bf16[4,2,128,128]{3,2,1,0:T(8,128)(2,1)S(1)} collective-permute-done((bf16[4,2,128,128]{3,2,1,0:T(8,128)(2,1)S(1)}, bf16[4,2,128,128]{3,2,1,0:T(8,128)(2,1)S(1)}, u32[]{:S(2)}, u32[]{:S(2)}) %collective-permute-start.10) | collective-permute-done | bytes 262176 | tf_op jit(solution)/shard_map/ppermute | solution.py:223
  22.9 2.1 %collective-permute-start.7 = (bf16[4,2,128,128]{3,2,1,0:T(8,128)(2,1)S(1)}, bf16[4,2,128,128]{3,2,1,0:T(8,128)(2,1)S(1)}, u32[]{:S(2)}, u32[]{:S(2)}) collective-permute-start(bf16[4,2,128,128]{3,2,1,0:T(8,128)(2,1)S(1)} %pad_maximum_fusion.refs_7_), channel_id=1, source_target_pairs={{0,8},{1,9},{2,10},{3,11},{4,12},{5,13},{6,14},{7,15},{8,0},{9,1},... | collective-permute-start | bytes 786440 | tf_op jit(solution)/shard_map/ppermute | solution.py:223
  25.0 2.5 %collective-permute-done.4.refs_8_ = bf16[4,2,128,128]{3,2,1,0:T(8,128)(2,1)S(1)} collective-permute-done((bf16[4,2,128,128]{3,2,1,0:T(8,128)(2,1)S(1)}, bf16[4,2,128,128]{3,2,1,0:T(8,128)(2,1)S(1)}, u32[]{:S(2)}, u32[]{:S(2)}) %collective-permute-start.4) | collective-permute-done | bytes 262176 | tf_op jit(solution)/shard_map/ppermute | solution.py:223
  27.5 3.8 %collective-permute-start.8 = (bf16[4,2,128,128]{3,2,1,0:T(8,128)(2,1)S(1)}, bf16[4,2,128,128]{3,2,1,0:T(8,128)(2,1)S(1)}, u32[]{:S(2)}, u32[]{:S(2)}) collective-permute-start(bf16[4,2,128,128]{3,2,1,0:T(8,128)(2,1)S(1)} %pad_maximum_fusion.refs_7_), channel_id=1, source_target_pairs={{0,10},{1,11},{2,8},{3,9},{4,14},{5,15},{6,12},{7,13},{8,2},{9,3},... | collective-permute-start | bytes 786440 | tf_op jit(solution)/shard_map/ppermute | solution.py:223
  31.5 2.7 %collective-permute-done.6.refs_10_ = bf16[4,2,128,128]{3,2,1,0:T(8,128)(2,1)S(1)} collective-permute-done((bf16[4,2,128,128]{3,2,1,0:T(8,128)(2,1)S(1)}, bf16[4,2,128,128]{3,2,1,0:T(8,128)(2,1)S(1)}, u32[]{:S(2)}, u32[]{:S(2)}) %collective-permute-start.6) | collective-permute-done | bytes 262176 | tf_op jit(solution)/shard_map/ppermute | solution.py:223
  34.2 6.5 %collective-permute-done.8.refs_12_ = bf16[4,2,128,128]{3,2,1,0:T(8,128)(2,1)S(1)} collective-permute-done((bf16[4,2,128,128]{3,2,1,0:T(8,128)(2,1)S(1)}, bf16[4,2,128,128]{3,2,1,0:T(8,128)(2,1)S(1)}, u32[]{:S(2)}, u32[]{:S(2)}) %collective-permute-start.8) | collective-permute-done | bytes 262176 | tf_op jit(solution)/shard_map/ppermute | solution.py:223
  40.7 4.6 %collective-permute-done.9.refs_13_ = bf16[4,2,128,128]{3,2,1,0:T(8,128)(2,1)S(1)} collective-permute-done((bf16[4,2,128,128]{3,2,1,0:T(8,128)(2,1)S(1)}, bf16[4,2,128,128]{3,2,1,0:T(8,128)(2,1)S(1)}, u32[]{:S(2)}, u32[]{:S(2)}) %collective-permute-start.9) | collective-permute-done | bytes 262176 | tf_op jit(solution)/shard_map/ppermute | solution.py:223
  45.3 13.1 %attend_blocks.2 = (bf16[2,128,128]{2,1,0:T(8,128)(2,1)S(1)}, bf16[2,128,128]{2,1,0:T(8,128)(2,1)S(1)}, bf16[8,2,2,2,128,128]{5,4,3,2,1,0:T(8,128)(2,1)S(1)}, bf...) custom-call(s32[2,16]{1,0:T(2,128)S(1)} %fusion.36.refs_0_, ...), custom_call_target="tpu_custom_call" | custom-call | flops 10000000000 | bytes 25165824 | tf_op jit(solution)/shard_map/attend_blocks/pallas_call | solution.py:168
  58.5 2.0 %collective-permute-start.18 = (bf16[2,2,2,2,128,128]{5,4,3,2,1,0:T(8,128)(2,1)S(1)}, bf16[2,2,2,2,128,128]{5,4,3,2,1,0:T(8,128)(2,1)S(1)}, u32[]{:S(2)}, u32[]{:S(2)}) collective-permute-start(bf16[2,2,2,2,128,128]{5,4,3,2,1,0:T(8,128)(2,1)S(1)} %get-tuple-element.93), channel_id=1, source_target_pairs={{0,16},{16,32},{32,48},{48,0},{64,80},{80,96},{96,112},{112,64},{1... | collective-permute-start | bytes 1572872 | tf_op jit(solution)/shard_map/ppermute | solution.py:228
  60.5 3.6 %collective-permute-start.19 = (bf16[2,2,2,2,128,128]{5,4,3,2,1,0:T(8,128)(2,1)S(1)}, bf16[2,2,2,2,128,128]{5,4,3,2,1,0:T(8,128)(2,1)S(1)}, u32[]{:S(2)}, u32[]{:S(2)}) collective-permute-start(bf16[2,2,2,2,128,128]{5,4,3,2,1,0:T(8,128)(2,1)S(1)} %get-tuple-element.95), channel_id=1, source_target_pairs={{0,32},{16,48},{32,0},{48,16},{64,96},{80,112},{96,64},{112,80},{1... | collective-permute-start | bytes 1572872 | tf_op jit(solution)/shard_map/ppermute | solution.py:228
  65.1 9.3 %attend_blocks.3 = (bf16[2,128,128]{2,1,0:T(8,128)(2,1)S(1)}, bf16[2,128,128]{2,1,0:T(8,128)(2,1)S(1)}, bf16[8,2,2,2,128,128]{5,4,3,2,1,0:T(8,128)(2,1)S(1)}, bf...) custom-call(s32[2,16]{1,0:T(2,128)S(1)} %fusion.41.refs_0_, ...), custom_call_target="tpu_custom_call" | custom-call | flops 10000000000 | bytes 25165824 | tf_op jit(solution)/shard_map/attend_blocks/pallas_call | solution.py:168
  74.5 2.8 %collective-permute-start.22 = (bf16[4,2,2,2,128,128]{5,4,3,2,1,0:T(8,128)(2,1)S(1)}, bf16[4,2,2,2,128,128]{5,4,3,2,1,0:T(8,128)(2,1)S(1)}, u32[]{:S(2)}, u32[]{:S(2)}) collective-permute-start(bf16[4,2,2,2,128,128]{5,4,3,2,1,0:T(8,128)(2,1)S(1)} %slice.125), channel_id=1, source_target_pairs={{0,64},{16,80},{32,96},{48,112},{64,0},{80,16},{96,32},{112,48},{1... | collective-permute-start | bytes 3145736 | tf_op jit(solution)/shard_map/ppermute | solution.py:228
  77.3 2.8 %collective-permute-start.12 = (bf16[2,4,2,128,128]{4,3,2,1,0:T(8,128)(2,1)S(1)}, bf16[2,4,2,128,128]{4,3,2,1,0:T(8,128)(2,1)S(1)}, u32[]{:S(2)}, u32[]{:S(2)}) collective-permute-start(bf16[2,4,2,128,128]{4,3,2,1,0:T(8,128)(2,1)S(1)} %bitcast.111), channel_id=1, source_target_pairs={{0,4},{1,5},{2,6},{3,7},{4,8},{5,9},{6,10},{7,11},{8,12},{9,13},{1... | collective-permute-start | bytes 1572872 | tf_op jit(solution)/shard_map/ppermute | solution.py:223
  81.1 1.8 %collective-permute-start.14 = (bf16[2,4,2,128,128]{4,3,2,1,0:T(8,128)(2,1)S(1)}, bf16[2,4,2,128,128]{4,3,2,1,0:T(8,128)(2,1)S(1)}, u32[]{:S(2)}, u32[]{:S(2)}) collective-permute-start(bf16[2,4,2,128,128]{4,3,2,1,0:T(8,128)(2,1)S(1)} %bitcast.109), channel_id=1, source_target_pairs={{0,12},{1,13},{2,14},{3,15},{4,0},{5,1},{6,2},{7,3},{8,4},{9,5},{1... | collective-permute-start | bytes 1572872 | tf_op jit(solution)/shard_map/ppermute | solution.py:223
  84.0 15.4 %collective-permute-done.22 = bf16[4,2,2,2,128,128]{5,4,3,2,1,0:T(8,128)(2,1)S(1)} collective-permute-done((bf16[4,2,2,2,128,128]{5,4,3,2,1,0:T(8,128)(2,1)S(1)}, bf16[4,2,2,2,128,128]{5,4,3,2,1,0:T(8,128)(2,1)S(1)}, u32[]{:S(2)}, u32[]{:S(2)}) %collective-permute-start.22) | collective-permute-done | bytes 1048608 | tf_op jit(solution)/shard_map/ppermute | solution.py:228
  99.4 2.5 %collective-permute-start.21 = (bf16[2,2,2,128,128]{4,3,2,1,0:T(8,128)(2,1)}, bf16[2,2,2,128,128]{4,3,2,1,0:T(8,128)(2,1)}, u32[]{:S(2)}, u32[]{:S(2)}) collective-permute-start(bf16[2,2,2,128,128]{4,3,2,1,0:T(8,128)(2,1)} %slice_bitcast_fusion.4), channel_id=1, source_target_pairs={{0,64},{16,80},{32,96},{48,112},{64,0},{80,16},{96,32},{112,48},{1... | collective-permute-start | bytes 786440 | tf_op jit(solution)/shard_map/ppermute | solution.py:228
  102.3 1.1 collective-permute-start.23
  104.1 2.0 %collective-permute-start.25 = (bf16[2,2,2,128,128]{4,3,2,1,0:T(8,128)(2,1)S(1)}, bf16[2,2,2,128,128]{4,3,2,1,0:T(8,128)(2,1)S(1)}, u32[]{:S(2)}, u32[]{:S(2)}) collective-permute-start(bf16[2,2,2,128,128]{4,3,2,1,0:T(8,128)(2,1)S(1)} %get-tuple-element.99), channel_id=1, source_target_pairs={{0,48},{16,0},{32,16},{48,32},{64,112},{80,64},{96,80},{112,96},{1... | collective-permute-start | bytes 786440 | tf_op jit(solution)/shard_map/ppermute | solution.py:228
  106.5 7.7 %collective-permute-done.23 = bf16[2,2,2,128,128]{4,3,2,1,0:T(8,128)(2,1)S(1)} collective-permute-done((bf16[2,2,2,128,128]{4,3,2,1,0:T(8,128)(2,1)S(1)}, bf16[2,2,2,128,128]{4,3,2,1,0:T(8,128)(2,1)S(1)}, u32[]{:S(2)}, u32[]{:S(2)}) %collective-permute-start.23) | collective-permute-done | bytes 262176 | tf_op jit(solution)/shard_map/ppermute | solution.py:228
  115.8 1.6 %collective-permute-start.17 = (bf16[2,2,128,128]{3,2,1,0:T(8,128)(2,1)S(1)}, bf16[2,2,128,128]{3,2,1,0:T(8,128)(2,1)S(1)}, u32[]{:S(2)}, u32[]{:S(2)}) collective-permute-start(bf16[2,2,128,128]{3,2,1,0:T(8,128)(2,1)S(1)} %get-tuple-element.101), channel_id=1, source_target_pairs={{0,3},{1,2},{2,1},{3,0},{4,7},{5,6},{6,5},{7,4},{8,11},{9,10},{10,... | collective-permute-start | bytes 393224 | tf_op jit(solution)/shard_map/ppermute | solution.py:223
  119.2 2.3 %collective-permute-done.15.xs = bf16[2,2,128,128]{3,2,1,0:T(8,128)(2,1)S(1)} collective-permute-done((bf16[2,2,128,128]{3,2,1,0:T(8,128)(2,1)S(1)}, bf16[2,2,128,128]{3,2,1,0:T(8,128)(2,1)S(1)}, u32[]{:S(2)}, u32[]{:S(2)}) %collective-permute-start.15) | collective-permute-done | bytes 131104 | tf_op jit(solution)/shard_map/ppermute | solution.py:223
  121.5 1.8 %collective-permute-done.17.xc = bf16[2,2,128,128]{3,2,1,0:T(8,128)(2,1)S(1)} collective-permute-done((bf16[2,2,128,128]{3,2,1,0:T(8,128)(2,1)S(1)}, bf16[2,2,128,128]{3,2,1,0:T(8,128)(2,1)S(1)}, u32[]{:S(2)}, u32[]{:S(2)}) %collective-permute-start.17) | collective-permute-done | bytes 131104 | tf_op jit(solution)/shard_map/ppermute | solution.py:223
  125.3 1.1 broadcast_select_fusion.1
  126.5 1.3 %copy.28 = bf16[2,4,128,2,128]{4,3,2,1,0:T(2,128)(2,1)} copy(bf16[2,4,128,2,128]{4,2,3,1,0:T(8,128)(2,1)S(1)} %maximum_bitcast_fusion) | data formatting | bytes 1048576
  (85 shorter events, 14.6 us)
Async XLA Ops:
  3.0 2.1 %collective-permute-start.2 = (bf16[2,2,128,128]{3,2,1,0:T(8,128)(2,1)S(1)}, bf16[2,2,128,128]{3,2,1,0:T(8,128)(2,1)S(1)}, u32[]{:S(2)}, u32[]{:S(2)}) collective-permute-start(bf16[2,2,128,128]{3,2,1,0:T(8,128)(2,1)S(1)} %pad_maximum_fusion.2), channel_id=1, source_target_pairs={{0,1},{1,0},{2,3},{3,2},{4,5},{5,4},{6,7},{7,6},{8,9},{9,8},{10,11... | collective-permute-start | bytes 393224 | tf_op jit(solution)/shard_map/ppermute | solution.py:223
  4.6 11.7 %collective-permute-start = (s32[2,17]{1,0:T(2,128)S(1)}, s32[2,17]{1,0:T(2,128)S(1)}, u32[]{:S(2)}, u32[]{:S(2)}) collective-permute-start(s32[2,17]{1,0:T(2,128)S(1)} %pad_add_fusion), channel_id=1, source_target_pairs={{0,1},{1,0},{2,3},{3,2},{4,5},{5,4},{6,7},{7,6},{8,9},{9,8},{10,11... | collective-permute-start | bytes 416 | tf_op jit(solution)/shard_map/ppermute | solution.py:223
  8.5 2.1 %copy-start.5 = (bf16[256,2,128]{2,1,0:T(2,128)(2,1)S(1)}, bf16[256,2,128]{2,1,0:T(2,128)(2,1)}, u32[]{:S(2)}) copy-start(bf16[256,2,128]{2,1,0:T(2,128)(2,1)} %param.12) | copy-start | bytes 393220
  10.2 6.2 %copy-start.6 = (s32[2,16]{1,0:T(2,128)S(1)}, s32[2,16]{1,0:T(2,128)}, u32[]{:S(2)}) copy-start(s32[2,16]{1,0:T(2,128)} %param.14) | copy-start | bytes 388
  10.2 35.1 %copy-start = (s32[2]{0:T(128)S(1)}, s32[2]{0:T(128)}, u32[]{:S(2)}) copy-start(s32[2]{0:T(128)} %refs_1_) | copy-start | bytes 28
  10.2 35.1 %collective-permute-start.3 = (bf16[2,2,16,128,128]{4,3,2,1,0:T(8,128)(2,1)}, bf16[2,2,16,128,128]{4,3,2,1,0:T(8,128)(2,1)}, u32[]{:S(2)}, u32[]{:S(2)}) collective-permute-start(bf16[2,2,16,128,128]{4,3,2,1,0:T(8,128)(2,1)} %get-tuple-element.91), channel_id=1, source_target_pairs={{0,1},{1,0},{2,3},{3,2},{4,5},{5,4},{6,7},{7,6},{8,9},{9,8},{10,11... | collective-permute-start | bytes 6291464 | tf_op jit(solution)/shard_map/ppermute | solution.py:223
  11.6 11.3 %collective-permute-start.10 = (bf16[4,2,128,128]{3,2,1,0:T(8,128)(2,1)S(1)}, bf16[4,2,128,128]{3,2,1,0:T(8,128)(2,1)S(1)}, u32[]{:S(2)}, u32[]{:S(2)}) collective-permute-start(bf16[4,2,128,128]{3,2,1,0:T(8,128)(2,1)S(1)} %pad_maximum_fusion.refs_7_), channel_id=1, source_target_pairs={{0,6},{1,7},{2,4},{3,5},{4,10},{5,11},{6,8},{7,9},{8,14},{9,15},{1... | collective-permute-start | bytes 786440 | tf_op jit(solution)/shard_map/ppermute | solution.py:223
  14.2 13.3 %collective-permute-start.4 = (bf16[4,2,128,128]{3,2,1,0:T(8,128)(2,1)S(1)}, bf16[4,2,128,128]{3,2,1,0:T(8,128)(2,1)S(1)}, u32[]{:S(2)}, u32[]{:S(2)}) collective-permute-start(bf16[4,2,128,128]{3,2,1,0:T(8,128)(2,1)S(1)} %pad_maximum_fusion.refs_7_), channel_id=1, source_target_pairs={{0,2},{1,3},{2,0},{3,1},{4,6},{5,7},{6,4},{7,5},{8,10},{9,11},{10,... | collective-permute-start | bytes 786440 | tf_op jit(solution)/shard_map/ppermute | solution.py:223
  14.7 16.6 %collective-permute-start.5 = (bf16[4,2,128,128]{3,2,1,0:T(8,128)(2,1)S(1)}, bf16[4,2,128,128]{3,2,1,0:T(8,128)(2,1)S(1)}, u32[]{:S(2)}, u32[]{:S(2)}) collective-permute-start(bf16[4,2,128,128]{3,2,1,0:T(8,128)(2,1)S(1)} %pad_maximum_fusion.refs_7_), channel_id=1, source_target_pairs={{0,12},{1,13},{2,14},{3,15},{4,0},{5,1},{6,2},{7,3},{8,4},{9,5},{1... | collective-permute-start | bytes 786440 | tf_op jit(solution)/shard_map/ppermute | solution.py:223
  16.3 1.7 %collective-permute-start.1 = (bf16[3,2,128,128]{3,2,1,0:T(8,128)(2,1)}, bf16[3,2,128,128]{3,2,1,0:T(8,128)(2,1)S(1)}, u32[]{:S(2)}, u32[]{:S(2)}) collective-permute-start(bf16[3,2,128,128]{3,2,1,0:T(8,128)(2,1)} %pad_maximum_fusion.1), channel_id=1, source_target_pairs={{0,1},{1,0},{2,3},{3,2},{4,5},{5,4},{6,7},{7,6},{8,9},{9,8},{10,11... | collective-permute-start | bytes 589832 | tf_op jit(solution)/shard_map/ppermute | solution.py:223
  18.1 16.2 %collective-permute-start.6 = (bf16[4,2,128,128]{3,2,1,0:T(8,128)(2,1)S(1)}, bf16[4,2,128,128]{3,2,1,0:T(8,128)(2,1)S(1)}, u32[]{:S(2)}, u32[]{:S(2)}) collective-permute-start(bf16[4,2,128,128]{3,2,1,0:T(8,128)(2,1)S(1)} %pad_maximum_fusion.refs_7_), channel_id=1, source_target_pairs={{0,14},{1,15},{2,12},{3,13},{4,2},{5,3},{6,0},{7,1},{8,6},{9,7},{1... | collective-permute-start | bytes 786440 | tf_op jit(solution)/shard_map/ppermute | solution.py:223
  22.9 11.4 %collective-permute-start.7 = (bf16[4,2,128,128]{3,2,1,0:T(8,128)(2,1)S(1)}, bf16[4,2,128,128]{3,2,1,0:T(8,128)(2,1)S(1)}, u32[]{:S(2)}, u32[]{:S(2)}) collective-permute-start(bf16[4,2,128,128]{3,2,1,0:T(8,128)(2,1)S(1)} %pad_maximum_fusion.refs_7_), channel_id=1, source_target_pairs={{0,8},{1,9},{2,10},{3,11},{4,12},{5,13},{6,14},{7,15},{8,0},{9,1},... | collective-permute-start | bytes 786440 | tf_op jit(solution)/shard_map/ppermute | solution.py:223
  27.5 13.2 %collective-permute-start.8 = (bf16[4,2,128,128]{3,2,1,0:T(8,128)(2,1)S(1)}, bf16[4,2,128,128]{3,2,1,0:T(8,128)(2,1)S(1)}, u32[]{:S(2)}, u32[]{:S(2)}) collective-permute-start(bf16[4,2,128,128]{3,2,1,0:T(8,128)(2,1)S(1)} %pad_maximum_fusion.refs_7_), channel_id=1, source_target_pairs={{0,10},{1,11},{2,8},{3,9},{4,14},{5,15},{6,12},{7,13},{8,2},{9,3},... | collective-permute-start | bytes 786440 | tf_op jit(solution)/shard_map/ppermute | solution.py:223
  31.3 13.9 %collective-permute-start.9 = (bf16[4,2,128,128]{3,2,1,0:T(8,128)(2,1)S(1)}, bf16[4,2,128,128]{3,2,1,0:T(8,128)(2,1)S(1)}, u32[]{:S(2)}, u32[]{:S(2)}) collective-permute-start(bf16[4,2,128,128]{3,2,1,0:T(8,128)(2,1)S(1)} %pad_maximum_fusion.refs_7_), channel_id=1, source_target_pairs={{0,4},{1,5},{2,6},{3,7},{4,8},{5,9},{6,10},{7,11},{8,12},{9,13},{1... | collective-permute-start | bytes 786440 | tf_op jit(solution)/shard_map/ppermute | solution.py:223
  58.4 16.1 %copy-start.1 = (bf16[2,128,128]{2,1,0:T(8,128)(2,1)}, bf16[2,128,128]{2,1,0:T(8,128)(2,1)S(1)}, u32[]{:S(2)}) copy-start(bf16[2,128,128]{2,1,0:T(8,128)(2,1)S(1)} %get-tuple-element.60.g) | copy-start | bytes 196612
  58.5 21.6 %collective-permute-start.18 = (bf16[2,2,2,2,128,128]{5,4,3,2,1,0:T(8,128)(2,1)S(1)}, bf16[2,2,2,2,128,128]{5,4,3,2,1,0:T(8,128)(2,1)S(1)}, u32[]{:S(2)}, u32[]{:S(2)}) collective-permute-start(bf16[2,2,2,2,128,128]{5,4,3,2,1,0:T(8,128)(2,1)S(1)} %get-tuple-element.93), channel_id=1, source_target_pairs={{0,16},{16,32},{32,48},{48,0},{64,80},{80,96},{96,112},{112,64},{1... | collective-permute-start | bytes 1572872 | tf_op jit(solution)/shard_map/ppermute | solution.py:228
  60.5 20.6 %collective-permute-start.19 = (bf16[2,2,2,2,128,128]{5,4,3,2,1,0:T(8,128)(2,1)S(1)}, bf16[2,2,2,2,128,128]{5,4,3,2,1,0:T(8,128)(2,1)S(1)}, u32[]{:S(2)}, u32[]{:S(2)}) collective-permute-start(bf16[2,2,2,2,128,128]{5,4,3,2,1,0:T(8,128)(2,1)S(1)} %get-tuple-element.95), channel_id=1, source_target_pairs={{0,32},{16,48},{32,0},{48,16},{64,96},{80,112},{96,64},{112,80},{1... | collective-permute-start | bytes 1572872 | tf_op jit(solution)/shard_map/ppermute | solution.py:228
  64.1 18.9 %collective-permute-start.20 = (bf16[2,2,2,2,128,128]{5,4,3,2,1,0:T(8,128)(2,1)S(1)}, bf16[2,2,2,2,128,128]{5,4,3,2,1,0:T(8,128)(2,1)S(1)}, u32[]{:S(2)}, u32[]{:S(2)}) collective-permute-start(bf16[2,2,2,2,128,128]{5,4,3,2,1,0:T(8,128)(2,1)S(1)} %get-tuple-element.94), channel_id=1, source_target_pairs={{0,48},{16,0},{32,16},{48,32},{64,112},{80,64},{96,80},{112,96},{1... | collective-permute-start | bytes 1572872 | tf_op jit(solution)/shard_map/ppermute | solution.py:228
  74.5 24.8 %collective-permute-start.22 = (bf16[4,2,2,2,128,128]{5,4,3,2,1,0:T(8,128)(2,1)S(1)}, bf16[4,2,2,2,128,128]{5,4,3,2,1,0:T(8,128)(2,1)S(1)}, u32[]{:S(2)}, u32[]{:S(2)}) collective-permute-start(bf16[4,2,2,2,128,128]{5,4,3,2,1,0:T(8,128)(2,1)S(1)} %slice.125), channel_id=1, source_target_pairs={{0,64},{16,80},{32,96},{48,112},{64,0},{80,16},{96,32},{112,48},{1... | collective-permute-start | bytes 3145736 | tf_op jit(solution)/shard_map/ppermute | solution.py:228
  77.3 24.9 %collective-permute-start.12 = (bf16[2,4,2,128,128]{4,3,2,1,0:T(8,128)(2,1)S(1)}, bf16[2,4,2,128,128]{4,3,2,1,0:T(8,128)(2,1)S(1)}, u32[]{:S(2)}, u32[]{:S(2)}) collective-permute-start(bf16[2,4,2,128,128]{4,3,2,1,0:T(8,128)(2,1)S(1)} %bitcast.111), channel_id=1, source_target_pairs={{0,4},{1,5},{2,6},{3,7},{4,8},{5,9},{6,10},{7,11},{8,12},{9,13},{1... | collective-permute-start | bytes 1572872 | tf_op jit(solution)/shard_map/ppermute | solution.py:223
  80.2 23.2 %collective-permute-start.13 = (bf16[2,4,2,128,128]{4,3,2,1,0:T(8,128)(2,1)S(1)}, bf16[2,4,2,128,128]{4,3,2,1,0:T(8,128)(2,1)S(1)}, u32[]{:S(2)}, u32[]{:S(2)}) collective-permute-start(bf16[2,4,2,128,128]{4,3,2,1,0:T(8,128)(2,1)S(1)} %bitcast.110), channel_id=1, source_target_pairs={{0,8},{1,9},{2,10},{3,11},{4,12},{5,13},{6,14},{7,15},{8,0},{9,1},... | collective-permute-start | bytes 1572872 | tf_op jit(solution)/shard_map/ppermute | solution.py:223
  81.1 23.0 %collective-permute-start.14 = (bf16[2,4,2,128,128]{4,3,2,1,0:T(8,128)(2,1)S(1)}, bf16[2,4,2,128,128]{4,3,2,1,0:T(8,128)(2,1)S(1)}, u32[]{:S(2)}, u32[]{:S(2)}) collective-permute-start(bf16[2,4,2,128,128]{4,3,2,1,0:T(8,128)(2,1)S(1)} %bitcast.109), channel_id=1, source_target_pairs={{0,12},{1,13},{2,14},{3,15},{4,0},{5,1},{6,2},{7,3},{8,4},{9,5},{1... | collective-permute-start | bytes 1572872 | tf_op jit(solution)/shard_map/ppermute | solution.py:223
  82.9 32.8 %collective-permute-start.11 = (bf16[2,2,128,128]{3,2,1,0:T(8,128)(2,1)S(1)}, bf16[2,2,128,128]{3,2,1,0:T(8,128)(2,1)S(1)}, u32[]{:S(2)}, u32[]{:S(2)}) collective-permute-start(bf16[2,2,128,128]{3,2,1,0:T(8,128)(2,1)S(1)} %pad_maximum_fusion.3), channel_id=1, source_target_pairs={{0,1},{1,0},{2,3},{3,2},{4,5},{5,4},{6,7},{7,6},{8,9},{9,8},{10,11... | collective-permute-start | bytes 393224 | tf_op jit(solution)/shard_map/ppermute | solution.py:223
  99.4 25.9 %collective-permute-start.21 = (bf16[2,2,2,128,128]{4,3,2,1,0:T(8,128)(2,1)}, bf16[2,2,2,128,128]{4,3,2,1,0:T(8,128)(2,1)}, u32[]{:S(2)}, u32[]{:S(2)}) collective-permute-start(bf16[2,2,2,128,128]{4,3,2,1,0:T(8,128)(2,1)} %slice_bitcast_fusion.4), channel_id=1, source_target_pairs={{0,64},{16,80},{32,96},{48,112},{64,0},{80,16},{96,32},{112,48},{1... | collective-permute-start | bytes 786440 | tf_op jit(solution)/shard_map/ppermute | solution.py:228
  102.3 11.9 %collective-permute-start.23 = (bf16[2,2,2,128,128]{4,3,2,1,0:T(8,128)(2,1)S(1)}, bf16[2,2,2,128,128]{4,3,2,1,0:T(8,128)(2,1)S(1)}, u32[]{:S(2)}, u32[]{:S(2)}) collective-permute-start(bf16[2,2,2,128,128]{4,3,2,1,0:T(8,128)(2,1)S(1)} %get-tuple-element.98), channel_id=1, source_target_pairs={{0,16},{16,32},{32,48},{48,0},{64,80},{80,96},{96,112},{112,64},{1... | collective-permute-start | bytes 786440 | tf_op jit(solution)/shard_map/ppermute | solution.py:228
  103.4 10.8 %collective-permute-start.24 = (bf16[2,2,2,128,128]{4,3,2,1,0:T(8,128)(2,1)S(1)}, bf16[2,2,2,128,128]{4,3,2,1,0:T(8,128)(2,1)S(1)}, u32[]{:S(2)}, u32[]{:S(2)}) collective-permute-start(bf16[2,2,2,128,128]{4,3,2,1,0:T(8,128)(2,1)S(1)} %get-tuple-element.100), channel_id=1, source_target_pairs={{0,32},{16,48},{32,0},{48,16},{64,96},{80,112},{96,64},{112,80},{1... | collective-permute-start | bytes 786440 | tf_op jit(solution)/shard_map/ppermute | solution.py:228
  104.1 10.7 %collective-permute-start.25 = (bf16[2,2,2,128,128]{4,3,2,1,0:T(8,128)(2,1)S(1)}, bf16[2,2,2,128,128]{4,3,2,1,0:T(8,128)(2,1)S(1)}, u32[]{:S(2)}, u32[]{:S(2)}) collective-permute-start(bf16[2,2,2,128,128]{4,3,2,1,0:T(8,128)(2,1)S(1)} %get-tuple-element.99), channel_id=1, source_target_pairs={{0,48},{16,0},{32,16},{48,32},{64,112},{80,64},{96,80},{112,96},{1... | collective-permute-start | bytes 786440 | tf_op jit(solution)/shard_map/ppermute | solution.py:228
  106.1 11.2 %copy-start.2 = (bf16[2,128,128]{2,1,0:T(8,128)(2,1)S(1)}, bf16[2,128,128]{2,1,0:T(8,128)(2,1)}, u32[]{:S(2)}) copy-start(bf16[2,128,128]{2,1,0:T(8,128)(2,1)} %copy-done.1) | copy-start | bytes 196612
  114.9 10.4 %collective-permute-start.26 = (bf16[2,2,2,128,128]{4,3,2,1,0:T(8,128)(2,1)S(1)}, bf16[2,2,2,128,128]{4,3,2,1,0:T(8,128)(2,1)S(1)}, u32[]{:S(2)}, u32[]{:S(2)}) collective-permute-start(bf16[2,2,2,128,128]{4,3,2,1,0:T(8,128)(2,1)S(1)} %fusion.10), channel_id=1, source_target_pairs={{0,1},{1,0},{2,3},{3,2},{4,5},{5,4},{6,7},{7,6},{8,9},{9,8},{10,11... | collective-permute-start | bytes 786440 | tf_op jit(solution)/shard_map/ppermute | solution.py:223
  115.1 6.5 %collective-permute-start.15 = (bf16[2,2,128,128]{3,2,1,0:T(8,128)(2,1)S(1)}, bf16[2,2,128,128]{3,2,1,0:T(8,128)(2,1)S(1)}, u32[]{:S(2)}, u32[]{:S(2)}) collective-permute-start(bf16[2,2,128,128]{3,2,1,0:T(8,128)(2,1)S(1)} %get-tuple-element.103), channel_id=1, source_target_pairs={{0,2},{1,3},{2,0},{3,1},{4,6},{5,7},{6,4},{7,5},{8,10},{9,11},{10,... | collective-permute-start | bytes 393224 | tf_op jit(solution)/shard_map/ppermute | solution.py:223
  115.2 6.4 %collective-permute-start.16 = (bf16[2,2,128,128]{3,2,1,0:T(8,128)(2,1)S(1)}, bf16[2,2,128,128]{3,2,1,0:T(8,128)(2,1)S(1)}, u32[]{:S(2)}, u32[]{:S(2)}) collective-permute-start(bf16[2,2,128,128]{3,2,1,0:T(8,128)(2,1)S(1)} %get-tuple-element.102), channel_id=1, source_target_pairs={{0,1},{1,0},{2,3},{3,2},{4,5},{5,4},{6,7},{7,6},{8,9},{9,8},{10,11... | collective-permute-start | bytes 393224 | tf_op jit(solution)/shard_map/ppermute | solution.py:223
  115.8 7.6 %collective-permute-start.17 = (bf16[2,2,128,128]{3,2,1,0:T(8,128)(2,1)S(1)}, bf16[2,2,128,128]{3,2,1,0:T(8,128)(2,1)S(1)}, u32[]{:S(2)}, u32[]{:S(2)}) collective-permute-start(bf16[2,2,128,128]{3,2,1,0:T(8,128)(2,1)S(1)} %get-tuple-element.101), channel_id=1, source_target_pairs={{0,3},{1,2},{2,1},{3,0},{4,7},{5,6},{6,5},{7,4},{8,11},{9,10},{10,... | collective-permute-start | bytes 393224 | tf_op jit(solution)/shard_map/ppermute | solution.py:223
  (2 other events, 3.6 us)
where the time goes:
time: 129 us; the launch traced here: 128 us
  waiting for transfers between devices  48.5 us (38%)
  starting transfers between devices  36.8 us (29%)
  Pallas kernels  23.1 us (18%)
  local copies, waits for them, and re-layouts  11.6 us (9%)
  other arithmetic  3.97 us (3%)
  matrix products  2.74 us (2%)
    ppermute x8, waiting for transfers between devices, to_row(): return lax.ppermute(x, 'row', pairs)  24.5 us
    ppermute x19, waiting for transfers between devices, to_col(): return lax.ppermute(x, 'col', pairs)  24 us
    pallas_call x2, Pallas kernels, attend_blocks(): pl.pallas_call(kernel, out_shape=tuple((jax.ShapeDtypeStruct(s, BF) for s...  22.4 us
    ppermute x19, starting transfers between devices, to_col(): return lax.ppermute(x, 'col', pairs)  21.1 us
    ppermute x8, starting transfers between devices, to_row(): return lax.ppermute(x, 'row', pairs)  15.7 us
    unnamed x19, local copies, waits for them, and re-layouts  4.53 us
    optimization_barrier x1, local copies, waits for them, and re-layouts, body(): shard, pair_bias = lax.optimization_barrier((shard, pair_bias))  3.36 us
    dot_general x5, matrix products, split(): lax.dot_general(x.reshape(2 * BS, 2 * BS), sel, NN, preferred_element_typ...  2.74 us
  transfers between devices with their start and end apart: 27, of which 12 were waited for; matrix products, arithmetic and copies ran while one was open for 10% of the time, Pallas kernels for 8%

commit v1 on v0

--- a/solution.py
+++ b/solution.py
@@ -25,40 +25,49 @@
     def two(k,c):
         f(2*k,0); f(2*k+1,0)
         return c
+
     lax.fori_loop(0,pairs//2,two,0)
+
     @pl.when(pairs%2==1)
     def _(): f(pairs-1,0)
 
 
-def attend_kernel(first, *refs):
+def attend_kernel(first,*refs):
     idx,cnt,chk,q,gate,cot,bias=refs[:7]
     pieces=refs[7:15]
-    k=15
-    prev=None
-    if not first: prev=refs[15:19]; k=19
-    dq,gg,bg=refs[k:k+3]
-    terms=refs[k+3:k+7]
-    s_ref,e_ref,m_ref,l_ref,o_ref,off_ref,qm,qt,dom,domt,acc,kv,sem=refs[k+7:]
+    if first:
+        dq,gg,bg,acc=refs[15:19]
+        rest=refs[19:]
+    else:
+        dq,gg,bg,acc=refs[16:20]
+        terms=refs[20:28]
+        rest=refs[28:]
+    s_ref,e_ref,m_ref,l_ref,o_ref,off_ref,qm,qt,dom,domt,kv,sem=rest
     for m in range(8):
         pltpu.make_async_copy(pieces[m],kv.at[pl.ds(4*m,4)],sem.at[m]).start()
     lane=lax.broadcasted_iota(jnp.int32,(BS,BS),1)//DH
-    acc[...]=jnp.zeros(acc.shape,F32)
+    chan=lax.broadcasted_iota(jnp.int32,(BS,BS),0)//DH
+    if first:
+        acc[...]=jnp.zeros(acc.shape,F32)
     for m in range(8):
         pltpu.make_async_copy(pieces[m],kv.at[pl.ds(4*m,4)],sem.at[m]).wait()
+
     def block(j,carry):
         n=cnt[j]
         pairs=(n+1)//2
         qj=q[j]
+        qj_t=qj.T
         for g in range(G):
             r=slice(g*BS,(g+1)*BS)
-            v=jnp.where(lane==g,qj,jnp.zeros_like(qj))
-            qm[r,:]=v
-            qt[:,r]=v.T
+            qm[r,:]=jnp.where(lane==g,qj,jnp.zeros_like(qj))
+            qt[:,r]=jnp.where(chan==g,qj_t,jnp.zeros_like(qj_t))
         m_ref[...]=jnp.full(m_ref.shape,-jnp.inf,F32)
         l_ref[...]=jnp.zeros(l_ref.shape,F32)
         o_ref[...]=jnp.zeros(o_ref.shape,F32)
+
         def both(p,w):
             return jnp.concatenate([kv[idx[j,2*p],w],kv[idx[j,2*p+1],w]],0)
+
         def score(p,c):
             k2=both(p,0)
             S=dot(qm[...],k2,NT)*(SCALE*LOG2E)
@@ -75,8 +84,10 @@
                     s_ref[p,r,BS:]=s1
                     m_ref[r,:]=jnp.maximum(m_ref[r,:],jnp.maximum(s0,s1))
             return c
+
         loop2(pairs,score)
         m_ref[...]=jnp.broadcast_to(jnp.max(m_ref[...],axis=1,keepdims=True),m_ref.shape)
+
         def attend(p,c):
             v2=both(p,1)
             for g in range(G):
@@ -88,23 +99,30 @@
                 e_ref[p,r,:]=e
             o_ref[...]+=dot(e_ref[p],v2,NN)
             return c
+
         loop2(pairs,attend)
-        att=jnp.zeros((BS,BS),F32); inv=[]
+        att=jnp.zeros((BS,BS),F32)
+        inv=jnp.zeros((BS,BS),F32)
         for g in range(G):
             r=slice(g*BS,(g+1)*BS)
-            inv.append(1.0/jnp.sum(l_ref[r,:],axis=1,keepdims=True))
-            att=jnp.where(lane==g,o_ref[r,:]*inv[g],att)
+            one=1.0/jnp.sum(l_ref[r,:],axis=1,keepdims=True)
+            att=jnp.where(lane==g,o_ref[r,:],att)
+            inv=jnp.where(lane==g,one,inv)
+        att=att*inv
         c=cot[j].astype(F32)
         opened=1.0/(1.0+jnp.exp(-gate[j].astype(F32)))
         gg[j]=(c*att*opened*(1.0-opened)).astype(BF)
-        core=(c*opened).astype(BF).astype(F32)
+        d=((c*opened).astype(BF).astype(F32)*inv).astype(BF)
+        d_t=d.T
+        x=d.astype(F32)*att
         for g in range(G):
             r=slice(g*BS,(g+1)*BS)
-            d=jnp.where(lane==g,core*inv[g],0.0).astype(BF)
-            dom[r,:]=d
-            domt[:,r]=d.T
-            off_ref[r,:]=jnp.broadcast_to(jnp.sum(d.astype(F32)*att,axis=1,keepdims=True),(BS,BS))
+            dom[r,:]=jnp.where(lane==g,d,jnp.zeros_like(d))
+            domt[:,r]=jnp.where(chan==g,d_t,jnp.zeros_like(d_t))
+            off=jnp.sum(jnp.where(lane==g,x,0.0),axis=1,keepdims=True)
+            off_ref[r,:]=jnp.broadcast_to(off,(BS,BS))
         o_ref[...]=jnp.zeros(o_ref.shape,F32)
+
         def backward(p,c):
             a0=idx[j,2*p]; a1=idx[j,2*p+1]
             ch=chk[p]
@@ -129,25 +147,25 @@
             acc[a0,0]+=dk[:,:BS]; acc[a1,0]+=dk[:,BS:]
             acc[a0,1]+=dv[:,:BS]; acc[a1,1]+=dv[:,BS:]
             return c
+
         loop2(pairs,backward)
+
         def clear(p,c):
             z=jnp.zeros((2,2,BS,BS),BF)
             bg[chk[p],j]=z
             return c
+
         lax.fori_loop(pairs,8,clear,0)
         x=jnp.zeros((BS,BS),F32)
         for g in range(G):
             x=jnp.where(lane==g,o_ref[g*BS:(g+1)*BS,:],x)
         dq[j]=(x*SCALE).astype(BF)
         return carry
+
     lax.fori_loop(0,2,block,0)
-    for dy in range(4):
-        def store(b,c):
-            a=acc[8*dy+b]
-            if not first: a=a+prev[dy][b].astype(F32)
-            terms[dy][b]=a.astype(BF)
-            return c
-        lax.fori_loop(0,8,store,0)
+    if not first:
+        for m in range(8):
+            terms[m][...]=acc[4*m:4*m+4].astype(BF)
 
 
 def attend_blocks(idx,cnt,chk,q,gate,cot,bias,pieces,prev):
@@ -157,38 +175,35 @@
     AN=pl.BlockSpec(memory_space=pl.ANY)
     args=[idx,cnt,chk,q,gate,cot,bias,*pieces]
     specs=[SM]*3+[VM]*4+[AN]*8
+    shapes=[((2,BS,BS),BF),((2,BS,BS),BF),((8,2,2,2,BS,BS),BF),((32,2,BS,BS),F32)]
     if not first:
-        args+=prev
-        specs+=[VM]*4
+        args.append(prev)
+        specs.append(VM)
+        shapes+=[((4,2,BS,BS),BF)]*8
 
     def kernel(*refs):
         attend_kernel(first,*refs)
 
-    shapes=((2,BS,BS),(2,BS,BS),(8,2,2,2,BS,BS))+((8,2,BS,BS),)*4
     return pl.pallas_call(
         kernel,
-        out_shape=tuple(jax.ShapeDtypeStruct(s,BF) for s in shapes),
+        out_shape=tuple(jax.ShapeDtypeStruct(*s) for s in shapes),
         in_specs=specs,
-        out_specs=(VM,)*7,
+        out_specs=(VM,)*len(shapes),
         scratch_shapes=[pltpu.VMEM((8,G*BS,2*BS),F32),pltpu.VMEM((8,G*BS,2*BS),BF)]
         +[pltpu.VMEM((G*BS,BS),F32)]*4
         +[pltpu.VMEM((G*BS,BS),BF),pltpu.VMEM((BS,G*BS),BF)]*2
-        +[pltpu.VMEM((32,2,BS,BS),F32),pltpu.VMEM((32,2,BS,BS),BF),pltpu.SemaphoreType.DMA((8,))],
+        +[pltpu.VMEM((32,2,BS,BS),BF),pltpu.SemaphoreType.DMA((8,))],
+        input_output_aliases={} if first else {15:3},
         compiler_params=pltpu.CompilerParams(vmem_limit_bytes=20<<20),
         cost_estimate=pl.CostEstimate(flops=10_000_000_000,bytes_accessed=24<<20,transcendentals=4<<20),
         name="attend_blocks",
     )(*args)
 
 
-def join_kernel(p,xs,cs,xc,sel,k_out,v_out):
+def join_kernel(own,far,sel,k_out,v_out):
     for w,out in ((0,k_out),(1,v_out)):
         for b in range(2):
-            own=p[b,w].astype(F32)+xs[b,w].astype(F32)
-            far=cs[b,w].astype(F32)+xc[b,w].astype(F32)
-            if w==0:
-                own=own*SCALE
-                far=far*SCALE
-            both=jnp.concatenate([own.astype(BF).T,far.astype(BF).T],1)
+            both=jnp.concatenate([own[b,w].T,far[b,w].T],1)
             full=dot(both,sel[...],NT).astype(BF)
             out[0,b*BS:(b+1)*BS,:]=full[:,:BS]
             out[1,b*BS:(b+1)*BS,:]=full[:,BS:]
@@ -226,6 +241,14 @@
 def to_row(x,dx,dz):
     pairs=[(s,((s//4)^dx)*4+(s%4+dz)%4) for s in range(8)]
     return lax.ppermute(x,"row",pairs)
+
+
+def cross(x):
+    pairs=[]
+    for r in range(8):
+        for c in range(16):
+            pairs.append((r*16+c,(r^4)*16+(c^1)))
+    return lax.ppermute(x,("row","col"),pairs)
 
 
 def swap(x):
@@ -267,10 +290,13 @@
     v_mine,v_send=split(value_vectors)
     shard=jnp.concatenate([jnp.stack([k_mine,v_mine],1),swap(jnp.stack([k_send,v_send],1))],0)
     shard,pair_bias=lax.optimization_barrier((shard,pair_bias))
-    pieces=[]
-    for dy in range(4):
-        for dx in range(2):
-            pieces.append(to_col(shard,(4-dy)%4,dx,0) if dy+dx else shard)
+
+    def gather(x,dy,dx):
+        return to_col(x,(4-dy)%4,dx,0)
+
+    near=gather(shard,0,1)
+    up,down,across=gather(shard,1,0),gather(shard,3,0),gather(shard,2,0)
+    pieces=[shard, near, up, gather(near,1,0), across, gather(across,0,1), down, gather(near,3,0)]
 
     table=jnp.concatenate([block_table,valid_counts[:,None]],1)
     tables=[table,swap(table)]
@@ -294,38 +320,46 @@
 
     ready=(places(tables[0]),tables[0][:,TAB],places(tables[1]),tables[1][:,TAB],mine,other,bias_mine,bias_other,pieces)
     idx0,cnt0,idx1,cnt1,mine,other,bias_mine,bias_other,pieces=lax.optimization_barrier(ready)
-    dq0,gg0,bg0,*terms=attend_blocks(idx0,cnt0,turn*2+far,*mine,bias_mine,pieces,None)
+    dq0,gg0,bg0,acc=attend_blocks(idx0,cnt0,turn*2+far,*mine,bias_mine,pieces,None)
     bg0=bg0.reshape(4,2,2,2,2,BS,BS)
-    bg0_in=[]
-    for dz in range(1,4):
-        bg0_in.append(to_row(bg0[dz],0,dz))
-    dq1,gg1,bg1,*terms=attend_blocks(
-        idx1,cnt1,far*4+turn,other[0],other[1],other[2],bias_other,pieces,terms
+
+    def row_sums(x):
+        out=[x[0]]
+        for dz in range(1,4):
+            out.append(to_row(x[dz],0,dz))
+        return out
+
+    bg0=row_sums(bg0)
+    dq1,gg1,bg1,_,*t=attend_blocks(
+        idx1,cnt1,turn*2+far,other[0],other[1],other[2],bias_other,pieces,acc
     )
-    bg1=bg1.reshape(2,4,2,2,2,BS,BS)
-
-    terms=[t.reshape(2,4,2,BS,BS) for t in terms]
-    part=plus(terms[0],*[to_col(terms[dy],dy,0,0) for dy in range(1,4)]).astype(BF)
-    bg1=plus(bg1[0],to_row(bg1[1],1,0)).astype(BF)
-    bg0=plus(bg0[0],*bg0_in).astype(BF)
-    bias1_in=[to_row(bg1[dz],0,dz) for dz in range(1,4)]
-    bias0=plus(bg0[0],to_row(bg0[1],1,0)).astype(BF)
-    bias1=plus(bg1[0],*bias1_in).astype(BF)
-    bias_back=swap(bias1)
-
+    bg1=bg1.reshape(4,2,2,2,2,BS,BS)
+
+    def step(x,dy,dx):
+        return to_col(x,dy,dx,0)
+
+    from_down,from_up=step(t[3],1,0),step(t[7],3,0)
+    from_near=step(t[5],0,1)
+    bg1=row_sums(bg1)
+    steps=[step(t[2],1,0),step(t[6],3,0)]
+    bg0=plus(*bg0).astype(BF)
+    bg0_far=to_row(bg0[1],1,0)
+    steps.append(step(plus(t[1],from_down,from_up).astype(BF),0,1))
+    steps.append(step(plus(t[4],from_near).astype(BF),2,0))
     q_back=swap(jnp.stack([dq1,gg1],0))
     query_grad,gate_grad=small_call(unite_kernel,dq0,gg0,q_back,sel)
-    key_grad,value_grad=small_call(
-        join_kernel,
-        part[0,:2],
-        to_col(part[1,:2],0,1,0),
-        swap(part[0,2:]),
-        to_col(part[1,2:],0,1,1),
-        sel,
-    )
-
-    a=jnp.where(core==0,bias0,bias_back)
-    b=jnp.where(core==0,bias_back,bias0)
+    bias0=plus(bg0[0],bg0_far).astype(BF)
+    own=plus(t[0],*steps)
+    own=jnp.stack([own[:,0]*SCALE,own[:,1]],1).astype(BF)
+    own_far=swap(own[2:])
+    key_grad,value_grad=small_call(join_kernel,own[:2],own_far,sel)
+
+    bg1=plus(*bg1).astype(BF)
+    turned=cross(bg1[1])
+    bias1=plus(swap(bg1[0]),turned).astype(BF)
+
+    a=jnp.where(core==0,bias0,bias1)
+    b=jnp.where(core==0,bias1,bias0)
     bias_grad=jnp.concatenate([a,b],1).transpose(0,1,3,2,4)
 
     def rows(x):

time: 129 us -> 135 us (1.047)
  starting transfers between devices: 36.8 us -> 41.5 us
  waiting for transfers between devices: 48.5 us -> 50.7 us
    ppermute x19 -> x21, waiting for transfers between devices: 24 us -> 16.5 us  [to_col(): return lax.ppermute(x, 'col', pairs)]
    ppermute x8 -> x7, waiting for transfers between devices: 24.5 us -> 31.7 us  [to_row(): return lax.ppermute(x, 'row', pairs)]
    ppermute x0 -> x1, starting transfers between devices: none -> 3.12 us  [cross(): return lax.ppermute(x, ('row', 'col'), pairs)]
    ppermute x0 -> x1, waiting for transfers between devices: none -> 2.47 us  [cross(): return lax.ppermute(x, ('row', 'col'), pairs)]
    ppermute x19 -> x21, starting transfers between devices: 21.1 us -> 22.1 us  [to_col(): return lax.ppermute(x, 'col', pairs)]
    ppermute x8 -> x7, starting transfers between devices: 15.7 us -> 16.3 us  [to_row(): return lax.ppermute(x, 'row', pairs)]
  transfers between devices with their start and end apart: 27 -> 29, of which waited for: 12 -> 11; matrix products, arithmetic and copies ran while one was open for 10% -> 10% of each run, Pallas kernels for 8% -> 0%
where the time goes in v1:
time: 135 us; the launch traced here: 134 us
  waiting for transfers between devices  50.7 us (38%)
  starting transfers between devices  41.5 us (31%)
  Pallas kernels  22.1 us (16%)
  local copies, waits for them, and re-layouts  11.5 us (9%)
  other arithmetic  4.15 us (3%)
  matrix products  2.74 us (2%)
    ppermute x7, waiting for transfers between devices, to_row(): return lax.ppermute(x, 'row', pairs)  31.7 us
    ppermute x21, starting transfers between devices, to_col(): return lax.ppermute(x, 'col', pairs)  22.1 us
    pallas_call x2, Pallas kernels, attend_blocks(): pl.pallas_call(kernel, out_shape=tuple((jax.ShapeDtypeStruct(*s) for s in...  21.5 us
    ppermute x21, waiting for transfers between devices, to_col(): return lax.ppermute(x, 'col', pairs)  16.5 us
    ppermute x7, starting transfers between devices, to_row(): return lax.ppermute(x, 'row', pairs)  16.3 us
    unnamed x19, local copies, waits for them, and re-layouts  5.15 us
    optimization_barrier x1, local copies, waits for them, and re-layouts, body(): shard, pair_bias = lax.optimization_barrier((shard, pair_bias))  3.36 us
    ppermute x1, starting transfers between devices, cross(): return lax.ppermute(x, ('row', 'col'), pairs)  3.12 us
  transfers between devices with their start and end apart: 29, of which 11 were waited for; matrix products, arithmetic and copies ran while one was open for 10% of the time, Pallas kernels for 0%

profile of v1, /device:TPU:0, one launch (start us, length us, event | category | flops | bytes accessed | tf_op | source)
XLA Modules:
  0.0 133.8 jit_solution(4818434525364912091)
XLA Ops:
  1.9 1.1 fusion.4
  3.9 1.3 pad_add_fusion
  5.7 3.4 %copy.23 = bf16[2,4,128,16,128]{4,2,3,1,0:T(8,128)(2,1)S(1)} copy(bf16[2,4,128,16,128]{4,3,2,1,0:T(8,128)(2,1)} %param.13) | data formatting | bytes 8388608 | tf_op jit(solution)/shard_map/optimization_barrier | solution.py:292
  9.1 1.6 %dynamic-slice_bitcast_fusion = (bf16[2,2,16,128,128]{4,3,2,1,0:T(8,128)(2,1)}, bf16[2,2,16,128,128]{4,3,2,1,0:T(8,128)(2,1)S(1)}) fusion(bf16[2,4,128,16,128]{4,2,3,1,0:T(8,128)(2,1)S(1)} %copy.23, s32[]{:T(128)S(6)} %select_n.153, s32[]{:T(128)S(6)} %select_n.152), kind=kLoop, calls=%fused_computation | loop fusion | bytes 8388616 | tf_op jit(solution)/shard_map/dynamic_slice | solution.py:316
  12.1 1.7 %collective-permute-start.9 = (bf16[4,2,128,128]{3,2,1,0:T(8,128)(2,1)S(1)}, bf16[4,2,128,128]{3,2,1,0:T(8,128)(2,1)S(1)}, u32[]{:S(2)}, u32[]{:S(2)}) collective-permute-start(bf16[4,2,128,128]{3,2,1,0:T(8,128)(2,1)S(1)} %pad_maximum_fusion.refs_7_), channel_id=1, source_target_pairs={{0,4},{1,5},{2,6},{3,7},{4,8},{5,9},{6,10},{7,11},{8,12},{9,13},{1... | collective-permute-start | bytes 786440 | tf_op jit(solution)/shard_map/ppermute | solution.py:238
  13.8 2.9 %collective-permute-start.7 = (bf16[4,2,128,128]{3,2,1,0:T(8,128)(2,1)S(1)}, bf16[4,2,128,128]{3,2,1,0:T(8,128)(2,1)S(1)}, u32[]{:S(2)}, u32[]{:S(2)}) collective-permute-start(bf16[4,2,128,128]{3,2,1,0:T(8,128)(2,1)S(1)} %pad_maximum_fusion.refs_7_), channel_id=1, source_target_pairs={{0,8},{1,9},{2,10},{3,11},{4,12},{5,13},{6,14},{7,15},{8,0},{9,1},... | collective-permute-start | bytes 786440 | tf_op jit(solution)/shard_map/ppermute | solution.py:238
  16.7 1.5 %collective-permute-start.4 = (bf16[4,2,128,128]{3,2,1,0:T(8,128)(2,1)S(1)}, bf16[4,2,128,128]{3,2,1,0:T(8,128)(2,1)S(1)}, u32[]{:S(2)}, u32[]{:S(2)}) collective-permute-start(bf16[4,2,128,128]{3,2,1,0:T(8,128)(2,1)S(1)} %pad_maximum_fusion.refs_7_), channel_id=1, source_target_pairs={{0,2},{1,3},{2,0},{3,1},{4,6},{5,7},{6,4},{7,5},{8,10},{9,11},{10,... | collective-permute-start | bytes 786440 | tf_op jit(solution)/shard_map/ppermute | solution.py:238
  18.4 1.6 %collective-permute-done.1 = bf16[3,2,128,128]{3,2,1,0:T(8,128)(2,1)S(1)} collective-permute-done((bf16[3,2,128,128]{3,2,1,0:T(8,128)(2,1)}, bf16[3,2,128,128]{3,2,1,0:T(8,128)(2,1)S(1)}, u32[]{:S(2)}, u32[]{:S(2)}) %collective-permute-start.1) | collective-permute-done | bytes 196640 | tf_op jit(solution)/shard_map/ppermute | solution.py:238
  20.0 1.3 %collective-permute-start.5 = (bf16[4,2,128,128]{3,2,1,0:T(8,128)(2,1)S(1)}, bf16[4,2,128,128]{3,2,1,0:T(8,128)(2,1)S(1)}, u32[]{:S(2)}, u32[]{:S(2)}) collective-permute-start(bf16[4,2,128,128]{3,2,1,0:T(8,128)(2,1)S(1)} %pad_maximum_fusion.refs_7_), channel_id=1, source_target_pairs={{0,12},{1,13},{2,14},{3,15},{4,0},{5,1},{6,2},{7,3},{8,4},{9,5},{1... | collective-permute-start | bytes 786440 | tf_op jit(solution)/shard_map/ppermute | solution.py:238
  21.4 3.5 %collective-permute-done.4.refs_8_ = bf16[4,2,128,128]{3,2,1,0:T(8,128)(2,1)S(1)} collective-permute-done((bf16[4,2,128,128]{3,2,1,0:T(8,128)(2,1)S(1)}, bf16[4,2,128,128]{3,2,1,0:T(8,128)(2,1)S(1)}, u32[]{:S(2)}, u32[]{:S(2)}) %collective-permute-start.4) | collective-permute-done | bytes 262176 | tf_op jit(solution)/shard_map/ppermute | solution.py:238
  24.9 3.2 %collective-permute-start.6 = (bf16[4,2,128,128]{3,2,1,0:T(8,128)(2,1)S(1)}, bf16[4,2,128,128]{3,2,1,0:T(8,128)(2,1)S(1)}, u32[]{:S(2)}, u32[]{:S(2)}) collective-permute-start(bf16[4,2,128,128]{3,2,1,0:T(8,128)(2,1)S(1)} %collective-permute-done.4.refs_8_), channel_id=1, source_target_pairs={{0,12},{1,13},{2,14},{3,15},{4,0},{5,1},{6,2},{7,3},{8,4},{9,5},{1... | collective-permute-start | bytes 786440 | tf_op jit(solution)/shard_map/ppermute | solution.py:238
  28.1 1.4 %collective-permute-done.7.refs_11_ = bf16[4,2,128,128]{3,2,1,0:T(8,128)(2,1)S(1)} collective-permute-done((bf16[4,2,128,128]{3,2,1,0:T(8,128)(2,1)S(1)}, bf16[4,2,128,128]{3,2,1,0:T(8,128)(2,1)S(1)}, u32[]{:S(2)}, u32[]{:S(2)}) %collective-permute-start.7) | collective-permute-done | bytes 262176 | tf_op jit(solution)/shard_map/ppermute | solution.py:238
  29.5 1.5 %collective-permute-start.8 = (bf16[4,2,128,128]{3,2,1,0:T(8,128)(2,1)S(1)}, bf16[4,2,128,128]{3,2,1,0:T(8,128)(2,1)S(1)}, u32[]{:S(2)}, u32[]{:S(2)}) collective-permute-start(bf16[4,2,128,128]{3,2,1,0:T(8,128)(2,1)S(1)} %collective-permute-done.7.refs_11_), channel_id=1, source_target_pairs={{0,2},{1,3},{2,0},{3,1},{4,6},{5,7},{6,4},{7,5},{8,10},{9,11},{10,... | collective-permute-start | bytes 786440 | tf_op jit(solution)/shard_map/ppermute | solution.py:238
  31.2 5.7 %collective-permute-done.8.refs_12_ = bf16[4,2,128,128]{3,2,1,0:T(8,128)(2,1)S(1)} collective-permute-done((bf16[4,2,128,128]{3,2,1,0:T(8,128)(2,1)S(1)}, bf16[4,2,128,128]{3,2,1,0:T(8,128)(2,1)S(1)}, u32[]{:S(2)}, u32[]{:S(2)}) %collective-permute-start.8) | collective-permute-done | bytes 262176 | tf_op jit(solution)/shard_map/ppermute | solution.py:238
  36.9 12.8 %attend_blocks.2 = (bf16[2,128,128]{2,1,0:T(8,128)(2,1)S(1)}, bf16[2,128,128]{2,1,0:T(8,128)(2,1)S(1)}, bf16[8,2,2,2,128,128]{5,4,3,2,1,0:T(8,128)(2,1)S(1)}, f32[32,2,128,128]{3,2,1,0:T(8,128)S(1)}) custom-call(s32[2,16]{1,0:T(2,128)S(1)} %fusion.32.refs_0_, s32[2]{0:T(128)S(1)} %copy-done, s32[8]{0:T(128)S(1)} %fusion.47.refs_2_, ...), custom_call_target="tpu_custom_call" | custom-call | flops 10000000000 | bytes 25165824 | tf_op jit(solution)/shard_map/attend_blocks/pallas_call | solution.py:187
  50.4 8.7 %attend_blocks.3 = (bf16[2,128,128]{2,1,0:T(8,128)(2,1)S(1)}, bf16[2,128,128]{2,1,0:T(8,128)(2,1)S(1)}, bf16[8,2,2,2,128,128]{5,4,3,2,1,0:T(8,128)(2,1)S(1)}, f3...) custom-call(s32[2,16]{1,0:T(2,128)S(1)} %fusion.37.refs_0_, ...), custom_call_target="tpu_custom_call", output_to_operand_aliasing={{3}: (15, {})} | custom-call | flops 10000000000 | bytes 25165824 | tf_op jit(solution)/shard_map/attend_blocks/pallas_call | solution.py:187
  59.1 3.5 %collective-permute-start.14 = (bf16[4,2,128,128]{3,2,1,0:T(8,128)(2,1)S(1)}, bf16[4,2,128,128]{3,2,1,0:T(8,128)(2,1)S(1)}, u32[]{:S(2)}, u32[]{:S(2)}) collective-permute-start(bf16[4,2,128,128]{3,2,1,0:T(8,128)(2,1)S(1)} %get-tuple-element.74), channel_id=1, source_target_pairs={{0,4},{1,5},{2,6},{3,7},{4,8},{5,9},{6,10},{7,11},{8,12},{9,13},{1... | collective-permute-start | bytes 786440 | tf_op jit(solution)/shard_map/ppermute | solution.py:238
  62.7 2.0 %collective-permute-start.20 = (bf16[2,2,2,2,128,128]{5,4,3,2,1,0:T(8,128)(2,1)S(1)}, bf16[2,2,2,2,128,128]{5,4,3,2,1,0:T(8,128)(2,1)S(1)}, u32[]{:S(2)}, u32[]{:S(2)}) collective-permute-start(bf16[2,2,2,2,128,128]{5,4,3,2,1,0:T(8,128)(2,1)S(1)} %get-tuple-element.95), channel_id=1, source_target_pairs={{0,16},{16,32},{32,48},{48,0},{64,80},{80,96},{96,112},{112,64},{1... | collective-permute-start | bytes 1572872 | tf_op jit(solution)/shard_map/ppermute | solution.py:243
  64.7 2.0 %collective-permute-start.12 = (bf16[4,2,128,128]{3,2,1,0:T(8,128)(2,1)S(1)}, bf16[4,2,128,128]{3,2,1,0:T(8,128)(2,1)S(1)}, u32[]{:S(2)}, u32[]{:S(2)}) collective-permute-start(bf16[4,2,128,128]{3,2,1,0:T(8,128)(2,1)S(1)} %get-tuple-element.71), channel_id=1, source_target_pairs={{0,4},{1,5},{2,6},{3,7},{4,8},{5,9},{6,10},{7,11},{8,12},{9,13},{1... | collective-permute-start | bytes 786440 | tf_op jit(solution)/shard_map/ppermute | solution.py:238
  66.7 2.5 %collective-permute-done.14 = bf16[4,2,128,128]{3,2,1,0:T(8,128)(2,1)S(1)} collective-permute-done((bf16[4,2,128,128]{3,2,1,0:T(8,128)(2,1)S(1)}, bf16[4,2,128,128]{3,2,1,0:T(8,128)(2,1)S(1)}, u32[]{:S(2)}, u32[]{:S(2)}) %collective-permute-start.14) | collective-permute-done | bytes 262176 | tf_op jit(solution)/shard_map/ppermute | solution.py:238
  69.2 1.3 collective-permute-done.15
  70.8 3.4 %collective-permute-start.18 = (bf16[4,2,128,128]{3,2,1,0:T(8,128)(2,1)S(1)}, bf16[4,2,128,128]{3,2,1,0:T(8,128)(2,1)S(1)}, u32[]{:S(2)}, u32[]{:S(2)}) collective-permute-start(bf16[4,2,128,128]{3,2,1,0:T(8,128)(2,1)S(1)} %add_convert_fusion.3), channel_id=1, source_target_pairs={{0,8},{1,9},{2,10},{3,11},{4,12},{5,13},{6,14},{7,15},{8,0},{9,1},... | collective-permute-start | bytes 786440 | tf_op jit(solution)/shard_map/ppermute | solution.py:238
  74.8 4.0 %collective-permute-start.22 = (bf16[2,2,2,2,128,128]{5,4,3,2,1,0:T(8,128)(2,1)S(1)}, bf16[2,2,2,2,128,128]{5,4,3,2,1,0:T(8,128)(2,1)S(1)}, u32[]{:S(2)}, u32[]{:S(2)}) collective-permute-start(bf16[2,2,2,2,128,128]{5,4,3,2,1,0:T(8,128)(2,1)S(1)} %get-tuple-element.96), channel_id=1, source_target_pairs={{0,48},{16,0},{32,16},{48,32},{64,112},{80,64},{96,80},{112,96},{1... | collective-permute-start | bytes 1572872 | tf_op jit(solution)/shard_map/ppermute | solution.py:243
  78.9 3.9 %collective-permute-start.21 = (bf16[2,2,2,2,128,128]{5,4,3,2,1,0:T(8,128)(2,1)S(1)}, bf16[2,2,2,2,128,128]{5,4,3,2,1,0:T(8,128)(2,1)S(1)}, u32[]{:S(2)}, u32[]{:S(2)}) collective-permute-start(bf16[2,2,2,2,128,128]{5,4,3,2,1,0:T(8,128)(2,1)S(1)} %get-tuple-element.97), channel_id=1, source_target_pairs={{0,32},{16,48},{32,0},{48,16},{64,96},{80,112},{96,64},{112,80},{1... | collective-permute-start | bytes 1572872 | tf_op jit(solution)/shard_map/ppermute | solution.py:243
  83.4 1.1 collective-permute-start.24
  84.8 2.3 %collective-permute-start.26 = (bf16[2,2,2,2,128,128]{5,4,3,2,1,0:T(8,128)(2,1)S(1)}, bf16[2,2,2,2,128,128]{5,4,3,2,1,0:T(8,128)(2,1)S(1)}, u32[]{:S(2)}, u32[]{:S(2)}) collective-permute-start(bf16[2,2,2,2,128,128]{5,4,3,2,1,0:T(8,128)(2,1)S(1)} %get-tuple-element.99), channel_id=1, source_target_pairs={{0,48},{16,0},{32,16},{48,32},{64,112},{80,64},{96,80},{112,96},{1... | collective-permute-start | bytes 1572872 | tf_op jit(solution)/shard_map/ppermute | solution.py:243
  87.0 15.4 %collective-permute-done.22 = bf16[2,2,2,2,128,128]{5,4,3,2,1,0:T(8,128)(2,1)S(1)} collective-permute-done((bf16[2,2,2,2,128,128]{5,4,3,2,1,0:T(8,128)(2,1)S(1)}, bf16[2,2,2,2,128,128]{5,4,3,2,1,0:T(8,128)(2,1)S(1)}, u32[]{:S(2)}, u32[]{:S(2)}) %collective-permute-start.22) | collective-permute-done | bytes 524320 | tf_op jit(solution)/shard_map/ppermute | solution.py:243
  102.8 3.1 %collective-permute-start.23 = (bf16[2,2,2,128,128]{4,3,2,1,0:T(8,128)(2,1)S(1)}, bf16[2,2,2,128,128]{4,3,2,1,0:T(8,128)(2,1)S(1)}, u32[]{:S(2)}, u32[]{:S(2)}) collective-permute-start(bf16[2,2,2,128,128]{4,3,2,1,0:T(8,128)(2,1)S(1)} %slice_bitcast_fusion.2), channel_id=1, source_target_pairs={{0,64},{16,80},{32,96},{48,112},{64,0},{80,16},{96,32},{112,48},{1... | collective-permute-start | bytes 786440 | tf_op jit(solution)/shard_map/ppermute | solution.py:243
  106.7 15.4 %collective-permute-done.26 = bf16[2,2,2,2,128,128]{5,4,3,2,1,0:T(8,128)(2,1)S(1)} collective-permute-done((bf16[2,2,2,2,128,128]{5,4,3,2,1,0:T(8,128)(2,1)S(1)}, bf16[2,2,2,2,128,128]{5,4,3,2,1,0:T(8,128)(2,1)S(1)}, u32[]{:S(2)}, u32[]{:S(2)}) %collective-permute-start.26) | collective-permute-done | bytes 524320 | tf_op jit(solution)/shard_map/ppermute | solution.py:243
  122.7 3.1 %collective-permute-start.28 = (bf16[2,2,2,128,128]{4,3,2,1,0:T(8,128)(2,1)S(1)}, bf16[2,2,2,128,128]{4,3,2,1,0:T(8,128)(2,1)S(1)}, u32[]{:S(2)}, u32[]{:S(2)}) collective-permute-start(bf16[2,2,2,128,128]{4,3,2,1,0:T(8,128)(2,1)S(1)} %get-tuple-element.104), channel_id=1, source_target_pairs={{0,65},{1,64},{2,67},{3,66},{4,69},{5,68},{6,71},{7,70},{8,73},{9,... | collective-permute-start | bytes 786440 | tf_op jit(solution)/shard_map/ppermute | solution.py:251
  129.8 2.5 %collective-permute-done.28 = bf16[2,2,2,128,128]{4,3,2,1,0:T(8,128)(2,1)S(1)} collective-permute-done((bf16[2,2,2,128,128]{4,3,2,1,0:T(8,128)(2,1)S(1)}, bf16[2,2,2,128,128]{4,3,2,1,0:T(8,128)(2,1)S(1)}, u32[]{:S(2)}, u32[]{:S(2)}) %collective-permute-start.28) | collective-permute-done | bytes 262176 | tf_op jit(solution)/shard_map/ppermute | solution.py:251
  132.5 1.3 copy.29
  (92 shorter events, 12.8 us)
Async XLA Ops:
  3.0 2.6 %collective-permute-start.2 = (bf16[2,2,128,128]{3,2,1,0:T(8,128)(2,1)S(1)}, bf16[2,2,128,128]{3,2,1,0:T(8,128)(2,1)S(1)}, u32[]{:S(2)}, u32[]{:S(2)}) collective-permute-start(bf16[2,2,128,128]{3,2,1,0:T(8,128)(2,1)S(1)} %pad_maximum_fusion.3), channel_id=1, source_target_pairs={{0,1},{1,0},{2,3},{3,2},{4,5},{5,4},{6,7},{7,6},{8,9},{9,8},{10,11... | collective-permute-start | bytes 393224 | tf_op jit(solution)/shard_map/ppermute | solution.py:238
  5.2 13.1 %collective-permute-start = (s32[2,17]{1,0:T(2,128)}, s32[2,17]{1,0:T(2,128)S(1)}, u32[]{:S(2)}, u32[]{:S(2)}) collective-permute-start(s32[2,17]{1,0:T(2,128)} %pad_add_fusion), channel_id=1, source_target_pairs={{0,1},{1,0},{2,3},{3,2},{4,5},{5,4},{6,7},{7,6},{8,9},{9,8},{10,11... | collective-permute-start | bytes 416 | tf_op jit(solution)/shard_map/ppermute | solution.py:238
  10.7 7.6 %copy-start.6 = (s32[2,16]{1,0:T(2,128)S(1)}, s32[2,16]{1,0:T(2,128)}, u32[]{:S(2)}) copy-start(s32[2,16]{1,0:T(2,128)} %param.14) | copy-start | bytes 388
  10.7 26.2 %copy-start = (s32[2]{0:T(128)S(1)}, s32[2]{0:T(128)}, u32[]{:S(2)}) copy-start(s32[2]{0:T(128)} %refs_1_) | copy-start | bytes 28
  10.7 26.1 %collective-permute-start.3 = (bf16[2,2,16,128,128]{4,3,2,1,0:T(8,128)(2,1)}, bf16[2,2,16,128,128]{4,3,2,1,0:T(8,128)(2,1)}, u32[]{:S(2)}, u32[]{:S(2)}) collective-permute-start(bf16[2,2,16,128,128]{4,3,2,1,0:T(8,128)(2,1)} %get-tuple-element.93), channel_id=1, source_target_pairs={{0,1},{1,0},{2,3},{3,2},{4,5},{5,4},{6,7},{7,6},{8,9},{9,8},{10,11... | collective-permute-start | bytes 6291464 | tf_op jit(solution)/shard_map/ppermute | solution.py:238
  12.1 12.7 %collective-permute-start.9 = (bf16[4,2,128,128]{3,2,1,0:T(8,128)(2,1)S(1)}, bf16[4,2,128,128]{3,2,1,0:T(8,128)(2,1)S(1)}, u32[]{:S(2)}, u32[]{:S(2)}) collective-permute-start(bf16[4,2,128,128]{3,2,1,0:T(8,128)(2,1)S(1)} %pad_maximum_fusion.refs_7_), channel_id=1, source_target_pairs={{0,4},{1,5},{2,6},{3,7},{4,8},{5,9},{6,10},{7,11},{8,12},{9,13},{1... | collective-permute-start | bytes 786440 | tf_op jit(solution)/shard_map/ppermute | solution.py:238
  13.8 15.7 %collective-permute-start.7 = (bf16[4,2,128,128]{3,2,1,0:T(8,128)(2,1)S(1)}, bf16[4,2,128,128]{3,2,1,0:T(8,128)(2,1)S(1)}, u32[]{:S(2)}, u32[]{:S(2)}) collective-permute-start(bf16[4,2,128,128]{3,2,1,0:T(8,128)(2,1)S(1)} %pad_maximum_fusion.refs_7_), channel_id=1, source_target_pairs={{0,8},{1,9},{2,10},{3,11},{4,12},{5,13},{6,14},{7,15},{8,0},{9,1},... | collective-permute-start | bytes 786440 | tf_op jit(solution)/shard_map/ppermute | solution.py:238
  16.7 8.1 %collective-permute-start.4 = (bf16[4,2,128,128]{3,2,1,0:T(8,128)(2,1)S(1)}, bf16[4,2,128,128]{3,2,1,0:T(8,128)(2,1)S(1)}, u32[]{:S(2)}, u32[]{:S(2)}) collective-permute-start(bf16[4,2,128,128]{3,2,1,0:T(8,128)(2,1)S(1)} %pad_maximum_fusion.refs_7_), channel_id=1, source_target_pairs={{0,2},{1,3},{2,0},{3,1},{4,6},{5,7},{6,4},{7,5},{8,10},{9,11},{10,... | collective-permute-start | bytes 786440 | tf_op jit(solution)/shard_map/ppermute | solution.py:238
  18.3 1.7 %collective-permute-start.1 = (bf16[3,2,128,128]{3,2,1,0:T(8,128)(2,1)}, bf16[3,2,128,128]{3,2,1,0:T(8,128)(2,1)S(1)}, u32[]{:S(2)}, u32[]{:S(2)}) collective-permute-start(bf16[3,2,128,128]{3,2,1,0:T(8,128)(2,1)} %pad_maximum_fusion.1), channel_id=1, source_target_pairs={{0,1},{1,0},{2,3},{3,2},{4,5},{5,4},{6,7},{7,6},{8,9},{9,8},{10,11... | collective-permute-start | bytes 589832 | tf_op jit(solution)/shard_map/ppermute | solution.py:238
  20.0 11.2 %collective-permute-start.5 = (bf16[4,2,128,128]{3,2,1,0:T(8,128)(2,1)S(1)}, bf16[4,2,128,128]{3,2,1,0:T(8,128)(2,1)S(1)}, u32[]{:S(2)}, u32[]{:S(2)}) collective-permute-start(bf16[4,2,128,128]{3,2,1,0:T(8,128)(2,1)S(1)} %pad_maximum_fusion.refs_7_), channel_id=1, source_target_pairs={{0,12},{1,13},{2,14},{3,15},{4,0},{5,1},{6,2},{7,3},{8,4},{9,5},{1... | collective-permute-start | bytes 786440 | tf_op jit(solution)/shard_map/ppermute | solution.py:238
  24.9 12.0 %collective-permute-start.10 = (bf16[4,2,128,128]{3,2,1,0:T(8,128)(2,1)S(1)}, bf16[4,2,128,128]{3,2,1,0:T(8,128)(2,1)S(1)}, u32[]{:S(2)}, u32[]{:S(2)}) collective-permute-start(bf16[4,2,128,128]{3,2,1,0:T(8,128)(2,1)S(1)} %collective-permute-done.4.refs_8_), channel_id=1, source_target_pairs={{0,4},{1,5},{2,6},{3,7},{4,8},{5,9},{6,10},{7,11},{8,12},{9,13},{1... | collective-permute-start | bytes 786440 | tf_op jit(solution)/shard_map/ppermute | solution.py:238
  24.9 12.0 %collective-permute-start.6 = (bf16[4,2,128,128]{3,2,1,0:T(8,128)(2,1)S(1)}, bf16[4,2,128,128]{3,2,1,0:T(8,128)(2,1)S(1)}, u32[]{:S(2)}, u32[]{:S(2)}) collective-permute-start(bf16[4,2,128,128]{3,2,1,0:T(8,128)(2,1)S(1)} %collective-permute-done.4.refs_8_), channel_id=1, source_target_pairs={{0,12},{1,13},{2,14},{3,15},{4,0},{5,1},{6,2},{7,3},{8,4},{9,5},{1... | collective-permute-start | bytes 786440 | tf_op jit(solution)/shard_map/ppermute | solution.py:238
  29.5 7.4 %collective-permute-start.8 = (bf16[4,2,128,128]{3,2,1,0:T(8,128)(2,1)S(1)}, bf16[4,2,128,128]{3,2,1,0:T(8,128)(2,1)S(1)}, u32[]{:S(2)}, u32[]{:S(2)}) collective-permute-start(bf16[4,2,128,128]{3,2,1,0:T(8,128)(2,1)S(1)} %collective-permute-done.7.refs_11_), channel_id=1, source_target_pairs={{0,2},{1,3},{2,0},{3,1},{4,6},{5,7},{6,4},{7,5},{8,10},{9,11},{10,... | collective-permute-start | bytes 786440 | tf_op jit(solution)/shard_map/ppermute | solution.py:238
  59.1 10.2 %collective-permute-start.14 = (bf16[4,2,128,128]{3,2,1,0:T(8,128)(2,1)S(1)}, bf16[4,2,128,128]{3,2,1,0:T(8,128)(2,1)S(1)}, u32[]{:S(2)}, u32[]{:S(2)}) collective-permute-start(bf16[4,2,128,128]{3,2,1,0:T(8,128)(2,1)S(1)} %get-tuple-element.74), channel_id=1, source_target_pairs={{0,4},{1,5},{2,6},{3,7},{4,8},{5,9},{6,10},{7,11},{8,12},{9,13},{1... | collective-permute-start | bytes 786440 | tf_op jit(solution)/shard_map/ppermute | solution.py:238
  62.5 8.0 %collective-permute-start.15 = (bf16[4,2,128,128]{3,2,1,0:T(8,128)(2,1)S(1)}, bf16[4,2,128,128]{3,2,1,0:T(8,128)(2,1)S(1)}, u32[]{:S(2)}, u32[]{:S(2)}) collective-permute-start(bf16[4,2,128,128]{3,2,1,0:T(8,128)(2,1)S(1)} %get-tuple-element.75), channel_id=1, source_target_pairs={{0,12},{1,13},{2,14},{3,15},{4,0},{5,1},{6,2},{7,3},{8,4},{9,5},{1... | collective-permute-start | bytes 786440 | tf_op jit(solution)/shard_map/ppermute | solution.py:238
  62.5 8.2 %collective-permute-start.17 = (bf16[4,2,128,128]{3,2,1,0:T(8,128)(2,1)S(1)}, bf16[4,2,128,128]{3,2,1,0:T(8,128)(2,1)S(1)}, u32[]{:S(2)}, u32[]{:S(2)}) collective-permute-start(bf16[4,2,128,128]{3,2,1,0:T(8,128)(2,1)S(1)} %get-tuple-element.77), channel_id=1, source_target_pairs={{0,2},{1,3},{2,0},{3,1},{4,6},{5,7},{6,4},{7,5},{8,10},{9,11},{10,... | collective-permute-start | bytes 786440 | tf_op jit(solution)/shard_map/ppermute | solution.py:238
  62.7 22.0 %collective-permute-start.20 = (bf16[2,2,2,2,128,128]{5,4,3,2,1,0:T(8,128)(2,1)S(1)}, bf16[2,2,2,2,128,128]{5,4,3,2,1,0:T(8,128)(2,1)S(1)}, u32[]{:S(2)}, u32[]{:S(2)}) collective-permute-start(bf16[2,2,2,2,128,128]{5,4,3,2,1,0:T(8,128)(2,1)S(1)} %get-tuple-element.95), channel_id=1, source_target_pairs={{0,16},{16,32},{32,48},{48,0},{64,80},{80,96},{96,112},{112,64},{1... | collective-permute-start | bytes 1572872 | tf_op jit(solution)/shard_map/ppermute | solution.py:243
  64.7 10.2 %collective-permute-start.12 = (bf16[4,2,128,128]{3,2,1,0:T(8,128)(2,1)S(1)}, bf16[4,2,128,128]{3,2,1,0:T(8,128)(2,1)S(1)}, u32[]{:S(2)}, u32[]{:S(2)}) collective-permute-start(bf16[4,2,128,128]{3,2,1,0:T(8,128)(2,1)S(1)} %get-tuple-element.71), channel_id=1, source_target_pairs={{0,4},{1,5},{2,6},{3,7},{4,8},{5,9},{6,10},{7,11},{8,12},{9,13},{1... | collective-permute-start | bytes 786440 | tf_op jit(solution)/shard_map/ppermute | solution.py:238
  69.2 9.7 %collective-permute-start.13 = (bf16[4,2,128,128]{3,2,1,0:T(8,128)(2,1)S(1)}, bf16[4,2,128,128]{3,2,1,0:T(8,128)(2,1)S(1)}, u32[]{:S(2)}, u32[]{:S(2)}) collective-permute-start(bf16[4,2,128,128]{3,2,1,0:T(8,128)(2,1)S(1)} %get-tuple-element.72), channel_id=1, source_target_pairs={{0,12},{1,13},{2,14},{3,15},{4,0},{5,1},{6,2},{7,3},{8,4},{9,5},{1... | collective-permute-start | bytes 786440 | tf_op jit(solution)/shard_map/ppermute | solution.py:238
  70.6 12.8 %collective-permute-start.16 = (bf16[4,2,128,128]{3,2,1,0:T(8,128)(2,1)S(1)}, bf16[4,2,128,128]{3,2,1,0:T(8,128)(2,1)S(1)}, u32[]{:S(2)}, u32[]{:S(2)}) collective-permute-start(bf16[4,2,128,128]{3,2,1,0:T(8,128)(2,1)S(1)} %add_convert_fusion.4), channel_id=1, source_target_pairs={{0,2},{1,3},{2,0},{3,1},{4,6},{5,7},{6,4},{7,5},{8,10},{9,11},{10,... | collective-permute-start | bytes 786440 | tf_op jit(solution)/shard_map/ppermute | solution.py:238
  70.8 12.6 %collective-permute-start.18 = (bf16[4,2,128,128]{3,2,1,0:T(8,128)(2,1)S(1)}, bf16[4,2,128,128]{3,2,1,0:T(8,128)(2,1)S(1)}, u32[]{:S(2)}, u32[]{:S(2)}) collective-permute-start(bf16[4,2,128,128]{3,2,1,0:T(8,128)(2,1)S(1)} %add_convert_fusion.3), channel_id=1, source_target_pairs={{0,8},{1,9},{2,10},{3,11},{4,12},{5,13},{6,14},{7,15},{8,0},{9,1},... | collective-permute-start | bytes 786440 | tf_op jit(solution)/shard_map/ppermute | solution.py:238
  74.8 27.6 %collective-permute-start.22 = (bf16[2,2,2,2,128,128]{5,4,3,2,1,0:T(8,128)(2,1)S(1)}, bf16[2,2,2,2,128,128]{5,4,3,2,1,0:T(8,128)(2,1)S(1)}, u32[]{:S(2)}, u32[]{:S(2)}) collective-permute-start(bf16[2,2,2,2,128,128]{5,4,3,2,1,0:T(8,128)(2,1)S(1)} %get-tuple-element.96), channel_id=1, source_target_pairs={{0,48},{16,0},{32,16},{48,32},{64,112},{80,64},{96,80},{112,96},{1... | collective-permute-start | bytes 1572872 | tf_op jit(solution)/shard_map/ppermute | solution.py:243
  78.9 23.6 %collective-permute-start.21 = (bf16[2,2,2,2,128,128]{5,4,3,2,1,0:T(8,128)(2,1)S(1)}, bf16[2,2,2,2,128,128]{5,4,3,2,1,0:T(8,128)(2,1)S(1)}, u32[]{:S(2)}, u32[]{:S(2)}) collective-permute-start(bf16[2,2,2,2,128,128]{5,4,3,2,1,0:T(8,128)(2,1)S(1)} %get-tuple-element.97), channel_id=1, source_target_pairs={{0,32},{16,48},{32,0},{48,16},{64,96},{80,112},{96,64},{112,80},{1... | collective-permute-start | bytes 1572872 | tf_op jit(solution)/shard_map/ppermute | solution.py:243
  83.4 42.6 %collective-permute-start.11 = (bf16[2,2,128,128]{3,2,1,0:T(8,128)(2,1)}, bf16[2,2,128,128]{3,2,1,0:T(8,128)(2,1)S(1)}, u32[]{:S(2)}, u32[]{:S(2)}) collective-permute-start(bf16[2,2,128,128]{3,2,1,0:T(8,128)(2,1)} %pad_maximum_fusion.4), channel_id=1, source_target_pairs={{0,1},{1,0},{2,3},{3,2},{4,5},{5,4},{6,7},{7,6},{8,9},{9,8},{10,11... | collective-permute-start | bytes 393224 | tf_op jit(solution)/shard_map/ppermute | solution.py:238
  83.4 23.3 %collective-permute-start.24 = (bf16[2,2,2,2,128,128]{5,4,3,2,1,0:T(8,128)(2,1)S(1)}, bf16[2,2,2,2,128,128]{5,4,3,2,1,0:T(8,128)(2,1)S(1)}, u32[]{:S(2)}, u32[]{:S(2)}) collective-permute-start(bf16[2,2,2,2,128,128]{5,4,3,2,1,0:T(8,128)(2,1)S(1)} %get-tuple-element.98), channel_id=1, source_target_pairs={{0,16},{16,32},{32,48},{48,0},{64,80},{80,96},{96,112},{112,64},{1... | collective-permute-start | bytes 1572872 | tf_op jit(solution)/shard_map/ppermute | solution.py:243
  84.8 37.4 %collective-permute-start.26 = (bf16[2,2,2,2,128,128]{5,4,3,2,1,0:T(8,128)(2,1)S(1)}, bf16[2,2,2,2,128,128]{5,4,3,2,1,0:T(8,128)(2,1)S(1)}, u32[]{:S(2)}, u32[]{:S(2)}) collective-permute-start(bf16[2,2,2,2,128,128]{5,4,3,2,1,0:T(8,128)(2,1)S(1)} %get-tuple-element.99), channel_id=1, source_target_pairs={{0,48},{16,0},{32,16},{48,32},{64,112},{80,64},{96,80},{112,96},{1... | collective-permute-start | bytes 1572872 | tf_op jit(solution)/shard_map/ppermute | solution.py:243
  102.4 19.8 %collective-permute-start.25 = (bf16[2,2,2,2,128,128]{5,4,3,2,1,0:T(8,128)(2,1)S(1)}, bf16[2,2,2,2,128,128]{5,4,3,2,1,0:T(8,128)(2,1)S(1)}, u32[]{:S(2)}, u32[]{:S(2)}) collective-permute-start(bf16[2,2,2,2,128,128]{5,4,3,2,1,0:T(8,128)(2,1)S(1)} %get-tuple-element.100), channel_id=1, source_target_pairs={{0,32},{16,48},{32,0},{48,16},{64,96},{80,112},{96,64},{112,80},{1... | collective-permute-start | bytes 1572872 | tf_op jit(solution)/shard_map/ppermute | solution.py:243
  102.8 23.2 %copy-start.2 = (bf16[2,128,128]{2,1,0:T(8,128)(2,1)S(1)}, bf16[2,128,128]{2,1,0:T(8,128)(2,1)}, u32[]{:S(2)}) copy-start(bf16[2,128,128]{2,1,0:T(8,128)(2,1)} %copy-done.1) | copy-start | bytes 196612
  102.8 27.0 %collective-permute-start.23 = (bf16[2,2,2,128,128]{4,3,2,1,0:T(8,128)(2,1)S(1)}, bf16[2,2,2,128,128]{4,3,2,1,0:T(8,128)(2,1)S(1)}, u32[]{:S(2)}, u32[]{:S(2)}) collective-permute-start(bf16[2,2,2,128,128]{4,3,2,1,0:T(8,128)(2,1)S(1)} %slice_bitcast_fusion.2), channel_id=1, source_target_pairs={{0,64},{16,80},{32,96},{48,112},{64,0},{80,16},{96,32},{112,48},{1... | collective-permute-start | bytes 786440 | tf_op jit(solution)/shard_map/ppermute | solution.py:243
  122.6 7.2 %collective-permute-start.27 = (bf16[2,2,2,128,128]{4,3,2,1,0:T(8,128)(2,1)S(1)}, bf16[2,2,2,128,128]{4,3,2,1,0:T(8,128)(2,1)S(1)}, u32[]{:S(2)}, u32[]{:S(2)}) collective-permute-start(bf16[2,2,2,128,128]{4,3,2,1,0:T(8,128)(2,1)S(1)} %get-tuple-element.103), channel_id=1, source_target_pairs={{0,1},{1,0},{2,3},{3,2},{4,5},{5,4},{6,7},{7,6},{8,9},{9,8},{10,11... | collective-permute-start | bytes 786440 | tf_op jit(solution)/shard_map/ppermute | solution.py:238
  122.7 9.6 %collective-permute-start.28 = (bf16[2,2,2,128,128]{4,3,2,1,0:T(8,128)(2,1)S(1)}, bf16[2,2,2,128,128]{4,3,2,1,0:T(8,128)(2,1)S(1)}, u32[]{:S(2)}, u32[]{:S(2)}) collective-permute-start(bf16[2,2,2,128,128]{4,3,2,1,0:T(8,128)(2,1)S(1)} %get-tuple-element.104), channel_id=1, source_target_pairs={{0,65},{1,64},{2,67},{3,66},{4,69},{5,68},{6,71},{7,70},{8,73},{9,... | collective-permute-start | bytes 786440 | tf_op jit(solution)/shard_map/ppermute | solution.py:251
  125.8 2.1 %collective-permute-start.19 = (bf16[2,2,128,128]{3,2,1,0:T(8,128)(2,1)S(1)}, bf16[2,2,128,128]{3,2,1,0:T(8,128)(2,1)S(1)}, u32[]{:S(2)}, u32[]{:S(2)}) collective-permute-start(bf16[2,2,128,128]{3,2,1,0:T(8,128)(2,1)S(1)} %get-tuple-element.105), channel_id=1, source_target_pairs={{0,1},{1,0},{2,3},{3,2},{4,5},{5,4},{6,7},{7,6},{8,9},{9,8},{10,11... | collective-permute-start | bytes 393224 | tf_op jit(solution)/shard_map/ppermute | solution.py:238
  (4 other events, 6.4 us)

commit v2 on v1

--- a/solution.py
+++ b/solution.py
@@ -33,15 +33,16 @@
 
 
 def attend_kernel(first,*refs):
-    idx,cnt,chk,q,gate,cot,bias=refs[:7]
-    pieces=refs[7:15]
+    idx,cnt,chk,qgc,bias=refs[:5]
+    q,gate,cot=qgc.at[0],qgc.at[1],qgc.at[2]
+    pieces=refs[5:13]
     if first:
-        dq,gg,bg,acc=refs[15:19]
-        rest=refs[19:]
+        dq,gg,bg,acc=refs[13:17]
+        rest=refs[17:]
     else:
-        dq,gg,bg,acc=refs[16:20]
-        terms=refs[20:28]
-        rest=refs[28:]
+        dq,gg,bg,acc=refs[14:18]
+        terms=refs[18:26]
+        rest=refs[26:]
     s_ref,e_ref,m_ref,l_ref,o_ref,off_ref,qm,qt,dom,domt,kv,sem=rest
     for m in range(8):
         pltpu.make_async_copy(pieces[m],kv.at[pl.ds(4*m,4)],sem.at[m]).start()
@@ -125,7 +126,7 @@
 
         def backward(p,c):
             a0=idx[j,2*p]; a1=idx[j,2*p+1]
-            ch=chk[p]
+            out=bg.at[chk[0,p],j] if first else bg.at[j,chk[j,p]]
             k2=both(p,0); v2=both(p,1)
             halves=[]; total=[None,None]
             WG=dot(dom[...],v2,NT)
@@ -137,7 +138,7 @@
                 if g<2: total[h]=ds
                 else:
                     b=(total[h]+ds).astype(BF)
-                    bg[ch,j,h,0]=b[:,:BS]; bg[ch,j,h,1]=b[:,BS:]
+                    out[h,0]=b[:,:BS]; out[h,1]=b[:,BS:]
                 half=ds.astype(BF)
                 halves.append(half)
             hs=jnp.concatenate(halves,0)
@@ -151,8 +152,8 @@
         loop2(pairs,backward)
 
         def clear(p,c):
-            z=jnp.zeros((2,2,BS,BS),BF)
-            bg[chk[p],j]=z
+            out=bg.at[chk[0,p],j] if first else bg.at[j,chk[j,p]]
+            out[...]=jnp.zeros((2,2,BS,BS),BF)
             return c
 
         lax.fori_loop(pairs,8,clear,0)
@@ -168,14 +169,15 @@
             terms[m][...]=acc[4*m:4*m+4].astype(BF)
 
 
-def attend_blocks(idx,cnt,chk,q,gate,cot,bias,pieces,prev):
+def attend_blocks(idx,cnt,chk,qgc,bias,pieces,prev):
     first=prev is None
     SM=pl.BlockSpec(memory_space=pltpu.SMEM)
     VM=pl.BlockSpec(memory_space=pltpu.VMEM)
     AN=pl.BlockSpec(memory_space=pl.ANY)
-    args=[idx,cnt,chk,q,gate,cot,bias,*pieces]
-    specs=[SM]*3+[VM]*4+[AN]*8
-    shapes=[((2,BS,BS),BF),((2,BS,BS),BF),((8,2,2,2,BS,BS),BF),((32,2,BS,BS),F32)]
+    args=[idx,cnt,chk,qgc,bias,*pieces]
+    specs=[SM]*3+[VM]*2+[AN]*8
+    lead=(8,2) if first else (2,8)
+    shapes=[((2,BS,BS),BF),((2,BS,BS),BF),(lead+(2,2,BS,BS),BF),((32,2,BS,BS),F32)]
     if not first:
         args.append(prev)
         specs.append(VM)
@@ -193,7 +195,7 @@
         +[pltpu.VMEM((G*BS,BS),F32)]*4
         +[pltpu.VMEM((G*BS,BS),BF),pltpu.VMEM((BS,G*BS),BF)]*2
         +[pltpu.VMEM((32,2,BS,BS),BF),pltpu.SemaphoreType.DMA((8,))],
-        input_output_aliases={} if first else {15:3},
+        input_output_aliases={} if first else {13:3},
         compiler_params=pltpu.CompilerParams(vmem_limit_bytes=20<<20),
         cost_estimate=pl.CostEstimate(flops=10_000_000_000,bytes_accessed=24<<20,transcendentals=4<<20),
         name="attend_blocks",
@@ -315,52 +317,58 @@
     bias_mine=lax.dynamic_slice_in_dim(bias,2*core,2,1)
     bias_other=swap(lax.dynamic_slice_in_dim(bias,2-2*core,2,1))
     parts=[split(x) for x in (query_vectors,gate_logits,cotangent)]
-    mine=[p[0] for p in parts]
+    mine=jnp.stack([p[0] for p in parts],0)
     other=swap(jnp.stack([p[1] for p in parts],0))
 
     ready=(places(tables[0]),tables[0][:,TAB],places(tables[1]),tables[1][:,TAB],mine,other,bias_mine,bias_other,pieces)
     idx0,cnt0,idx1,cnt1,mine,other,bias_mine,bias_other,pieces=lax.optimization_barrier(ready)
-    dq0,gg0,bg0,acc=attend_blocks(idx0,cnt0,turn*2+far,*mine,bias_mine,pieces,None)
-    bg0=bg0.reshape(4,2,2,2,2,BS,BS)
+    by_z,by_x=turn*2+far,far*4+turn
 
     def row_sums(x):
         out=[x[0]]
         for dz in range(1,4):
             out.append(to_row(x[dz],0,dz))
-        return out
-
-    bg0=row_sums(bg0)
-    dq1,gg1,bg1,_,*t=attend_blocks(
-        idx1,cnt1,turn*2+far,other[0],other[1],other[2],bias_other,pieces,acc
-    )
-    bg1=bg1.reshape(4,2,2,2,2,BS,BS)
+        return plus(*out)
 
     def step(x,dy,dx):
         return to_col(x,dy,dx,0)
 
-    from_down,from_up=step(t[3],1,0),step(t[7],3,0)
-    from_near=step(t[5],0,1)
-    bg1=row_sums(bg1)
-    steps=[step(t[2],1,0),step(t[6],3,0)]
-    bg0=plus(*bg0).astype(BF)
-    bg0_far=to_row(bg0[1],1,0)
-    steps.append(step(plus(t[1],from_down,from_up).astype(BF),0,1))
-    steps.append(step(plus(t[4],from_near).astype(BF),2,0))
+    dq1,gg1,bg1,acc=attend_blocks(idx1,cnt1,by_z[None],other,bias_other,pieces,None)
     q_back=swap(jnp.stack([dq1,gg1],0))
+    bg1=row_sums(bg1.reshape(4,2,2,2,2,BS,BS)).astype(BF)
+    dq0,gg0,bg0,_,*t=attend_blocks(
+        idx0,cnt0,jnp.stack([by_z,by_x],0),mine,bias_mine,pieces,acc
+    )
+
+    straight=bg0[0].reshape(4,2,2,2,BS,BS)
+    turned=bg0[1].reshape(2,4,2,2,BS,BS)
+    turned_in=to_row(turned[1],1,0)
+    straight=row_sums(straight).astype(BF)
+    turned=plus(turned[0],turned_in).astype(BF)
+    up=step(jnp.stack([t[2],t[3]],0),1,0)
+    down=step(jnp.stack([t[6],t[7]],0),3,0)
+    near=step(t[5],0,1)
+    steps=[up[0],down[0]]
+    side=plus(t[1],up[1],down[1]).astype(BF)
+    over=plus(t[4],near).astype(BF)
+    steps+=[step(side,0,1),step(over,2,0)]
+    bias_far=cross(bg1[1])
+    bias_near=swap(bg1[0])
+    bias_other=plus(bias_near,bias_far).astype(BF)
+    straight_in=to_row(straight[1],1,0)
+    straight=plus(straight[0],straight_in).astype(BF)
+    turned=row_sums(turned).astype(BF)
+
     query_grad,gate_grad=small_call(unite_kernel,dq0,gg0,q_back,sel)
-    bias0=plus(bg0[0],bg0_far).astype(BF)
     own=plus(t[0],*steps)
     own=jnp.stack([own[:,0]*SCALE,own[:,1]],1).astype(BF)
     own_far=swap(own[2:])
     key_grad,value_grad=small_call(join_kernel,own[:2],own_far,sel)
 
-    bg1=plus(*bg1).astype(BF)
-    turned=cross(bg1[1])
-    bias1=plus(swap(bg1[0]),turned).astype(BF)
-
-    a=jnp.where(core==0,bias0,bias1)
-    b=jnp.where(core==0,bias1,bias0)
-    bias_grad=jnp.concatenate([a,b],1).transpose(0,1,3,2,4)
+    bias_own=jnp.stack([straight,turned],0)
+    low=jnp.where(core==0,bias_own,bias_other)
+    high=jnp.where(core==0,bias_other,bias_own)
+    bias_grad=jnp.concatenate([low,high],1).transpose(0,1,3,2,4)
 
     def rows(x):
         return x.transpose(1,0,2)

time: 135 us -> 153 us (1.13)
  the two profiles are of different devices: /device:TPU:0 before, /device:TPU:9 now
where the time goes in v2:
time: 153 us
  waiting for transfers between devices  58.4 us (38%)
  starting transfers between devices  50.1 us (33%)
  Pallas kernels  25.8 us (17%)
  local copies, waits for them, and re-layouts  10.9 us (7%)
  matrix products  3.64 us (2%)
  other arithmetic  3.12 us (2%)
    ppermute x19, waiting for transfers between devices, to_col(): return lax.ppermute(x, 'col', pairs)  38 us
    ppermute x19, starting transfers between devices, to_col(): return lax.ppermute(x, 'col', pairs)  35.6 us
    pallas_call x2, Pallas kernels, attend_blocks(): pl.pallas_call(kernel, out_shape=tuple((jax.ShapeDtypeStruct(*s) for s in...  25.2 us
    ppermute x11, waiting for transfers between devices, to_row(): return lax.ppermute(x, 'row', pairs)  16.7 us
    ppermute x11, starting transfers between devices, to_row(): return lax.ppermute(x, 'row', pairs)  14 us
    unnamed x13, local copies, waits for them, and re-layouts  4.52 us
    ppermute x1, waiting for transfers between devices, cross(): return lax.ppermute(x, ('row', 'col'), pairs)  3.69 us
    dot_general x5, matrix products, split(): lax.dot_general(x.reshape(2 * BS, 2 * BS), sel, NN, preferred_element_typ...  3.64 us
  transfers between devices with their start and end apart: 31, of which 14 were waited for; matrix products, arithmetic and copies ran while one was open for 9% of the time, Pallas kernels for 0%

profile of v2, /device:TPU:9, one launch (start us, length us, event | category | flops | bytes accessed | tf_op | source)
XLA Modules:
  0.0 153.1 jit_solution(4889138581680061290)
XLA Ops:
  0.8 1.1 fusion.3
  1.9 1.1 fusion.4
  5.3 1.1 fusion
  6.4 3.4 %copy.23 = bf16[2,4,128,16,128]{4,2,3,1,0:T(8,128)(2,1)S(1)} copy(bf16[2,4,128,16,128]{4,3,2,1,0:T(8,128)(2,1)} %param.13) | data formatting | bytes 8388608 | tf_op jit(solution)/shard_map/optimization_barrier | solution.py:294
  9.8 1.6 %dynamic-slice_bitcast_fusion = (bf16[2,2,16,128,128]{4,3,2,1,0:T(8,128)(2,1)}, bf16[2,2,16,128,128]{4,3,2,1,0:T(8,128)(2,1)S(1)}) fusion(bf16[2,4,128,16,128]{4,2,3,1,0:T(8,128)(2,1)S(1)} %copy.23, s32[]{:T(128)S(6)} %select_n.186, s32[]{:T(128)S(6)} %select_n.185), kind=kLoop, calls=%fused_computation | loop fusion | bytes 8388616 | tf_op jit(solution)/shard_map/dynamic_slice | solution.py:318
  13.2 1.3 collective-permute-start.4
  14.5 2.0 %collective-permute-start.7 = (bf16[4,2,128,128]{3,2,1,0:T(8,128)(2,1)S(1)}, bf16[4,2,128,128]{3,2,1,0:T(8,128)(2,1)S(1)}, u32[]{:S(2)}, u32[]{:S(2)}) collective-permute-start(bf16[4,2,128,128]{3,2,1,0:T(8,128)(2,1)S(1)} %pad_maximum_fusion.2.refs_5_), channel_id=1, source_target_pairs={{0,8},{1,9},{2,10},{3,11},{4,12},{5,13},{6,14},{7,15},{8,0},{9,1},... | collective-permute-start | bytes 786440 | tf_op jit(solution)/shard_map/ppermute | solution.py:240
  18.5 1.2 collective-permute-done.1.refs_3_
  21.1 1.3 collective-permute-start.10
  22.4 1.2 collective-permute-done.7.refs_9_
  23.7 6.1 %collective-permute-done.5.refs_7_ = bf16[4,2,128,128]{3,2,1,0:T(8,128)(2,1)S(1)} collective-permute-done((bf16[4,2,128,128]{3,2,1,0:T(8,128)(2,1)S(1)}, bf16[4,2,128,128]{3,2,1,0:T(8,128)(2,1)S(1)}, u32[]{:S(2)}, u32[]{:S(2)}) %collective-permute-start.5) | collective-permute-done | bytes 262176 | tf_op jit(solution)/shard_map/ppermute | solution.py:240
  30.3 4.6 %collective-permute-done.10.refs_12_ = bf16[4,2,128,128]{3,2,1,0:T(8,128)(2,1)S(1)} collective-permute-done((bf16[4,2,128,128]{3,2,1,0:T(8,128)(2,1)S(1)}, bf16[4,2,128,128]{3,2,1,0:T(8,128)(2,1)S(1)}, u32[]{:S(2)}, u32[]{:S(2)}) %collective-permute-start.10) | collective-permute-done | bytes 262176 | tf_op jit(solution)/shard_map/ppermute | solution.py:240
  35.4 1.7 %collective-permute-done.8.refs_10_ = bf16[4,2,128,128]{3,2,1,0:T(8,128)(2,1)S(1)} collective-permute-done((bf16[4,2,128,128]{3,2,1,0:T(8,128)(2,1)S(1)}, bf16[4,2,128,128]{3,2,1,0:T(8,128)(2,1)S(1)}, u32[]{:S(2)}, u32[]{:S(2)}) %collective-permute-start.8) | collective-permute-done | bytes 262176 | tf_op jit(solution)/shard_map/ppermute | solution.py:240
  37.1 13.9 %attend_blocks.2 = (bf16[2,128,128]{2,1,0:T(8,128)(2,1)S(1)}, bf16[2,128,128]{2,1,0:T(8,128)(2,1)S(1)}, bf16[8,2,2,2,128,128]{5,4,3,2,1,0:T(8,128)(2,1)S(1)}, f32[32,2,128,128]{3,2,1,0:T(8,128)S(1)}) custom-call(s32[2,16]{1,0:T(2,128)S(1)} %fusion.49.refs_0_, s32[2]{0:T(128)S(1)} %slice_reduce_fusion.refs_1_, s32[1,8]{1,0:T(1,128)S(1)} %get-tuple-element.117.refs_2_, ...), custom_call_target="tpu_custom_call" | custom-call | flops 10000000000 | bytes 25165824 | tf_op jit(solution)/shard_map/attend_blocks/pallas_call | solution.py:189
  51.0 11.4 %attend_blocks.3 = (bf16[2,128,128]{2,1,0:T(8,128)(2,1)S(1)}, bf16[2,128,128]{2,1,0:T(8,128)(2,1)S(1)}, bf16[2,8,2,2,128,128]{5,4,3,2,1,0:T(8,128)(2,1)S(1)}, f3...) custom-call(s32[2,16]{1,0:T(2,128)S(1)} %fusion.44.refs_0_, ...), custom_call_target="tpu_custom_call", output_to_operand_aliasing={{3}: (13, {})} | custom-call | flops 10000000000 | bytes 25165824 | tf_op jit(solution)/shard_map/attend_blocks/pallas_call | solution.py:189
  62.6 1.9 %collective-permute-start.26 = (bf16[2,2,2,2,128,128]{5,4,3,2,1,0:T(8,128)(2,1)S(1)}, bf16[2,2,2,2,128,128]{5,4,3,2,1,0:T(8,128)(2,1)S(1)}, u32[]{:S(2)}, u32[]{:S(2)}) collective-permute-start(bf16[2,2,2,2,128,128]{5,4,3,2,1,0:T(8,128)(2,1)S(1)} %get-tuple-element.91), channel_id=1, source_target_pairs={{0,16},{16,32},{32,48},{48,0},{64,80},{80,96},{96,112},{112,64},{1... | collective-permute-start | bytes 1572872 | tf_op jit(solution)/shard_map/ppermute | solution.py:245
  64.5 1.6 %collective-permute-start.18 = (bf16[2,2,2,128,128]{4,3,2,1,0:T(8,128)(2,1)S(1)}, bf16[2,2,2,128,128]{4,3,2,1,0:T(8,128)(2,1)S(1)}, u32[]{:S(2)}, u32[]{:S(2)}) collective-permute-start(bf16[2,2,2,128,128]{4,3,2,1,0:T(8,128)(2,1)S(1)} %get-tuple-element.94), channel_id=1, source_target_pairs={{0,16},{16,32},{32,48},{48,0},{64,80},{80,96},{96,112},{112,64},{1... | collective-permute-start | bytes 786440 | tf_op jit(solution)/shard_map/ppermute | solution.py:245
  66.2 1.8 %collective-permute-start.19 = (bf16[2,2,2,128,128]{4,3,2,1,0:T(8,128)(2,1)S(1)}, bf16[2,2,2,128,128]{4,3,2,1,0:T(8,128)(2,1)S(1)}, u32[]{:S(2)}, u32[]{:S(2)}) collective-permute-start(bf16[2,2,2,128,128]{4,3,2,1,0:T(8,128)(2,1)S(1)} %get-tuple-element.96), channel_id=1, source_target_pairs={{0,32},{16,48},{32,0},{48,16},{64,96},{80,112},{96,64},{112,80},{1... | collective-permute-start | bytes 786440 | tf_op jit(solution)/shard_map/ppermute | solution.py:245
  67.9 2.0 %collective-permute-start.20 = (bf16[2,2,2,128,128]{4,3,2,1,0:T(8,128)(2,1)S(1)}, bf16[2,2,2,128,128]{4,3,2,1,0:T(8,128)(2,1)S(1)}, u32[]{:S(2)}, u32[]{:S(2)}) collective-permute-start(bf16[2,2,2,128,128]{4,3,2,1,0:T(8,128)(2,1)S(1)} %get-tuple-element.95), channel_id=1, source_target_pairs={{0,48},{16,0},{32,16},{48,32},{64,112},{80,64},{96,80},{112,96},{1... | collective-permute-start | bytes 786440 | tf_op jit(solution)/shard_map/ppermute | solution.py:245
  69.9 2.7 %collective-permute-start.11 = (bf16[2,2,128,128]{3,2,1,0:T(8,128)(2,1)S(1)}, bf16[2,2,128,128]{3,2,1,0:T(8,128)(2,1)S(1)}, u32[]{:S(2)}, u32[]{:S(2)}) collective-permute-start(bf16[2,2,128,128]{3,2,1,0:T(8,128)(2,1)S(1)} %pad_maximum_fusion.8), channel_id=1, source_target_pairs={{0,1},{1,0},{2,3},{3,2},{4,5},{5,4},{6,7},{7,6},{8,9},{9,8},{10,11... | collective-permute-start | bytes 393224 | tf_op jit(solution)/shard_map/ppermute | solution.py:240
  75.5 7.7 %collective-permute-done.18 = bf16[2,2,2,128,128]{4,3,2,1,0:T(8,128)(2,1)S(1)} collective-permute-done((bf16[2,2,2,128,128]{4,3,2,1,0:T(8,128)(2,1)S(1)}, bf16[2,2,2,128,128]{4,3,2,1,0:T(8,128)(2,1)S(1)}, u32[]{:S(2)}, u32[]{:S(2)}) %collective-permute-start.18) | collective-permute-done | bytes 262176 | tf_op jit(solution)/shard_map/ppermute | solution.py:245
  83.1 2.5 %collective-permute-start.22 = (bf16[4,2,2,128,128]{4,3,2,1,0:T(8,128)(2,1)S(1)}, bf16[4,2,2,128,128]{4,3,2,1,0:T(8,128)(2,1)S(1)}, u32[]{:S(2)}, u32[]{:S(2)}) collective-permute-start(bf16[4,2,2,128,128]{4,3,2,1,0:T(8,128)(2,1)S(1)} %slice_bitcast_fusion), channel_id=1, source_target_pairs={{0,64},{16,80},{32,96},{48,112},{64,0},{80,16},{96,32},{112,48},{1... | collective-permute-start | bytes 1572872 | tf_op jit(solution)/shard_map/ppermute | solution.py:245
  85.6 4.1 %collective-permute-done.19 = bf16[2,2,2,128,128]{4,3,2,1,0:T(8,128)(2,1)S(1)} collective-permute-done((bf16[2,2,2,128,128]{4,3,2,1,0:T(8,128)(2,1)S(1)}, bf16[2,2,2,128,128]{4,3,2,1,0:T(8,128)(2,1)S(1)}, u32[]{:S(2)}, u32[]{:S(2)}) %collective-permute-start.19) | collective-permute-done | bytes 262176 | tf_op jit(solution)/shard_map/ppermute | solution.py:245
  89.8 9.9 %collective-permute-done.15 = bf16[4,2,128,128]{3,2,1,0:T(8,128)(2,1)S(1)} collective-permute-done((bf16[4,2,128,128]{3,2,1,0:T(8,128)(2,1)S(1)}, bf16[4,2,128,128]{3,2,1,0:T(8,128)(2,1)S(1)}, u32[]{:S(2)}, u32[]{:S(2)}) %collective-permute-start.15) | collective-permute-done | bytes 262176 | tf_op jit(solution)/shard_map/ppermute | solution.py:240
  100.3 5.0 %collective-permute-done.21 = bf16[2,2,128,128]{3,2,1,0:T(8,128)(2,1)S(1)} collective-permute-done((bf16[2,2,128,128]{3,2,1,0:T(8,128)(2,1)S(1)}, bf16[2,2,128,128]{3,2,1,0:T(8,128)(2,1)S(1)}, u32[]{:S(2)}, u32[]{:S(2)}) %collective-permute-start.21) | collective-permute-done | bytes 131104 | tf_op jit(solution)/shard_map/ppermute | solution.py:245
  106.5 10.9 %collective-permute-done.13 = bf16[2,4,2,128,128]{4,3,2,1,0:T(8,128)(2,1)S(1)} collective-permute-done((bf16[2,4,2,128,128]{4,3,2,1,0:T(8,128)(2,1)S(1)}, bf16[2,4,2,128,128]{4,3,2,1,0:T(8,128)(2,1)S(1)}, u32[]{:S(2)}, u32[]{:S(2)}) %collective-permute-start.13) | collective-permute-done | bytes 524320 | tf_op jit(solution)/shard_map/ppermute | solution.py:240
  117.6 2.7 %collective-permute-start.24 = (bf16[2,2,128,128]{3,2,1,0:T(8,128)(2,1)S(1)}, bf16[2,2,128,128]{3,2,1,0:T(8,128)(2,1)S(1)}, u32[]{:S(2)}, u32[]{:S(2)}) collective-permute-start(bf16[2,2,128,128]{3,2,1,0:T(8,128)(2,1)S(1)} %get-tuple-element.103), channel_id=1, source_target_pairs={{0,32},{16,48},{32,0},{48,16},{64,96},{80,112},{96,64},{112,80},{1... | collective-permute-start | bytes 393224 | tf_op jit(solution)/shard_map/ppermute | solution.py:245
  120.4 1.8 %collective-permute-start.14 = (bf16[4,2,128,128]{3,2,1,0:T(8,128)(2,1)S(1)}, bf16[4,2,128,128]{3,2,1,0:T(8,128)(2,1)S(1)}, u32[]{:S(2)}, u32[]{:S(2)}) collective-permute-start(bf16[4,2,128,128]{3,2,1,0:T(8,128)(2,1)S(1)} %fusion.9), channel_id=1, source_target_pairs={{0,2},{1,3},{2,0},{3,1},{4,6},{5,7},{6,4},{7,5},{8,10},{9,11},{10,... | collective-permute-start | bytes 786440 | tf_op jit(solution)/shard_map/ppermute | solution.py:240
  122.6 17.5 %collective-permute-start.29 = (bf16[2,2,2,128,128]{4,3,2,1,0:T(8,128)(2,1)S(1)}, bf16[2,2,2,128,128]{4,3,2,1,0:T(8,128)(2,1)S(1)}, u32[]{:S(2)}, u32[]{:S(2)}) collective-permute-start(bf16[2,2,2,128,128]{4,3,2,1,0:T(8,128)(2,1)S(1)} %get-tuple-element.99), channel_id=1, source_target_pairs={{0,1},{1,0},{2,3},{3,2},{4,5},{5,4},{6,7},{7,6},{8,9},{9,8},{10,11... | collective-permute-start | bytes 786440 | tf_op jit(solution)/shard_map/ppermute | solution.py:240
  140.9 5.0 %collective-permute-start.17 = (bf16[2,2,128,128]{3,2,1,0:T(8,128)(2,1)S(1)}, bf16[2,2,128,128]{3,2,1,0:T(8,128)(2,1)S(1)}, u32[]{:S(2)}, u32[]{:S(2)}) collective-permute-start(bf16[2,2,128,128]{3,2,1,0:T(8,128)(2,1)S(1)} %get-tuple-element.104), channel_id=1, source_target_pairs={{0,1},{1,0},{2,3},{3,2},{4,5},{5,4},{6,7},{7,6},{8,9},{9,8},{10,11... | collective-permute-start | bytes 393224 | tf_op jit(solution)/shard_map/ppermute | solution.py:240
  146.0 3.7 %collective-permute-done.30 = bf16[2,2,2,128,128]{4,3,2,1,0:T(8,128)(2,1)S(1)} collective-permute-done((bf16[2,2,2,128,128]{4,3,2,1,0:T(8,128)(2,1)S(1)}, bf16[2,2,2,128,128]{4,3,2,1,0:T(8,128)(2,1)S(1)}, u32[]{:S(2)}, u32[]{:S(2)}) %collective-permute-start.30) | collective-permute-done | bytes 262176 | tf_op jit(solution)/shard_map/ppermute | solution.py:253
  149.9 1.3 copy.29
  (98 shorter events, 17.2 us)
Async XLA Ops:
  3.0 3.4 %collective-permute-start.2 = (bf16[2,2,128,128]{3,2,1,0:T(8,128)(2,1)S(1)}, bf16[2,2,128,128]{3,2,1,0:T(8,128)(2,1)S(1)}, u32[]{:S(2)}, u32[]{:S(2)}) collective-permute-start(bf16[2,2,128,128]{3,2,1,0:T(8,128)(2,1)S(1)} %pad_maximum_fusion.7), channel_id=1, source_target_pairs={{0,1},{1,0},{2,3},{3,2},{4,5},{5,4},{6,7},{7,6},{8,9},{9,8},{10,11... | collective-permute-start | bytes 393224 | tf_op jit(solution)/shard_map/ppermute | solution.py:240
  5.3 12.3 %collective-permute-start = (s32[2,17]{1,0:T(2,128)S(1)}, s32[2,17]{1,0:T(2,128)S(1)}, u32[]{:S(2)}, u32[]{:S(2)}) collective-permute-start(s32[2,17]{1,0:T(2,128)S(1)} %pad_add_fusion), channel_id=1, source_target_pairs={{0,1},{1,0},{2,3},{3,2},{4,5},{5,4},{6,7},{7,6},{8,9},{9,8},{10,11... | collective-permute-start | bytes 416 | tf_op jit(solution)/shard_map/ppermute | solution.py:240
  11.5 25.6 %collective-permute-start.3 = (bf16[2,2,16,128,128]{4,3,2,1,0:T(8,128)(2,1)}, bf16[2,2,16,128,128]{4,3,2,1,0:T(8,128)(2,1)}, u32[]{:S(2)}, u32[]{:S(2)}) collective-permute-start(bf16[2,2,16,128,128]{4,3,2,1,0:T(8,128)(2,1)} %get-tuple-element.89), channel_id=1, source_target_pairs={{0,1},{1,0},{2,3},{3,2},{4,5},{5,4},{6,7},{7,6},{8,9},{9,8},{10,11... | collective-permute-start | bytes 6291464 | tf_op jit(solution)/shard_map/ppermute | solution.py:240
  13.2 7.9 %collective-permute-start.4 = (bf16[4,2,128,128]{3,2,1,0:T(8,128)(2,1)S(1)}, bf16[4,2,128,128]{3,2,1,0:T(8,128)(2,1)S(1)}, u32[]{:S(2)}, u32[]{:S(2)}) collective-permute-start(bf16[4,2,128,128]{3,2,1,0:T(8,128)(2,1)S(1)} %pad_maximum_fusion.2.refs_5_), channel_id=1, source_target_pairs={{0,2},{1,3},{2,0},{3,1},{4,6},{5,7},{6,4},{7,5},{8,10},{9,11},{10,... | collective-permute-start | bytes 786440 | tf_op jit(solution)/shard_map/ppermute | solution.py:240
  14.5 9.1 %collective-permute-start.7 = (bf16[4,2,128,128]{3,2,1,0:T(8,128)(2,1)S(1)}, bf16[4,2,128,128]{3,2,1,0:T(8,128)(2,1)S(1)}, u32[]{:S(2)}, u32[]{:S(2)}) collective-permute-start(bf16[4,2,128,128]{3,2,1,0:T(8,128)(2,1)S(1)} %pad_maximum_fusion.2.refs_5_), channel_id=1, source_target_pairs={{0,8},{1,9},{2,10},{3,11},{4,12},{5,13},{6,14},{7,15},{8,0},{9,1},... | collective-permute-start | bytes 786440 | tf_op jit(solution)/shard_map/ppermute | solution.py:240
  16.5 13.3 %collective-permute-start.5 = (bf16[4,2,128,128]{3,2,1,0:T(8,128)(2,1)S(1)}, bf16[4,2,128,128]{3,2,1,0:T(8,128)(2,1)S(1)}, u32[]{:S(2)}, u32[]{:S(2)}) collective-permute-start(bf16[4,2,128,128]{3,2,1,0:T(8,128)(2,1)S(1)} %pad_maximum_fusion.2.refs_5_), channel_id=1, source_target_pairs={{0,12},{1,13},{2,14},{3,15},{4,0},{5,1},{6,2},{7,3},{8,4},{9,5},{1... | collective-permute-start | bytes 786440 | tf_op jit(solution)/shard_map/ppermute | solution.py:240
  17.5 2.2 %collective-permute-start.1 = (bf16[3,2,128,128]{3,2,1,0:T(8,128)(2,1)}, bf16[3,2,128,128]{3,2,1,0:T(8,128)(2,1)S(1)}, u32[]{:S(2)}, u32[]{:S(2)}) collective-permute-start(bf16[3,2,128,128]{3,2,1,0:T(8,128)(2,1)} %pad_maximum_fusion.5), channel_id=1, source_target_pairs={{0,1},{1,0},{2,3},{3,2},{4,5},{5,4},{6,7},{7,6},{8,9},{9,8},{10,11... | collective-permute-start | bytes 589832 | tf_op jit(solution)/shard_map/ppermute | solution.py:240
  19.8 10.5 %collective-permute-start.9 = (bf16[4,2,128,128]{3,2,1,0:T(8,128)(2,1)S(1)}, bf16[4,2,128,128]{3,2,1,0:T(8,128)(2,1)S(1)}, u32[]{:S(2)}, u32[]{:S(2)}) collective-permute-start(bf16[4,2,128,128]{3,2,1,0:T(8,128)(2,1)S(1)} %pad_maximum_fusion.2.refs_5_), channel_id=1, source_target_pairs={{0,4},{1,5},{2,6},{3,7},{4,8},{5,9},{6,10},{7,11},{8,12},{9,13},{1... | collective-permute-start | bytes 786440 | tf_op jit(solution)/shard_map/ppermute | solution.py:240
  21.1 13.8 %collective-permute-start.10 = (bf16[4,2,128,128]{3,2,1,0:T(8,128)(2,1)S(1)}, bf16[4,2,128,128]{3,2,1,0:T(8,128)(2,1)S(1)}, u32[]{:S(2)}, u32[]{:S(2)}) collective-permute-start(bf16[4,2,128,128]{3,2,1,0:T(8,128)(2,1)S(1)} %collective-permute-done.4.refs_6_), channel_id=1, source_target_pairs={{0,4},{1,5},{2,6},{3,7},{4,8},{5,9},{6,10},{7,11},{8,12},{9,13},{1... | collective-permute-start | bytes 786440 | tf_op jit(solution)/shard_map/ppermute | solution.py:240
  23.6 11.8 %collective-permute-start.6 = (bf16[4,2,128,128]{3,2,1,0:T(8,128)(2,1)S(1)}, bf16[4,2,128,128]{3,2,1,0:T(8,128)(2,1)S(1)}, u32[]{:S(2)}, u32[]{:S(2)}) collective-permute-start(bf16[4,2,128,128]{3,2,1,0:T(8,128)(2,1)S(1)} %collective-permute-done.4.refs_6_), channel_id=1, source_target_pairs={{0,12},{1,13},{2,14},{3,15},{4,0},{5,1},{6,2},{7,3},{8,4},{9,5},{1... | collective-permute-start | bytes 786440 | tf_op jit(solution)/shard_map/ppermute | solution.py:240
  29.8 7.3 %collective-permute-start.8 = (bf16[4,2,128,128]{3,2,1,0:T(8,128)(2,1)S(1)}, bf16[4,2,128,128]{3,2,1,0:T(8,128)(2,1)S(1)}, u32[]{:S(2)}, u32[]{:S(2)}) collective-permute-start(bf16[4,2,128,128]{3,2,1,0:T(8,128)(2,1)S(1)} %collective-permute-done.7.refs_9_), channel_id=1, source_target_pairs={{0,2},{1,3},{2,0},{3,1},{4,6},{5,7},{6,4},{7,5},{8,10},{9,11},{10,... | collective-permute-start | bytes 786440 | tf_op jit(solution)/shard_map/ppermute | solution.py:240
  37.1 13.9 %copy-start = (s32[2]{0:T(128)S(1)}, s32[2]{0:T(128)}, u32[]{:S(2)}) copy-start(s32[2]{0:T(128)} %refs_1_) | copy-start | bytes 28
  62.6 54.9 %collective-permute-start.26 = (bf16[2,2,2,2,128,128]{5,4,3,2,1,0:T(8,128)(2,1)S(1)}, bf16[2,2,2,2,128,128]{5,4,3,2,1,0:T(8,128)(2,1)S(1)}, u32[]{:S(2)}, u32[]{:S(2)}) collective-permute-start(bf16[2,2,2,2,128,128]{5,4,3,2,1,0:T(8,128)(2,1)S(1)} %get-tuple-element.91), channel_id=1, source_target_pairs={{0,16},{16,32},{32,48},{48,0},{64,80},{80,96},{96,112},{112,64},{1... | collective-permute-start | bytes 1572872 | tf_op jit(solution)/shard_map/ppermute | solution.py:245
  64.5 18.6 %collective-permute-start.18 = (bf16[2,2,2,128,128]{4,3,2,1,0:T(8,128)(2,1)S(1)}, bf16[2,2,2,128,128]{4,3,2,1,0:T(8,128)(2,1)S(1)}, u32[]{:S(2)}, u32[]{:S(2)}) collective-permute-start(bf16[2,2,2,128,128]{4,3,2,1,0:T(8,128)(2,1)S(1)} %get-tuple-element.94), channel_id=1, source_target_pairs={{0,16},{16,32},{32,48},{48,0},{64,80},{80,96},{96,112},{112,64},{1... | collective-permute-start | bytes 786440 | tf_op jit(solution)/shard_map/ppermute | solution.py:245
  66.2 23.5 %collective-permute-start.19 = (bf16[2,2,2,128,128]{4,3,2,1,0:T(8,128)(2,1)S(1)}, bf16[2,2,2,128,128]{4,3,2,1,0:T(8,128)(2,1)S(1)}, u32[]{:S(2)}, u32[]{:S(2)}) collective-permute-start(bf16[2,2,2,128,128]{4,3,2,1,0:T(8,128)(2,1)S(1)} %get-tuple-element.96), channel_id=1, source_target_pairs={{0,32},{16,48},{32,0},{48,16},{64,96},{80,112},{96,64},{112,80},{1... | collective-permute-start | bytes 786440 | tf_op jit(solution)/shard_map/ppermute | solution.py:245
  67.9 21.7 %collective-permute-start.20 = (bf16[2,2,2,128,128]{4,3,2,1,0:T(8,128)(2,1)S(1)}, bf16[2,2,2,128,128]{4,3,2,1,0:T(8,128)(2,1)S(1)}, u32[]{:S(2)}, u32[]{:S(2)}) collective-permute-start(bf16[2,2,2,128,128]{4,3,2,1,0:T(8,128)(2,1)S(1)} %get-tuple-element.95), channel_id=1, source_target_pairs={{0,48},{16,0},{32,16},{48,32},{64,112},{80,64},{96,80},{112,96},{1... | collective-permute-start | bytes 786440 | tf_op jit(solution)/shard_map/ppermute | solution.py:245
  69.9 3.6 %collective-permute-start.11 = (bf16[2,2,128,128]{3,2,1,0:T(8,128)(2,1)S(1)}, bf16[2,2,128,128]{3,2,1,0:T(8,128)(2,1)S(1)}, u32[]{:S(2)}, u32[]{:S(2)}) collective-permute-start(bf16[2,2,128,128]{3,2,1,0:T(8,128)(2,1)S(1)} %pad_maximum_fusion.8), channel_id=1, source_target_pairs={{0,1},{1,0},{2,3},{3,2},{4,5},{5,4},{6,7},{7,6},{8,9},{9,8},{10,11... | collective-permute-start | bytes 393224 | tf_op jit(solution)/shard_map/ppermute | solution.py:240
  73.6 46.7 %collective-permute-start.27 = (bf16[2,2,2,2,128,128]{5,4,3,2,1,0:T(8,128)(2,1)S(1)}, bf16[2,2,2,2,128,128]{5,4,3,2,1,0:T(8,128)(2,1)S(1)}, u32[]{:S(2)}, u32[]{:S(2)}) collective-permute-start(bf16[2,2,2,2,128,128]{5,4,3,2,1,0:T(8,128)(2,1)S(1)} %get-tuple-element.93), channel_id=1, source_target_pairs={{0,32},{16,48},{32,0},{48,16},{64,96},{80,112},{96,64},{112,80},{1... | collective-permute-start | bytes 1572872 | tf_op jit(solution)/shard_map/ppermute | solution.py:245
  83.1 22.2 %collective-permute-start.22 = (bf16[4,2,2,128,128]{4,3,2,1,0:T(8,128)(2,1)S(1)}, bf16[4,2,2,128,128]{4,3,2,1,0:T(8,128)(2,1)S(1)}, u32[]{:S(2)}, u32[]{:S(2)}) collective-permute-start(bf16[4,2,2,128,128]{4,3,2,1,0:T(8,128)(2,1)S(1)} %slice_bitcast_fusion), channel_id=1, source_target_pairs={{0,64},{16,80},{32,96},{48,112},{64,0},{80,16},{96,32},{112,48},{1... | collective-permute-start | bytes 1572872 | tf_op jit(solution)/shard_map/ppermute | solution.py:245
  89.6 16.8 %collective-permute-start.12 = (bf16[2,4,2,128,128]{4,3,2,1,0:T(8,128)(2,1)S(1)}, bf16[2,4,2,128,128]{4,3,2,1,0:T(8,128)(2,1)S(1)}, u32[]{:S(2)}, u32[]{:S(2)}) collective-permute-start(bf16[2,4,2,128,128]{4,3,2,1,0:T(8,128)(2,1)S(1)} %pad_maximum_fusion), channel_id=1, source_target_pairs={{0,4},{1,5},{2,6},{3,7},{4,8},{5,9},{6,10},{7,11},{8,12},{9,13},{1... | collective-permute-start | bytes 1572872 | tf_op jit(solution)/shard_map/ppermute | solution.py:240
  89.6 10.1 %collective-permute-start.15 = (bf16[4,2,128,128]{3,2,1,0:T(8,128)(2,1)S(1)}, bf16[4,2,128,128]{3,2,1,0:T(8,128)(2,1)S(1)}, u32[]{:S(2)}, u32[]{:S(2)}) collective-permute-start(bf16[4,2,128,128]{3,2,1,0:T(8,128)(2,1)S(1)} %get-tuple-element.73), channel_id=1, source_target_pairs={{0,2},{1,3},{2,0},{3,1},{4,6},{5,7},{6,4},{7,5},{8,10},{9,11},{10,... | collective-permute-start | bytes 786440 | tf_op jit(solution)/shard_map/ppermute | solution.py:240
  99.7 5.6 %collective-permute-start.21 = (bf16[2,2,128,128]{3,2,1,0:T(8,128)(2,1)S(1)}, bf16[2,2,128,128]{3,2,1,0:T(8,128)(2,1)S(1)}, u32[]{:S(2)}, u32[]{:S(2)}) collective-permute-start(bf16[2,2,128,128]{3,2,1,0:T(8,128)(2,1)S(1)} %slice_bitcast_fusion.14), channel_id=1, source_target_pairs={{0,64},{16,80},{32,96},{48,112},{64,0},{80,16},{96,32},{112,48},{1... | collective-permute-start | bytes 393224 | tf_op jit(solution)/shard_map/ppermute | solution.py:245
  105.3 12.2 %collective-permute-start.13 = (bf16[2,4,2,128,128]{4,3,2,1,0:T(8,128)(2,1)S(1)}, bf16[2,4,2,128,128]{4,3,2,1,0:T(8,128)(2,1)S(1)}, u32[]{:S(2)}, u32[]{:S(2)}) collective-permute-start(bf16[2,4,2,128,128]{4,3,2,1,0:T(8,128)(2,1)S(1)} %pad_maximum_fusion.1), channel_id=1, source_target_pairs={{0,12},{1,13},{2,14},{3,15},{4,0},{5,1},{6,2},{7,3},{8,4},{9,5},{1... | collective-permute-start | bytes 1572872 | tf_op jit(solution)/shard_map/ppermute | solution.py:240
  105.3 15.1 %collective-permute-start.28 = (bf16[2,2,2,2,128,128]{5,4,3,2,1,0:T(8,128)(2,1)S(1)}, bf16[2,2,2,2,128,128]{5,4,3,2,1,0:T(8,128)(2,1)S(1)}, u32[]{:S(2)}, u32[]{:S(2)}) collective-permute-start(bf16[2,2,2,2,128,128]{5,4,3,2,1,0:T(8,128)(2,1)S(1)} %get-tuple-element.92), channel_id=1, source_target_pairs={{0,48},{16,0},{32,16},{48,32},{64,112},{80,64},{96,80},{112,96},{1... | collective-permute-start | bytes 1572872 | tf_op jit(solution)/shard_map/ppermute | solution.py:245
  106.4 34.2 %collective-permute-start.16 = (bf16[4,2,128,128]{3,2,1,0:T(8,128)(2,1)S(1)}, bf16[4,2,128,128]{3,2,1,0:T(8,128)(2,1)S(1)}, u32[]{:S(2)}, u32[]{:S(2)}) collective-permute-start(bf16[4,2,128,128]{3,2,1,0:T(8,128)(2,1)S(1)} %add_convert_fusion.2), channel_id=1, source_target_pairs={{0,8},{1,9},{2,10},{3,11},{4,12},{5,13},{6,14},{7,15},{8,0},{9,1},... | collective-permute-start | bytes 786440 | tf_op jit(solution)/shard_map/ppermute | solution.py:240
  117.5 5.1 %collective-permute-start.23 = (bf16[2,2,128,128]{3,2,1,0:T(8,128)(2,1)S(1)}, bf16[2,2,128,128]{3,2,1,0:T(8,128)(2,1)S(1)}, u32[]{:S(2)}, u32[]{:S(2)}) collective-permute-start(bf16[2,2,128,128]{3,2,1,0:T(8,128)(2,1)S(1)} %get-tuple-element.101), channel_id=1, source_target_pairs={{0,16},{16,32},{32,48},{48,0},{64,80},{80,96},{96,112},{112,64},{1... | collective-permute-start | bytes 393224 | tf_op jit(solution)/shard_map/ppermute | solution.py:245
  117.6 22.5 %collective-permute-start.24 = (bf16[2,2,128,128]{3,2,1,0:T(8,128)(2,1)S(1)}, bf16[2,2,128,128]{3,2,1,0:T(8,128)(2,1)S(1)}, u32[]{:S(2)}, u32[]{:S(2)}) collective-permute-start(bf16[2,2,128,128]{3,2,1,0:T(8,128)(2,1)S(1)} %get-tuple-element.103), channel_id=1, source_target_pairs={{0,32},{16,48},{32,0},{48,16},{64,96},{80,112},{96,64},{112,80},{1... | collective-permute-start | bytes 393224 | tf_op jit(solution)/shard_map/ppermute | solution.py:245
  120.3 20.3 %collective-permute-start.25 = (bf16[2,2,128,128]{3,2,1,0:T(8,128)(2,1)S(1)}, bf16[2,2,128,128]{3,2,1,0:T(8,128)(2,1)S(1)}, u32[]{:S(2)}, u32[]{:S(2)}) collective-permute-start(bf16[2,2,128,128]{3,2,1,0:T(8,128)(2,1)S(1)} %get-tuple-element.102), channel_id=1, source_target_pairs={{0,48},{16,0},{32,16},{48,32},{64,112},{80,64},{96,80},{112,96},{1... | collective-permute-start | bytes 393224 | tf_op jit(solution)/shard_map/ppermute | solution.py:245
  120.4 20.2 %collective-permute-start.14 = (bf16[4,2,128,128]{3,2,1,0:T(8,128)(2,1)S(1)}, bf16[4,2,128,128]{3,2,1,0:T(8,128)(2,1)S(1)}, u32[]{:S(2)}, u32[]{:S(2)}) collective-permute-start(bf16[4,2,128,128]{3,2,1,0:T(8,128)(2,1)S(1)} %fusion.9), channel_id=1, source_target_pairs={{0,2},{1,3},{2,0},{3,1},{4,6},{5,7},{6,4},{7,5},{8,10},{9,11},{10,... | collective-permute-start | bytes 786440 | tf_op jit(solution)/shard_map/ppermute | solution.py:240
  122.6 23.4 %collective-permute-start.29 = (bf16[2,2,2,128,128]{4,3,2,1,0:T(8,128)(2,1)S(1)}, bf16[2,2,2,128,128]{4,3,2,1,0:T(8,128)(2,1)S(1)}, u32[]{:S(2)}, u32[]{:S(2)}) collective-permute-start(bf16[2,2,2,128,128]{4,3,2,1,0:T(8,128)(2,1)S(1)} %get-tuple-element.99), channel_id=1, source_target_pairs={{0,1},{1,0},{2,3},{3,2},{4,5},{5,4},{6,7},{7,6},{8,9},{9,8},{10,11... | collective-permute-start | bytes 786440 | tf_op jit(solution)/shard_map/ppermute | solution.py:240
  140.1 9.6 %collective-permute-start.30 = (bf16[2,2,2,128,128]{4,3,2,1,0:T(8,128)(2,1)S(1)}, bf16[2,2,2,128,128]{4,3,2,1,0:T(8,128)(2,1)S(1)}, u32[]{:S(2)}, u32[]{:S(2)}) collective-permute-start(bf16[2,2,2,128,128]{4,3,2,1,0:T(8,128)(2,1)S(1)} %get-tuple-element.100), channel_id=1, source_target_pairs={{0,65},{1,64},{2,67},{3,66},{4,69},{5,68},{6,71},{7,70},{8,73},{9,... | collective-permute-start | bytes 786440 | tf_op jit(solution)/shard_map/ppermute | solution.py:253
  140.9 10.3 %collective-permute-start.17 = (bf16[2,2,128,128]{3,2,1,0:T(8,128)(2,1)S(1)}, bf16[2,2,128,128]{3,2,1,0:T(8,128)(2,1)S(1)}, u32[]{:S(2)}, u32[]{:S(2)}) collective-permute-start(bf16[2,2,128,128]{3,2,1,0:T(8,128)(2,1)S(1)} %get-tuple-element.104), channel_id=1, source_target_pairs={{0,1},{1,0},{2,3},{3,2},{4,5},{5,4},{6,7},{7,6},{8,9},{9,8},{10,11... | collective-permute-start | bytes 393224 | tf_op jit(solution)/shard_map/ppermute | solution.py:240
  (3 other events, 11.6 us)

commit v3 on v2

--- a/solution.py
+++ b/solution.py
@@ -25,9 +25,14 @@
     def two(k,c):
         f(2*k,0); f(2*k+1,0)
         return c
-
-    lax.fori_loop(0,pairs//2,two,0)
-
+    def four(k,c):
+        for u in range(4):
+            f(4*k+u,0)
+        return c
+    lax.fori_loop(0,pairs//4,four,0)
+    @pl.when(pairs%4>=2)
+    def _():
+        two(pairs//4*2,0)
     @pl.when(pairs%2==1)
     def _(): f(pairs-1,0)
 
@@ -41,8 +46,8 @@
         rest=refs[17:]
     else:
         dq,gg,bg,acc=refs[14:18]
-        terms=refs[18:26]
-        rest=refs[26:]
+        terms=refs[18:24]
+        rest=refs[24:]
     s_ref,e_ref,m_ref,l_ref,o_ref,off_ref,qm,qt,dom,domt,kv,sem=rest
     for m in range(8):
         pltpu.make_async_copy(pieces[m],kv.at[pl.ds(4*m,4)],sem.at[m]).start()
@@ -52,6 +57,13 @@
         acc[...]=jnp.zeros(acc.shape,F32)
     for m in range(8):
         pltpu.make_async_copy(pieces[m],kv.at[pl.ds(4*m,4)],sem.at[m]).wait()
+
+    def spot(j,p,h):
+        if first:
+            return chk[0,p]*4+2*j+h
+        if h==0:
+            return chk[0,p]*3+2*j
+        return jnp.where(j==0,chk[0,p]*3+1,24+chk[1,p])
 
     def block(j,carry):
         n=cnt[j]
@@ -65,10 +77,8 @@
         m_ref[...]=jnp.full(m_ref.shape,-jnp.inf,F32)
         l_ref[...]=jnp.zeros(l_ref.shape,F32)
         o_ref[...]=jnp.zeros(o_ref.shape,F32)
-
         def both(p,w):
             return jnp.concatenate([kv[idx[j,2*p],w],kv[idx[j,2*p+1],w]],0)
-
         def score(p,c):
             k2=both(p,0)
             S=dot(qm[...],k2,NT)*(SCALE*LOG2E)
@@ -85,10 +95,8 @@
                     s_ref[p,r,BS:]=s1
                     m_ref[r,:]=jnp.maximum(m_ref[r,:],jnp.maximum(s0,s1))
             return c
-
         loop2(pairs,score)
         m_ref[...]=jnp.broadcast_to(jnp.max(m_ref[...],axis=1,keepdims=True),m_ref.shape)
-
         def attend(p,c):
             v2=both(p,1)
             for g in range(G):
@@ -100,7 +108,6 @@
                 e_ref[p,r,:]=e
             o_ref[...]+=dot(e_ref[p],v2,NN)
             return c
-
         loop2(pairs,attend)
         att=jnp.zeros((BS,BS),F32)
         inv=jnp.zeros((BS,BS),F32)
@@ -123,10 +130,9 @@
             off=jnp.sum(jnp.where(lane==g,x,0.0),axis=1,keepdims=True)
             off_ref[r,:]=jnp.broadcast_to(off,(BS,BS))
         o_ref[...]=jnp.zeros(o_ref.shape,F32)
-
         def backward(p,c):
             a0=idx[j,2*p]; a1=idx[j,2*p+1]
-            out=bg.at[chk[0,p],j] if first else bg.at[j,chk[j,p]]
+            spots=[spot(j,p,h) for h in range(2)]
             k2=both(p,0); v2=both(p,1)
             halves=[]; total=[None,None]
             WG=dot(dom[...],v2,NT)
@@ -138,7 +144,7 @@
                 if g<2: total[h]=ds
                 else:
                     b=(total[h]+ds).astype(BF)
-                    out[h,0]=b[:,:BS]; out[h,1]=b[:,BS:]
+                    bg[spots[h],0]=b[:,:BS]; bg[spots[h],1]=b[:,BS:]
                 half=ds.astype(BF)
                 halves.append(half)
             hs=jnp.concatenate(halves,0)
@@ -148,25 +154,21 @@
             acc[a0,0]+=dk[:,:BS]; acc[a1,0]+=dk[:,BS:]
             acc[a0,1]+=dv[:,:BS]; acc[a1,1]+=dv[:,BS:]
             return c
-
         loop2(pairs,backward)
-
         def clear(p,c):
-            out=bg.at[chk[0,p],j] if first else bg.at[j,chk[j,p]]
-            out[...]=jnp.zeros((2,2,BS,BS),BF)
+            for h in range(2):
+                bg[spot(j,p,h)]=jnp.zeros((2,BS,BS),BF)
             return c
-
         lax.fori_loop(pairs,8,clear,0)
         x=jnp.zeros((BS,BS),F32)
         for g in range(G):
             x=jnp.where(lane==g,o_ref[g*BS:(g+1)*BS,:],x)
         dq[j]=(x*SCALE).astype(BF)
         return carry
-
     lax.fori_loop(0,2,block,0)
     if not first:
-        for m in range(8):
-            terms[m][...]=acc[4*m:4*m+4].astype(BF)
+        for out,m in zip(terms,(0,1,2,4,5,6)):
+            out[...]=acc[4*m:4*m+out.shape[0]].astype(BF)
 
 
 def attend_blocks(idx,cnt,chk,qgc,bias,pieces,prev):
@@ -176,12 +178,11 @@
     AN=pl.BlockSpec(memory_space=pl.ANY)
     args=[idx,cnt,chk,qgc,bias,*pieces]
     specs=[SM]*3+[VM]*2+[AN]*8
-    lead=(8,2) if first else (2,8)
-    shapes=[((2,BS,BS),BF),((2,BS,BS),BF),(lead+(2,2,BS,BS),BF),((32,2,BS,BS),F32)]
+    shapes=[((2,BS,BS),BF),((2,BS,BS),BF),((32,2,BS,BS),BF),((32,2,BS,BS),F32)]
     if not first:
         args.append(prev)
         specs.append(VM)
-        shapes+=[((4,2,BS,BS),BF)]*8
+        shapes+=[((n,2,BS,BS),BF) for n in (4,4,8,4,4,8)]
 
     def kernel(*refs):
         attend_kernel(first,*refs)
@@ -292,7 +293,6 @@
     v_mine,v_send=split(value_vectors)
     shard=jnp.concatenate([jnp.stack([k_mine,v_mine],1),swap(jnp.stack([k_send,v_send],1))],0)
     shard,pair_bias=lax.optimization_barrier((shard,pair_bias))
-
     def gather(x,dy,dx):
         return to_col(x,(4-dy)%4,dx,0)
 
@@ -334,23 +334,24 @@
         return to_col(x,dy,dx,0)
 
     dq1,gg1,bg1,acc=attend_blocks(idx1,cnt1,by_z[None],other,bias_other,pieces,None)
-    q_back=swap(jnp.stack([dq1,gg1],0))
     bg1=row_sums(bg1.reshape(4,2,2,2,2,BS,BS)).astype(BF)
+    second=jnp.stack([by_z,by_x],0)
     dq0,gg0,bg0,_,*t=attend_blocks(
-        idx0,cnt0,jnp.stack([by_z,by_x],0),mine,bias_mine,pieces,acc
+        idx0,cnt0,second,mine,bias_mine,pieces,acc
     )
 
-    straight=bg0[0].reshape(4,2,2,2,BS,BS)
-    turned=bg0[1].reshape(2,4,2,2,BS,BS)
+    straight=bg0[:24].reshape(4,2,3,2,BS,BS)
+    turned=bg0[24:].reshape(2,4,2,BS,BS)
     turned_in=to_row(turned[1],1,0)
     straight=row_sums(straight).astype(BF)
     turned=plus(turned[0],turned_in).astype(BF)
-    up=step(jnp.stack([t[2],t[3]],0),1,0)
-    down=step(jnp.stack([t[6],t[7]],0),3,0)
-    near=step(t[5],0,1)
-    steps=[up[0],down[0]]
-    side=plus(t[1],up[1],down[1]).astype(BF)
-    over=plus(t[4],near).astype(BF)
+    t00,t01,t1,t20,t21,t3=t
+    up=step(t1,1,0)
+    down=step(t3,3,0)
+    near=step(t21,0,1)
+    steps=[up[:4],down[:4]]
+    side=plus(t01,up[4:],down[4:]).astype(BF)
+    over=plus(t20,near).astype(BF)
     steps+=[step(side,0,1),step(over,2,0)]
     bias_far=cross(bg1[1])
     bias_near=swap(bg1[0])
@@ -359,13 +360,14 @@
     straight=plus(straight[0],straight_in).astype(BF)
     turned=row_sums(turned).astype(BF)
 
+    q_back=swap(jnp.stack([dq1,gg1],0))
     query_grad,gate_grad=small_call(unite_kernel,dq0,gg0,q_back,sel)
-    own=plus(t[0],*steps)
+    own=plus(t00,*steps)
     own=jnp.stack([own[:,0]*SCALE,own[:,1]],1).astype(BF)
     own_far=swap(own[2:])
     key_grad,value_grad=small_call(join_kernel,own[:2],own_far,sel)
 
-    bias_own=jnp.stack([straight,turned],0)
+    bias_own=jnp.concatenate([straight,turned[None]],0).reshape(2,2,2,BS,BS)
     low=jnp.where(core==0,bias_own,bias_other)
     high=jnp.where(core==0,bias_other,bias_own)
     bias_grad=jnp.concatenate([low,high],1).transpose(0,1,3,2,4)

time: 153 us -> 139 us (0.908)
  starting transfers between devices: 50.1 us -> 42.2 us
  waiting for transfers between devices: 58.4 us -> 54.1 us
  Pallas kernels: 25.8 us -> 23.8 us
    ppermute x19, starting transfers between devices: 35.6 us -> 15.4 us  [to_col(): return lax.ppermute(x, 'col', pairs)]
    ppermute x11, starting transfers between devices: 14 us -> 24.3 us  [to_row(): return lax.ppermute(x, 'row', pairs)]
    ppermute x19, waiting for transfers between devices: 38 us -> 27.9 us  [to_col(): return lax.ppermute(x, 'col', pairs)]
    ppermute x11, waiting for transfers between devices: 16.7 us -> 26.3 us  [to_row(): return lax.ppermute(x, 'row', pairs)]
    ppermute x1, waiting for transfers between devices: 3.69 us -> 0.01 us  [cross(): return lax.ppermute(x, ('row', 'col'), pairs)]
    pallas_call x2, Pallas kernels: 25.2 us -> 23.1 us  [attend_blocks(): pl.pallas_call(kernel, out_shape=tuple((jax.ShapeDtypeStruct(*s) for s in...]
    ppermute x1, starting transfers between devices: 0.5 us -> 2.44 us  [cross(): return lax.ppermute(x, ('row', 'col'), pairs)]
  transfers between devices with their start and end apart: 31 -> 31, of which waited for: 14 -> 13; matrix products, arithmetic and copies ran while one was open for 9% -> 10% of each run, Pallas kernels for 0% -> 0%
where the time goes in v3:
time: 139 us
  waiting for transfers between devices  54.1 us (39%)
  starting transfers between devices  42.2 us (30%)
  Pallas kernels  23.8 us (17%)
  local copies, waits for them, and re-layouts  11 us (8%)
  matrix products  3.64 us (3%)
  other arithmetic  3.03 us (2%)
    ppermute x19, waiting for transfers between devices, to_col(): return lax.ppermute(x, 'col', pairs)  27.9 us
    ppermute x11, waiting for transfers between devices, to_row(): return lax.ppermute(x, 'row', pairs)  26.3 us
    ppermute x11, starting transfers between devices, to_row(): return lax.ppermute(x, 'row', pairs)  24.3 us
    pallas_call x2, Pallas kernels, attend_blocks(): pl.pallas_call(kernel, out_shape=tuple((jax.ShapeDtypeStruct(*s) for s in...  23.1 us
    ppermute x19, starting transfers between devices, to_col(): return lax.ppermute(x, 'col', pairs)  15.4 us
    unnamed x13, local copies, waits for them, and re-layouts  4.52 us
    dot_general x5, matrix products, split(): lax.dot_general(x.reshape(2 * BS, 2 * BS), sel, NN, preferred_element_typ...  3.64 us
    optimization_barrier x1, local copies, waits for them, and re-layouts, body(): shard, pair_bias = lax.optimization_barrier((shard, pair_bias))  3.36 us
  transfers between devices with their start and end apart: 31, of which 13 were waited for; matrix products, arithmetic and copies ran while one was open for 10% of the time, Pallas kernels for 0%

profile of v3, /device:TPU:9, one launch (start us, length us, event | category | flops | bytes accessed | tf_op | source)
XLA Modules:
  0.0 138.8 jit_solution(1458635404892671079)
XLA Ops:
  1.9 1.1 fusion.4
  6.4 3.4 %copy.39 = bf16[2,4,128,16,128]{4,2,3,1,0:T(8,128)(2,1)S(1)} copy(bf16[2,4,128,16,128]{4,3,2,1,0:T(8,128)(2,1)} %param.13) | data formatting | bytes 8388608 | tf_op jit(solution)/shard_map/optimization_barrier | solution.py:295
  9.8 1.6 %dynamic-slice_bitcast_fusion = (bf16[2,2,16,128,128]{4,3,2,1,0:T(8,128)(2,1)}, bf16[2,2,16,128,128]{4,3,2,1,0:T(8,128)(2,1)S(1)}) fusion(bf16[2,4,128,16,128]{4,2,3,1,0:T(8,128)(2,1)S(1)} %copy.39, s32[]{:T(128)S(6)} %select_n.186, s32[]{:T(128)S(6)} %select_n.185), kind=kLoop, calls=%fused_computation | loop fusion | bytes 8388616 | tf_op jit(solution)/shard_map/dynamic_slice | solution.py:318
  13.2 1.3 collective-permute-start.4
  14.5 2.0 %collective-permute-start.7 = (bf16[4,2,128,128]{3,2,1,0:T(8,128)(2,1)S(1)}, bf16[4,2,128,128]{3,2,1,0:T(8,128)(2,1)S(1)}, u32[]{:S(2)}, u32[]{:S(2)}) collective-permute-start(bf16[4,2,128,128]{3,2,1,0:T(8,128)(2,1)S(1)} %pad_maximum_fusion.refs_5_), channel_id=1, source_target_pairs={{0,8},{1,9},{2,10},{3,11},{4,12},{5,13},{6,14},{7,15},{8,0},{9,1},... | collective-permute-start | bytes 786440 | tf_op jit(solution)/shard_map/ppermute | solution.py:241
  18.5 1.2 collective-permute-done.1.refs_3_
  21.1 1.3 collective-permute-start.10
  22.4 1.2 collective-permute-done.7.refs_9_
  23.7 6.1 %collective-permute-done.5.refs_7_ = bf16[4,2,128,128]{3,2,1,0:T(8,128)(2,1)S(1)} collective-permute-done((bf16[4,2,128,128]{3,2,1,0:T(8,128)(2,1)S(1)}, bf16[4,2,128,128]{3,2,1,0:T(8,128)(2,1)S(1)}, u32[]{:S(2)}, u32[]{:S(2)}) %collective-permute-start.5) | collective-permute-done | bytes 262176 | tf_op jit(solution)/shard_map/ppermute | solution.py:241
  30.3 4.6 %collective-permute-done.10.refs_12_ = bf16[4,2,128,128]{3,2,1,0:T(8,128)(2,1)S(1)} collective-permute-done((bf16[4,2,128,128]{3,2,1,0:T(8,128)(2,1)S(1)}, bf16[4,2,128,128]{3,2,1,0:T(8,128)(2,1)S(1)}, u32[]{:S(2)}, u32[]{:S(2)}) %collective-permute-start.10) | collective-permute-done | bytes 262176 | tf_op jit(solution)/shard_map/ppermute | solution.py:241
  35.4 1.7 %collective-permute-done.8.refs_10_ = bf16[4,2,128,128]{3,2,1,0:T(8,128)(2,1)S(1)} collective-permute-done((bf16[4,2,128,128]{3,2,1,0:T(8,128)(2,1)S(1)}, bf16[4,2,128,128]{3,2,1,0:T(8,128)(2,1)S(1)}, u32[]{:S(2)}, u32[]{:S(2)}) %collective-permute-start.8) | collective-permute-done | bytes 262176 | tf_op jit(solution)/shard_map/ppermute | solution.py:241
  37.1 12.8 %attend_blocks.2 = (bf16[2,128,128]{2,1,0:T(8,128)(2,1)S(1)}, bf16[2,128,128]{2,1,0:T(8,128)(2,1)S(1)}, bf16[32,2,128,128]{3,2,1,0:T(8,128)(2,1)S(1)}, f32[32,2,128,128]{3,2,1,0:T(8,128)S(1)}) custom-call(s32[2,16]{1,0:T(2,128)S(1)} %fusion.47.refs_0_, s32[2]{0:T(128)S(1)} %slice_reduce_fusion.refs_1_, s32[1,8]{1,0:T(1,128)S(1)} %get-tuple-element.120.refs_2_, ...), custom_call_target="tpu_custom_call" | custom-call | flops 10000000000 | bytes 25165824 | tf_op jit(solution)/shard_map/attend_blocks/pallas_call | solution.py:190
  49.9 10.3 %attend_blocks.3 = (bf16[2,128,128]{2,1,0:T(8,128)(2,1)S(1)}, bf16[2,128,128]{2,1,0:T(8,128)(2,1)S(1)}, bf16[32,2,128,128]{3,2,1,0:T(8,128)(2,1)S(1)}, f32[32,2,...) custom-call(s32[2,16]{1,0:T(2,128)S(1)} %fusion.42.refs_0_, ...), custom_call_target="tpu_custom_call", output_to_operand_aliasing={{3}: (13, {})} | custom-call | flops 10000000000 | bytes 25165824 | tf_op jit(solution)/shard_map/attend_blocks/pallas_call | solution.py:190
  60.3 2.5 %collective-permute-start.22 = (bf16[4,2,128,128]{3,2,1,0:T(8,128)(2,1)S(1)}, bf16[4,2,128,128]{3,2,1,0:T(8,128)(2,1)S(1)}, u32[]{:S(2)}, u32[]{:S(2)}) collective-permute-start(bf16[4,2,128,128]{3,2,1,0:T(8,128)(2,1)S(1)} %slice.160), channel_id=1, source_target_pairs={{0,64},{16,80},{32,96},{48,112},{64,0},{80,16},{96,32},{112,48},{1... | collective-permute-start | bytes 786440 | tf_op jit(solution)/shard_map/ppermute | solution.py:246
  62.9 1.7 %collective-permute-start.18 = (bf16[2,3,2,128,128]{4,3,2,1,0:T(8,128)(2,1)S(1)}, bf16[2,3,2,128,128]{4,3,2,1,0:T(8,128)(2,1)S(1)}, u32[]{:S(2)}, u32[]{:S(2)}) collective-permute-start(bf16[2,3,2,128,128]{4,3,2,1,0:T(8,128)(2,1)S(1)} %bitcast.108), channel_id=1, source_target_pairs={{0,16},{16,32},{32,48},{48,0},{64,80},{80,96},{96,112},{112,64},{1... | collective-permute-start | bytes 1179656 | tf_op jit(solution)/shard_map/ppermute | solution.py:246
  64.7 2.1 %collective-permute-start.11 = (bf16[2,2,128,128]{3,2,1,0:T(8,128)(2,1)S(1)}, bf16[2,2,128,128]{3,2,1,0:T(8,128)(2,1)S(1)}, u32[]{:S(2)}, u32[]{:S(2)}) collective-permute-start(bf16[2,2,128,128]{3,2,1,0:T(8,128)(2,1)S(1)} %pad_maximum_fusion.6), channel_id=1, source_target_pairs={{0,1},{1,0},{2,3},{3,2},{4,5},{5,4},{6,7},{7,6},{8,9},{9,8},{10,11... | collective-permute-start | bytes 393224 | tf_op jit(solution)/shard_map/ppermute | solution.py:241
  66.8 1.5 %collective-permute-done.22 = bf16[4,2,128,128]{3,2,1,0:T(8,128)(2,1)S(1)} collective-permute-done((bf16[4,2,128,128]{3,2,1,0:T(8,128)(2,1)S(1)}, bf16[4,2,128,128]{3,2,1,0:T(8,128)(2,1)S(1)}, u32[]{:S(2)}, u32[]{:S(2)}) %collective-permute-start.22) | collective-permute-done | bytes 262176 | tf_op jit(solution)/shard_map/ppermute | solution.py:246
  68.4 1.7 %collective-permute-start.23 = (bf16[2,128,128]{2,1,0:T(8,128)(2,1)S(1)}, bf16[2,128,128]{2,1,0:T(8,128)(2,1)S(1)}, u32[]{:S(2)}, u32[]{:S(2)}) collective-permute-start(bf16[2,128,128]{2,1,0:T(8,128)(2,1)S(1)} %get-tuple-element.104), channel_id=1, source_target_pairs={{0,16},{16,32},{32,48},{48,0},{64,80},{80,96},{96,112},{112,64},{1... | collective-permute-start | bytes 196616 | tf_op jit(solution)/shard_map/ppermute | solution.py:246
  70.3 3.4 %collective-permute-start.19 = (bf16[2,3,2,128,128]{4,3,2,1,0:T(8,128)(2,1)S(1)}, bf16[2,3,2,128,128]{4,3,2,1,0:T(8,128)(2,1)S(1)}, u32[]{:S(2)}, u32[]{:S(2)}) collective-permute-start(bf16[2,3,2,128,128]{4,3,2,1,0:T(8,128)(2,1)S(1)} %bitcast.107), channel_id=1, source_target_pairs={{0,32},{16,48},{32,0},{48,16},{64,96},{80,112},{96,64},{112,80},{1... | collective-permute-start | bytes 1179656 | tf_op jit(solution)/shard_map/ppermute | solution.py:246
  76.8 2.7 %collective-permute-start.25 = (bf16[2,128,128]{2,1,0:T(8,128)(2,1)S(1)}, bf16[2,128,128]{2,1,0:T(8,128)(2,1)S(1)}, u32[]{:S(2)}, u32[]{:S(2)}) collective-permute-start(bf16[2,128,128]{2,1,0:T(8,128)(2,1)S(1)} %get-tuple-element.105), channel_id=1, source_target_pairs={{0,48},{16,0},{32,16},{48,32},{64,112},{80,64},{96,80},{112,96},{1... | collective-permute-start | bytes 196616 | tf_op jit(solution)/shard_map/ppermute | solution.py:246
  79.5 7.1 %collective-permute-done.24 = bf16[2,128,128]{2,1,0:T(8,128)(2,1)S(1)} collective-permute-done((bf16[2,128,128]{2,1,0:T(8,128)(2,1)S(1)}, bf16[2,128,128]{2,1,0:T(8,128)(2,1)S(1)}, u32[]{:S(2)}, u32[]{:S(2)}) %collective-permute-start.24) | collective-permute-done | bytes 65568 | tf_op jit(solution)/shard_map/ppermute | solution.py:246
  86.7 3.0 %collective-permute-start.26 = (bf16[2,2,2,2,128,128]{5,4,3,2,1,0:T(8,128)(2,1)S(1)}, bf16[2,2,2,2,128,128]{5,4,3,2,1,0:T(8,128)(2,1)S(1)}, u32[]{:S(2)}, u32[]{:S(2)}) collective-permute-start(bf16[2,2,2,2,128,128]{5,4,3,2,1,0:T(8,128)(2,1)S(1)} %bitcast.105), channel_id=1, source_target_pairs={{0,16},{16,32},{32,48},{48,0},{64,80},{80,96},{96,112},{112,64},{1... | collective-permute-start | bytes 1572872 | tf_op jit(solution)/shard_map/ppermute | solution.py:246
  90.8 2.9 %collective-permute-start.27 = (bf16[2,2,2,2,128,128]{5,4,3,2,1,0:T(8,128)(2,1)S(1)}, bf16[2,2,2,2,128,128]{5,4,3,2,1,0:T(8,128)(2,1)S(1)}, u32[]{:S(2)}, u32[]{:S(2)}) collective-permute-start(bf16[2,2,2,2,128,128]{5,4,3,2,1,0:T(8,128)(2,1)S(1)} %bitcast.104), channel_id=1, source_target_pairs={{0,32},{16,48},{32,0},{48,16},{64,96},{80,112},{96,64},{112,80},{1... | collective-permute-start | bytes 1572872 | tf_op jit(solution)/shard_map/ppermute | solution.py:246
  93.6 2.8 %collective-permute-start.28 = (bf16[2,2,2,2,128,128]{5,4,3,2,1,0:T(8,128)(2,1)S(1)}, bf16[2,2,2,2,128,128]{5,4,3,2,1,0:T(8,128)(2,1)S(1)}, u32[]{:S(2)}, u32[]{:S(2)}) collective-permute-start(bf16[2,2,2,2,128,128]{5,4,3,2,1,0:T(8,128)(2,1)S(1)} %bitcast.103), channel_id=1, source_target_pairs={{0,48},{16,0},{32,16},{48,32},{64,112},{80,64},{96,80},{112,96},{1... | collective-permute-start | bytes 1572872 | tf_op jit(solution)/shard_map/ppermute | solution.py:246
  96.6 1.4 %collective-permute-start.13 = (bf16[8,2,128,128]{3,2,1,0:T(8,128)(2,1)S(1)}, bf16[8,2,128,128]{3,2,1,0:T(8,128)(2,1)S(1)}, u32[]{:S(2)}, u32[]{:S(2)}) collective-permute-start(bf16[8,2,128,128]{3,2,1,0:T(8,128)(2,1)S(1)} %get-tuple-element.66), channel_id=1, source_target_pairs={{0,12},{1,13},{2,14},{3,15},{4,0},{5,1},{6,2},{7,3},{8,4},{9,5},{1... | collective-permute-start | bytes 1572872 | tf_op jit(solution)/shard_map/ppermute | solution.py:241
  98.4 9.8 %collective-permute-done.27 = bf16[2,2,2,2,128,128]{5,4,3,2,1,0:T(8,128)(2,1)S(1)} collective-permute-done((bf16[2,2,2,2,128,128]{5,4,3,2,1,0:T(8,128)(2,1)S(1)}, bf16[2,2,2,2,128,128]{5,4,3,2,1,0:T(8,128)(2,1)S(1)}, u32[]{:S(2)}, u32[]{:S(2)}) %collective-permute-start.27) | collective-permute-done | bytes 524320 | tf_op jit(solution)/shard_map/ppermute | solution.py:246
  108.2 2.5 %collective-permute-start.21 = (bf16[3,2,128,128]{3,2,1,0:T(8,128)(2,1)S(1)}, bf16[3,2,128,128]{3,2,1,0:T(8,128)(2,1)S(1)}, u32[]{:S(2)}, u32[]{:S(2)}) collective-permute-start(bf16[3,2,128,128]{3,2,1,0:T(8,128)(2,1)S(1)} %slice_bitcast_fusion.2), channel_id=1, source_target_pairs={{0,64},{16,80},{32,96},{48,112},{64,0},{80,16},{96,32},{112,48},{1... | collective-permute-start | bytes 589832 | tf_op jit(solution)/shard_map/ppermute | solution.py:246
  110.6 6.7 %collective-permute-done.28 = bf16[2,2,2,2,128,128]{5,4,3,2,1,0:T(8,128)(2,1)S(1)} collective-permute-done((bf16[2,2,2,2,128,128]{5,4,3,2,1,0:T(8,128)(2,1)S(1)}, bf16[2,2,2,2,128,128]{5,4,3,2,1,0:T(8,128)(2,1)S(1)}, u32[]{:S(2)}, u32[]{:S(2)}) %collective-permute-start.28) | collective-permute-done | bytes 524320 | tf_op jit(solution)/shard_map/ppermute | solution.py:246
  117.7 1.6 %collective-permute-start.29 = (bf16[2,2,2,128,128]{4,3,2,1,0:T(8,128)(2,1)S(1)}, bf16[2,2,2,128,128]{4,3,2,1,0:T(8,128)(2,1)S(1)}, u32[]{:S(2)}, u32[]{:S(2)}) collective-permute-start(bf16[2,2,2,128,128]{4,3,2,1,0:T(8,128)(2,1)S(1)} %get-tuple-element.102), channel_id=1, source_target_pairs={{0,1},{1,0},{2,3},{3,2},{4,5},{5,4},{6,7},{7,6},{8,9},{9,8},{10,11... | collective-permute-start | bytes 786440 | tf_op jit(solution)/shard_map/ppermute | solution.py:241
  119.4 2.4 %collective-permute-start.30 = (bf16[2,2,2,128,128]{4,3,2,1,0:T(8,128)(2,1)S(1)}, bf16[2,2,2,128,128]{4,3,2,1,0:T(8,128)(2,1)S(1)}, u32[]{:S(2)}, u32[]{:S(2)}) collective-permute-start(bf16[2,2,2,128,128]{4,3,2,1,0:T(8,128)(2,1)S(1)} %get-tuple-element.103), channel_id=1, source_target_pairs={{0,65},{1,64},{2,67},{3,66},{4,69},{5,68},{6,71},{7,70},{8,73},{9,... | collective-permute-start | bytes 786440 | tf_op jit(solution)/shard_map/ppermute | solution.py:254
  122.4 11.6 %collective-permute-done.14 = bf16[4,2,128,128]{3,2,1,0:T(8,128)(2,1)S(1)} collective-permute-done((bf16[4,2,128,128]{3,2,1,0:T(8,128)(2,1)S(1)}, bf16[4,2,128,128]{3,2,1,0:T(8,128)(2,1)S(1)}, u32[]{:S(2)}, u32[]{:S(2)}) %collective-permute-start.14) | collective-permute-done | bytes 262176 | tf_op jit(solution)/shard_map/ppermute | solution.py:241
  135.6 1.3 copy.45
  (97 shorter events, 20.2 us)
Async XLA Ops:
  3.0 3.4 %collective-permute-start.2 = (bf16[2,2,128,128]{3,2,1,0:T(8,128)(2,1)S(1)}, bf16[2,2,128,128]{3,2,1,0:T(8,128)(2,1)S(1)}, u32[]{:S(2)}, u32[]{:S(2)}) collective-permute-start(bf16[2,2,128,128]{3,2,1,0:T(8,128)(2,1)S(1)} %pad_maximum_fusion.5), channel_id=1, source_target_pairs={{0,1},{1,0},{2,3},{3,2},{4,5},{5,4},{6,7},{7,6},{8,9},{9,8},{10,11... | collective-permute-start | bytes 393224 | tf_op jit(solution)/shard_map/ppermute | solution.py:241
  5.3 12.3 %collective-permute-start = (s32[2,17]{1,0:T(2,128)S(1)}, s32[2,17]{1,0:T(2,128)S(1)}, u32[]{:S(2)}, u32[]{:S(2)}) collective-permute-start(s32[2,17]{1,0:T(2,128)S(1)} %pad_add_fusion), channel_id=1, source_target_pairs={{0,1},{1,0},{2,3},{3,2},{4,5},{5,4},{6,7},{7,6},{8,9},{9,8},{10,11... | collective-permute-start | bytes 416 | tf_op jit(solution)/shard_map/ppermute | solution.py:241
  11.5 25.6 %collective-permute-start.3 = (bf16[2,2,16,128,128]{4,3,2,1,0:T(8,128)(2,1)}, bf16[2,2,16,128,128]{4,3,2,1,0:T(8,128)(2,1)}, u32[]{:S(2)}, u32[]{:S(2)}) collective-permute-start(bf16[2,2,16,128,128]{4,3,2,1,0:T(8,128)(2,1)} %get-tuple-element.90), channel_id=1, source_target_pairs={{0,1},{1,0},{2,3},{3,2},{4,5},{5,4},{6,7},{7,6},{8,9},{9,8},{10,11... | collective-permute-start | bytes 6291464 | tf_op jit(solution)/shard_map/ppermute | solution.py:241
  13.2 7.9 %collective-permute-start.4 = (bf16[4,2,128,128]{3,2,1,0:T(8,128)(2,1)S(1)}, bf16[4,2,128,128]{3,2,1,0:T(8,128)(2,1)S(1)}, u32[]{:S(2)}, u32[]{:S(2)}) collective-permute-start(bf16[4,2,128,128]{3,2,1,0:T(8,128)(2,1)S(1)} %pad_maximum_fusion.refs_5_), channel_id=1, source_target_pairs={{0,2},{1,3},{2,0},{3,1},{4,6},{5,7},{6,4},{7,5},{8,10},{9,11},{10,... | collective-permute-start | bytes 786440 | tf_op jit(solution)/shard_map/ppermute | solution.py:241
  14.5 9.1 %collective-permute-start.7 = (bf16[4,2,128,128]{3,2,1,0:T(8,128)(2,1)S(1)}, bf16[4,2,128,128]{3,2,1,0:T(8,128)(2,1)S(1)}, u32[]{:S(2)}, u32[]{:S(2)}) collective-permute-start(bf16[4,2,128,128]{3,2,1,0:T(8,128)(2,1)S(1)} %pad_maximum_fusion.refs_5_), channel_id=1, source_target_pairs={{0,8},{1,9},{2,10},{3,11},{4,12},{5,13},{6,14},{7,15},{8,0},{9,1},... | collective-permute-start | bytes 786440 | tf_op jit(solution)/shard_map/ppermute | solution.py:241
  16.5 13.3 %collective-permute-start.5 = (bf16[4,2,128,128]{3,2,1,0:T(8,128)(2,1)S(1)}, bf16[4,2,128,128]{3,2,1,0:T(8,128)(2,1)S(1)}, u32[]{:S(2)}, u32[]{:S(2)}) collective-permute-start(bf16[4,2,128,128]{3,2,1,0:T(8,128)(2,1)S(1)} %pad_maximum_fusion.refs_5_), channel_id=1, source_target_pairs={{0,12},{1,13},{2,14},{3,15},{4,0},{5,1},{6,2},{7,3},{8,4},{9,5},{1... | collective-permute-start | bytes 786440 | tf_op jit(solution)/shard_map/ppermute | solution.py:241
  17.5 2.2 %collective-permute-start.1 = (bf16[3,2,128,128]{3,2,1,0:T(8,128)(2,1)}, bf16[3,2,128,128]{3,2,1,0:T(8,128)(2,1)S(1)}, u32[]{:S(2)}, u32[]{:S(2)}) collective-permute-start(bf16[3,2,128,128]{3,2,1,0:T(8,128)(2,1)} %pad_maximum_fusion.3), channel_id=1, source_target_pairs={{0,1},{1,0},{2,3},{3,2},{4,5},{5,4},{6,7},{7,6},{8,9},{9,8},{10,11... | collective-permute-start | bytes 589832 | tf_op jit(solution)/shard_map/ppermute | solution.py:241
  19.8 10.5 %collective-permute-start.9 = (bf16[4,2,128,128]{3,2,1,0:T(8,128)(2,1)S(1)}, bf16[4,2,128,128]{3,2,1,0:T(8,128)(2,1)S(1)}, u32[]{:S(2)}, u32[]{:S(2)}) collective-permute-start(bf16[4,2,128,128]{3,2,1,0:T(8,128)(2,1)S(1)} %pad_maximum_fusion.refs_5_), channel_id=1, source_target_pairs={{0,4},{1,5},{2,6},{3,7},{4,8},{5,9},{6,10},{7,11},{8,12},{9,13},{1... | collective-permute-start | bytes 786440 | tf_op jit(solution)/shard_map/ppermute | solution.py:241
  21.1 13.8 %collective-permute-start.10 = (bf16[4,2,128,128]{3,2,1,0:T(8,128)(2,1)S(1)}, bf16[4,2,128,128]{3,2,1,0:T(8,128)(2,1)S(1)}, u32[]{:S(2)}, u32[]{:S(2)}) collective-permute-start(bf16[4,2,128,128]{3,2,1,0:T(8,128)(2,1)S(1)} %collective-permute-done.4.refs_6_), channel_id=1, source_target_pairs={{0,4},{1,5},{2,6},{3,7},{4,8},{5,9},{6,10},{7,11},{8,12},{9,13},{1... | collective-permute-start | bytes 786440 | tf_op jit(solution)/shard_map/ppermute | solution.py:241
  23.6 11.8 %collective-permute-start.6 = (bf16[4,2,128,128]{3,2,1,0:T(8,128)(2,1)S(1)}, bf16[4,2,128,128]{3,2,1,0:T(8,128)(2,1)S(1)}, u32[]{:S(2)}, u32[]{:S(2)}) collective-permute-start(bf16[4,2,128,128]{3,2,1,0:T(8,128)(2,1)S(1)} %collective-permute-done.4.refs_6_), channel_id=1, source_target_pairs={{0,12},{1,13},{2,14},{3,15},{4,0},{5,1},{6,2},{7,3},{8,4},{9,5},{1... | collective-permute-start | bytes 786440 | tf_op jit(solution)/shard_map/ppermute | solution.py:241
  29.8 7.3 %collective-permute-start.8 = (bf16[4,2,128,128]{3,2,1,0:T(8,128)(2,1)S(1)}, bf16[4,2,128,128]{3,2,1,0:T(8,128)(2,1)S(1)}, u32[]{:S(2)}, u32[]{:S(2)}) collective-permute-start(bf16[4,2,128,128]{3,2,1,0:T(8,128)(2,1)S(1)} %collective-permute-done.7.refs_9_), channel_id=1, source_target_pairs={{0,2},{1,3},{2,0},{3,1},{4,6},{5,7},{6,4},{7,5},{8,10},{9,11},{10,... | collective-permute-start | bytes 786440 | tf_op jit(solution)/shard_map/ppermute | solution.py:241
  37.1 12.8 %copy-start = (s32[2]{0:T(128)S(1)}, s32[2]{0:T(128)}, u32[]{:S(2)}) copy-start(s32[2]{0:T(128)} %refs_1_) | copy-start | bytes 28
  60.3 8.0 %collective-permute-start.22 = (bf16[4,2,128,128]{3,2,1,0:T(8,128)(2,1)S(1)}, bf16[4,2,128,128]{3,2,1,0:T(8,128)(2,1)S(1)}, u32[]{:S(2)}, u32[]{:S(2)}) collective-permute-start(bf16[4,2,128,128]{3,2,1,0:T(8,128)(2,1)S(1)} %slice.160), channel_id=1, source_target_pairs={{0,64},{16,80},{32,96},{48,112},{64,0},{80,16},{96,32},{112,48},{1... | collective-permute-start | bytes 786440 | tf_op jit(solution)/shard_map/ppermute | solution.py:246
  62.9 30.7 %collective-permute-start.18 = (bf16[2,3,2,128,128]{4,3,2,1,0:T(8,128)(2,1)S(1)}, bf16[2,3,2,128,128]{4,3,2,1,0:T(8,128)(2,1)S(1)}, u32[]{:S(2)}, u32[]{:S(2)}) collective-permute-start(bf16[2,3,2,128,128]{4,3,2,1,0:T(8,128)(2,1)S(1)} %bitcast.108), channel_id=1, source_target_pairs={{0,16},{16,32},{32,48},{48,0},{64,80},{80,96},{96,112},{112,64},{1... | collective-permute-start | bytes 1179656 | tf_op jit(solution)/shard_map/ppermute | solution.py:246
  64.7 11.7 %collective-permute-start.15 = (bf16[4,2,128,128]{3,2,1,0:T(8,128)(2,1)S(1)}, bf16[4,2,128,128]{3,2,1,0:T(8,128)(2,1)S(1)}, u32[]{:S(2)}, u32[]{:S(2)}) collective-permute-start(bf16[4,2,128,128]{3,2,1,0:T(8,128)(2,1)S(1)} %get-tuple-element.69), channel_id=1, source_target_pairs={{0,2},{1,3},{2,0},{3,1},{4,6},{5,7},{6,4},{7,5},{8,10},{9,11},{10,... | collective-permute-start | bytes 786440 | tf_op jit(solution)/shard_map/ppermute | solution.py:241
  64.7 9.0 %collective-permute-start.11 = (bf16[2,2,128,128]{3,2,1,0:T(8,128)(2,1)S(1)}, bf16[2,2,128,128]{3,2,1,0:T(8,128)(2,1)S(1)}, u32[]{:S(2)}, u32[]{:S(2)}) collective-permute-start(bf16[2,2,128,128]{3,2,1,0:T(8,128)(2,1)S(1)} %pad_maximum_fusion.6), channel_id=1, source_target_pairs={{0,1},{1,0},{2,3},{3,2},{4,5},{5,4},{6,7},{7,6},{8,9},{9,8},{10,11... | collective-permute-start | bytes 393224 | tf_op jit(solution)/shard_map/ppermute | solution.py:241
  68.4 8.4 %collective-permute-start.23 = (bf16[2,128,128]{2,1,0:T(8,128)(2,1)S(1)}, bf16[2,128,128]{2,1,0:T(8,128)(2,1)S(1)}, u32[]{:S(2)}, u32[]{:S(2)}) collective-permute-start(bf16[2,128,128]{2,1,0:T(8,128)(2,1)S(1)} %get-tuple-element.104), channel_id=1, source_target_pairs={{0,16},{16,32},{32,48},{48,0},{64,80},{80,96},{96,112},{112,64},{1... | collective-permute-start | bytes 196616 | tf_op jit(solution)/shard_map/ppermute | solution.py:246
  70.3 26.1 %collective-permute-start.19 = (bf16[2,3,2,128,128]{4,3,2,1,0:T(8,128)(2,1)S(1)}, bf16[2,3,2,128,128]{4,3,2,1,0:T(8,128)(2,1)S(1)}, u32[]{:S(2)}, u32[]{:S(2)}) collective-permute-start(bf16[2,3,2,128,128]{4,3,2,1,0:T(8,128)(2,1)S(1)} %bitcast.107), channel_id=1, source_target_pairs={{0,32},{16,48},{32,0},{48,16},{64,96},{80,112},{96,64},{112,80},{1... | collective-permute-start | bytes 1179656 | tf_op jit(solution)/shard_map/ppermute | solution.py:246
  73.7 22.9 %collective-permute-start.20 = (bf16[2,3,2,128,128]{4,3,2,1,0:T(8,128)(2,1)S(1)}, bf16[2,3,2,128,128]{4,3,2,1,0:T(8,128)(2,1)S(1)}, u32[]{:S(2)}, u32[]{:S(2)}) collective-permute-start(bf16[2,3,2,128,128]{4,3,2,1,0:T(8,128)(2,1)S(1)} %bitcast.106), channel_id=1, source_target_pairs={{0,48},{16,0},{32,16},{48,32},{64,112},{80,64},{96,80},{112,96},{1... | collective-permute-start | bytes 1179656 | tf_op jit(solution)/shard_map/ppermute | solution.py:246
  76.4 10.3 %collective-permute-start.24 = (bf16[2,128,128]{2,1,0:T(8,128)(2,1)S(1)}, bf16[2,128,128]{2,1,0:T(8,128)(2,1)S(1)}, u32[]{:S(2)}, u32[]{:S(2)}) collective-permute-start(bf16[2,128,128]{2,1,0:T(8,128)(2,1)S(1)} %get-tuple-element.106), channel_id=1, source_target_pairs={{0,32},{16,48},{32,0},{48,16},{64,96},{80,112},{96,64},{112,80},{1... | collective-permute-start | bytes 196616 | tf_op jit(solution)/shard_map/ppermute | solution.py:246
  76.8 13.9 %collective-permute-start.25 = (bf16[2,128,128]{2,1,0:T(8,128)(2,1)S(1)}, bf16[2,128,128]{2,1,0:T(8,128)(2,1)S(1)}, u32[]{:S(2)}, u32[]{:S(2)}) collective-permute-start(bf16[2,128,128]{2,1,0:T(8,128)(2,1)S(1)} %get-tuple-element.105), channel_id=1, source_target_pairs={{0,48},{16,0},{32,16},{48,32},{64,112},{80,64},{96,80},{112,96},{1... | collective-permute-start | bytes 196616 | tf_op jit(solution)/shard_map/ppermute | solution.py:246
  86.7 11.6 %collective-permute-start.26 = (bf16[2,2,2,2,128,128]{5,4,3,2,1,0:T(8,128)(2,1)S(1)}, bf16[2,2,2,2,128,128]{5,4,3,2,1,0:T(8,128)(2,1)S(1)}, u32[]{:S(2)}, u32[]{:S(2)}) collective-permute-start(bf16[2,2,2,2,128,128]{5,4,3,2,1,0:T(8,128)(2,1)S(1)} %bitcast.105), channel_id=1, source_target_pairs={{0,16},{16,32},{32,48},{48,0},{64,80},{80,96},{96,112},{112,64},{1... | collective-permute-start | bytes 1572872 | tf_op jit(solution)/shard_map/ppermute | solution.py:246
  90.8 17.4 %collective-permute-start.27 = (bf16[2,2,2,2,128,128]{5,4,3,2,1,0:T(8,128)(2,1)S(1)}, bf16[2,2,2,2,128,128]{5,4,3,2,1,0:T(8,128)(2,1)S(1)}, u32[]{:S(2)}, u32[]{:S(2)}) collective-permute-start(bf16[2,2,2,2,128,128]{5,4,3,2,1,0:T(8,128)(2,1)S(1)} %bitcast.104), channel_id=1, source_target_pairs={{0,32},{16,48},{32,0},{48,16},{64,96},{80,112},{96,64},{112,80},{1... | collective-permute-start | bytes 1572872 | tf_op jit(solution)/shard_map/ppermute | solution.py:246
  93.6 23.7 %collective-permute-start.28 = (bf16[2,2,2,2,128,128]{5,4,3,2,1,0:T(8,128)(2,1)S(1)}, bf16[2,2,2,2,128,128]{5,4,3,2,1,0:T(8,128)(2,1)S(1)}, u32[]{:S(2)}, u32[]{:S(2)}) collective-permute-start(bf16[2,2,2,2,128,128]{5,4,3,2,1,0:T(8,128)(2,1)S(1)} %bitcast.103), channel_id=1, source_target_pairs={{0,48},{16,0},{32,16},{48,32},{64,112},{80,64},{96,80},{112,96},{1... | collective-permute-start | bytes 1572872 | tf_op jit(solution)/shard_map/ppermute | solution.py:246
  96.5 22.9 %collective-permute-start.12 = (bf16[8,2,128,128]{3,2,1,0:T(8,128)(2,1)S(1)}, bf16[8,2,128,128]{3,2,1,0:T(8,128)(2,1)S(1)}, u32[]{:S(2)}, u32[]{:S(2)}) collective-permute-start(bf16[8,2,128,128]{3,2,1,0:T(8,128)(2,1)S(1)} %get-tuple-element.65), channel_id=1, source_target_pairs={{0,4},{1,5},{2,6},{3,7},{4,8},{5,9},{6,10},{7,11},{8,12},{9,13},{1... | collective-permute-start | bytes 1572872 | tf_op jit(solution)/shard_map/ppermute | solution.py:241
  96.6 25.2 %collective-permute-start.13 = (bf16[8,2,128,128]{3,2,1,0:T(8,128)(2,1)S(1)}, bf16[8,2,128,128]{3,2,1,0:T(8,128)(2,1)S(1)}, u32[]{:S(2)}, u32[]{:S(2)}) collective-permute-start(bf16[8,2,128,128]{3,2,1,0:T(8,128)(2,1)S(1)} %get-tuple-element.66), channel_id=1, source_target_pairs={{0,12},{1,13},{2,14},{3,15},{4,0},{5,1},{6,2},{7,3},{8,4},{9,5},{1... | collective-permute-start | bytes 1572872 | tf_op jit(solution)/shard_map/ppermute | solution.py:241
  98.3 24.1 %collective-permute-start.16 = (bf16[4,2,128,128]{3,2,1,0:T(8,128)(2,1)S(1)}, bf16[4,2,128,128]{3,2,1,0:T(8,128)(2,1)S(1)}, u32[]{:S(2)}, u32[]{:S(2)}) collective-permute-start(bf16[4,2,128,128]{3,2,1,0:T(8,128)(2,1)S(1)} %add_convert_fusion.2), channel_id=1, source_target_pairs={{0,8},{1,9},{2,10},{3,11},{4,12},{5,13},{6,14},{7,15},{8,0},{9,1},... | collective-permute-start | bytes 786440 | tf_op jit(solution)/shard_map/ppermute | solution.py:241
  108.2 14.1 %collective-permute-start.21 = (bf16[3,2,128,128]{3,2,1,0:T(8,128)(2,1)S(1)}, bf16[3,2,128,128]{3,2,1,0:T(8,128)(2,1)S(1)}, u32[]{:S(2)}, u32[]{:S(2)}) collective-permute-start(bf16[3,2,128,128]{3,2,1,0:T(8,128)(2,1)S(1)} %slice_bitcast_fusion.2), channel_id=1, source_target_pairs={{0,64},{16,80},{32,96},{48,112},{64,0},{80,16},{96,32},{112,48},{1... | collective-permute-start | bytes 589832 | tf_op jit(solution)/shard_map/ppermute | solution.py:246
  117.7 17.6 %collective-permute-start.29 = (bf16[2,2,2,128,128]{4,3,2,1,0:T(8,128)(2,1)S(1)}, bf16[2,2,2,128,128]{4,3,2,1,0:T(8,128)(2,1)S(1)}, u32[]{:S(2)}, u32[]{:S(2)}) collective-permute-start(bf16[2,2,2,128,128]{4,3,2,1,0:T(8,128)(2,1)S(1)} %get-tuple-element.102), channel_id=1, source_target_pairs={{0,1},{1,0},{2,3},{3,2},{4,5},{5,4},{6,7},{7,6},{8,9},{9,8},{10,11... | collective-permute-start | bytes 786440 | tf_op jit(solution)/shard_map/ppermute | solution.py:241
  119.4 16.0 %collective-permute-start.30 = (bf16[2,2,2,128,128]{4,3,2,1,0:T(8,128)(2,1)S(1)}, bf16[2,2,2,128,128]{4,3,2,1,0:T(8,128)(2,1)S(1)}, u32[]{:S(2)}, u32[]{:S(2)}) collective-permute-start(bf16[2,2,2,128,128]{4,3,2,1,0:T(8,128)(2,1)S(1)} %get-tuple-element.103), channel_id=1, source_target_pairs={{0,65},{1,64},{2,67},{3,66},{4,69},{5,68},{6,71},{7,70},{8,73},{9,... | collective-permute-start | bytes 786440 | tf_op jit(solution)/shard_map/ppermute | solution.py:254
  121.9 12.1 %collective-permute-start.14 = (bf16[4,2,128,128]{3,2,1,0:T(8,128)(2,1)S(1)}, bf16[4,2,128,128]{3,2,1,0:T(8,128)(2,1)S(1)}, u32[]{:S(2)}, u32[]{:S(2)}) collective-permute-start(bf16[4,2,128,128]{3,2,1,0:T(8,128)(2,1)S(1)} %add_convert_fusion.3), channel_id=1, source_target_pairs={{0,2},{1,3},{2,0},{3,1},{4,6},{5,7},{6,4},{7,5},{8,10},{9,11},{10,... | collective-permute-start | bytes 786440 | tf_op jit(solution)/shard_map/ppermute | solution.py:241
  134.3 2.6 %collective-permute-start.17 = (bf16[2,2,128,128]{3,2,1,0:T(8,128)(2,1)S(1)}, bf16[2,2,128,128]{3,2,1,0:T(8,128)(2,1)S(1)}, u32[]{:S(2)}, u32[]{:S(2)}) collective-permute-start(bf16[2,2,128,128]{3,2,1,0:T(8,128)(2,1)S(1)} %get-tuple-element.107), channel_id=1, source_target_pairs={{0,1},{1,0},{2,3},{3,2},{4,5},{5,4},{6,7},{7,6},{8,9},{9,8},{10,11... | collective-permute-start | bytes 393224 | tf_op jit(solution)/shard_map/ppermute | solution.py:241
  (3 other events, 11.6 us)

commit v4 on v3

--- a/solution.py
+++ b/solution.py
@@ -57,13 +57,6 @@
         acc[...]=jnp.zeros(acc.shape,F32)
     for m in range(8):
         pltpu.make_async_copy(pieces[m],kv.at[pl.ds(4*m,4)],sem.at[m]).wait()
-
-    def spot(j,p,h):
-        if first:
-            return chk[0,p]*4+2*j+h
-        if h==0:
-            return chk[0,p]*3+2*j
-        return jnp.where(j==0,chk[0,p]*3+1,24+chk[1,p])
 
     def block(j,carry):
         n=cnt[j]
@@ -132,7 +125,7 @@
         o_ref[...]=jnp.zeros(o_ref.shape,F32)
         def backward(p,c):
             a0=idx[j,2*p]; a1=idx[j,2*p+1]
-            spots=[spot(j,p,h) for h in range(2)]
+            out=bg.at[chk[0,p],j] if first else bg.at[j,chk[j,p]]
             k2=both(p,0); v2=both(p,1)
             halves=[]; total=[None,None]
             WG=dot(dom[...],v2,NT)
@@ -144,7 +137,7 @@
                 if g<2: total[h]=ds
                 else:
                     b=(total[h]+ds).astype(BF)
-                    bg[spots[h],0]=b[:,:BS]; bg[spots[h],1]=b[:,BS:]
+                    out[h,0]=b[:,:BS]; out[h,1]=b[:,BS:]
                 half=ds.astype(BF)
                 halves.append(half)
             hs=jnp.concatenate(halves,0)
@@ -156,8 +149,8 @@
             return c
         loop2(pairs,backward)
         def clear(p,c):
-            for h in range(2):
-                bg[spot(j,p,h)]=jnp.zeros((2,BS,BS),BF)
+            out=bg.at[chk[0,p],j] if first else bg.at[j,chk[j,p]]
+            out[...]=jnp.zeros((2,2,BS,BS),BF)
             return c
         lax.fori_loop(pairs,8,clear,0)
         x=jnp.zeros((BS,BS),F32)
@@ -178,7 +171,8 @@
     AN=pl.BlockSpec(memory_space=pl.ANY)
     args=[idx,cnt,chk,qgc,bias,*pieces]
     specs=[SM]*3+[VM]*2+[AN]*8
-    shapes=[((2,BS,BS),BF),((2,BS,BS),BF),((32,2,BS,BS),BF),((32,2,BS,BS),F32)]
+    lead=(8,2) if first else (2,8)
+    shapes=[((2,BS,BS),BF),((2,BS,BS),BF),(lead+(2,2,BS,BS),BF),((32,2,BS,BS),F32)]
     if not first:
         args.append(prev)
         specs.append(VM)
@@ -340,8 +334,8 @@
         idx0,cnt0,second,mine,bias_mine,pieces,acc
     )
 
-    straight=bg0[:24].reshape(4,2,3,2,BS,BS)
-    turned=bg0[24:].reshape(2,4,2,BS,BS)
+    straight=bg0[0].reshape(4,2,2,2,BS,BS)
+    turned=bg0[1].reshape(2,4,2,2,BS,BS)
     turned_in=to_row(turned[1],1,0)
     straight=row_sums(straight).astype(BF)
     turned=plus(turned[0],turned_in).astype(BF)
@@ -367,7 +361,7 @@
     own_far=swap(own[2:])
     key_grad,value_grad=small_call(join_kernel,own[:2],own_far,sel)
 
-    bias_own=jnp.concatenate([straight,turned[None]],0).reshape(2,2,2,BS,BS)
+    bias_own=jnp.stack([straight,turned],0)
     low=jnp.where(core==0,bias_own,bias_other)
     high=jnp.where(core==0,bias_other,bias_own)
     bias_grad=jnp.concatenate([low,high],1).transpose(0,1,3,2,4)

time: 139 us -> 152 us (1.094)
  the two profiles are of different devices: /device:TPU:9 before, /device:TPU:0 now
where the time goes in v4:
time: 152 us; the launch traced here: 151 us
  starting transfers between devices  62.6 us (41%)
  waiting for transfers between devices  49.1 us (32%)
  Pallas kernels  20.5 us (13%)
  local copies, waits for them, and re-layouts  10.9 us (7%)
  matrix products  3.64 us (2%)
  other arithmetic  3.01 us (2%)
    ppermute x11, starting transfers between devices, to_row(): return lax.ppermute(x, 'row', pairs)  36.4 us
    ppermute x19, waiting for transfers between devices, to_col(): return lax.ppermute(x, 'col', pairs)  35.3 us
    ppermute x19, starting transfers between devices, to_col(): return lax.ppermute(x, 'col', pairs)  25.4 us
    pallas_call x2, Pallas kernels, attend_blocks(): pl.pallas_call(kernel, out_shape=tuple((jax.ShapeDtypeStruct(*s) for s in...  19.9 us
    ppermute x11, waiting for transfers between devices, to_row(): return lax.ppermute(x, 'row', pairs)  10.6 us
    unnamed x13, local copies, waits for them, and re-layouts  4.52 us
    dot_general x5, matrix products, split(): lax.dot_general(x.reshape(2 * BS, 2 * BS), sel, NN, preferred_element_typ...  3.64 us
    optimization_barrier x1, local copies, waits for them, and re-layouts, body(): shard, pair_bias = lax.optimization_barrier((shard, pair_bias))  3.36 us
  transfers between devices with their start and end apart: 31, of which 15 were waited for; matrix products, arithmetic and copies ran while one was open for 9% of the time, Pallas kernels for 8%

profile of v4, /device:TPU:0, one launch (start us, length us, event | category | flops | bytes accessed | tf_op | source)
XLA Modules:
  0.0 150.8 jit_solution(15105831269947260791)
XLA Ops:
  6.2 3.4 %copy.23 = bf16[2,4,128,16,128]{4,2,3,1,0:T(8,128)(2,1)S(1)} copy(bf16[2,4,128,16,128]{4,3,2,1,0:T(8,128)(2,1)} %param.13) | data formatting | bytes 8388608 | tf_op jit(solution)/shard_map/optimization_barrier | solution.py:289
  9.6 1.6 %dynamic-slice_bitcast_fusion = (bf16[2,2,16,128,128]{4,3,2,1,0:T(8,128)(2,1)}, bf16[2,2,16,128,128]{4,3,2,1,0:T(8,128)(2,1)S(1)}) fusion(bf16[2,4,128,16,128]{4,2,3,1,0:T(8,128)(2,1)S(1)} %copy.23, s32[]{:T(128)S(6)} %select_n.186, s32[]{:T(128)S(6)} %select_n.185), kind=kLoop, calls=%fused_computation | loop fusion | bytes 8388616 | tf_op jit(solution)/shard_map/dynamic_slice | solution.py:312
  12.5 1.7 %collective-permute-start.4 = (bf16[4,2,128,128]{3,2,1,0:T(8,128)(2,1)S(1)}, bf16[4,2,128,128]{3,2,1,0:T(8,128)(2,1)S(1)}, u32[]{:S(2)}, u32[]{:S(2)}) collective-permute-start(bf16[4,2,128,128]{3,2,1,0:T(8,128)(2,1)S(1)} %pad_maximum_fusion.refs_5_), channel_id=1, source_target_pairs={{0,2},{1,3},{2,0},{3,1},{4,6},{5,7},{6,4},{7,5},{8,10},{9,11},{10,... | collective-permute-start | bytes 786440 | tf_op jit(solution)/shard_map/ppermute | solution.py:235
  14.2 3.2 %collective-permute-start.7 = (bf16[4,2,128,128]{3,2,1,0:T(8,128)(2,1)S(1)}, bf16[4,2,128,128]{3,2,1,0:T(8,128)(2,1)S(1)}, u32[]{:S(2)}, u32[]{:S(2)}) collective-permute-start(bf16[4,2,128,128]{3,2,1,0:T(8,128)(2,1)S(1)} %pad_maximum_fusion.refs_5_), channel_id=1, source_target_pairs={{0,8},{1,9},{2,10},{3,11},{4,12},{5,13},{6,14},{7,15},{8,0},{9,1},... | collective-permute-start | bytes 786440 | tf_op jit(solution)/shard_map/ppermute | solution.py:235
  18.6 1.6 %collective-permute-done.1.refs_3_ = bf16[3,2,128,128]{3,2,1,0:T(8,128)(2,1)S(1)} collective-permute-done((bf16[3,2,128,128]{3,2,1,0:T(8,128)(2,1)}, bf16[3,2,128,128]{3,2,1,0:T(8,128)(2,1)S(1)}, u32[]{:S(2)}, u32[]{:S(2)}) %collective-permute-start.1) | collective-permute-done | bytes 196640 | tf_op jit(solution)/shard_map/ppermute | solution.py:235
  21.3 1.7 %collective-permute-start.10 = (bf16[4,2,128,128]{3,2,1,0:T(8,128)(2,1)S(1)}, bf16[4,2,128,128]{3,2,1,0:T(8,128)(2,1)S(1)}, u32[]{:S(2)}, u32[]{:S(2)}) collective-permute-start(bf16[4,2,128,128]{3,2,1,0:T(8,128)(2,1)S(1)} %collective-permute-done.4.refs_6_), channel_id=1, source_target_pairs={{0,4},{1,5},{2,6},{3,7},{4,8},{5,9},{6,10},{7,11},{8,12},{9,13},{1... | collective-permute-start | bytes 786440 | tf_op jit(solution)/shard_map/ppermute | solution.py:235
  23.0 1.9 %collective-permute-done.7.refs_9_ = bf16[4,2,128,128]{3,2,1,0:T(8,128)(2,1)S(1)} collective-permute-done((bf16[4,2,128,128]{3,2,1,0:T(8,128)(2,1)S(1)}, bf16[4,2,128,128]{3,2,1,0:T(8,128)(2,1)S(1)}, u32[]{:S(2)}, u32[]{:S(2)}) %collective-permute-start.7) | collective-permute-done | bytes 262176 | tf_op jit(solution)/shard_map/ppermute | solution.py:235
  24.9 3.0 %collective-permute-start.6 = (bf16[4,2,128,128]{3,2,1,0:T(8,128)(2,1)S(1)}, bf16[4,2,128,128]{3,2,1,0:T(8,128)(2,1)S(1)}, u32[]{:S(2)}, u32[]{:S(2)}) collective-permute-start(bf16[4,2,128,128]{3,2,1,0:T(8,128)(2,1)S(1)} %collective-permute-done.4.refs_6_), channel_id=1, source_target_pairs={{0,12},{1,13},{2,14},{3,15},{4,0},{5,1},{6,2},{7,3},{8,4},{9,5},{1... | collective-permute-start | bytes 786440 | tf_op jit(solution)/shard_map/ppermute | solution.py:235
  27.9 2.9 %collective-permute-done.5.refs_7_ = bf16[4,2,128,128]{3,2,1,0:T(8,128)(2,1)S(1)} collective-permute-done((bf16[4,2,128,128]{3,2,1,0:T(8,128)(2,1)S(1)}, bf16[4,2,128,128]{3,2,1,0:T(8,128)(2,1)S(1)}, u32[]{:S(2)}, u32[]{:S(2)}) %collective-permute-start.5) | collective-permute-done | bytes 262176 | tf_op jit(solution)/shard_map/ppermute | solution.py:235
  31.6 4.1 %collective-permute-done.10.refs_12_ = bf16[4,2,128,128]{3,2,1,0:T(8,128)(2,1)S(1)} collective-permute-done((bf16[4,2,128,128]{3,2,1,0:T(8,128)(2,1)S(1)}, bf16[4,2,128,128]{3,2,1,0:T(8,128)(2,1)S(1)}, u32[]{:S(2)}, u32[]{:S(2)}) %collective-permute-start.10) | collective-permute-done | bytes 262176 | tf_op jit(solution)/shard_map/ppermute | solution.py:235
  35.7 1.9 %collective-permute-done.8.refs_10_ = bf16[4,2,128,128]{3,2,1,0:T(8,128)(2,1)S(1)} collective-permute-done((bf16[4,2,128,128]{3,2,1,0:T(8,128)(2,1)S(1)}, bf16[4,2,128,128]{3,2,1,0:T(8,128)(2,1)S(1)}, u32[]{:S(2)}, u32[]{:S(2)}) %collective-permute-start.8) | collective-permute-done | bytes 262176 | tf_op jit(solution)/shard_map/ppermute | solution.py:235
  37.7 8.2 %attend_blocks.2 = (bf16[2,128,128]{2,1,0:T(8,128)(2,1)S(1)}, bf16[2,128,128]{2,1,0:T(8,128)(2,1)S(1)}, bf16[8,2,2,2,128,128]{5,4,3,2,1,0:T(8,128)(2,1)S(1)}, f32[32,2,128,128]{3,2,1,0:T(8,128)S(1)}) custom-call(s32[2,16]{1,0:T(2,128)S(1)} %fusion.46.refs_0_, s32[2]{0:T(128)S(1)} %slice_reduce_fusion.refs_1_, s32[1,8]{1,0:T(1,128)S(1)} %get-tuple-element.113.refs_2_, ...), custom_call_target="tpu_custom_call" | custom-call | flops 10000000000 | bytes 25165824 | tf_op jit(solution)/shard_map/attend_blocks/pallas_call | solution.py:184
  46.1 2.2 %collective-permute-start.26 = (bf16[2,2,2,2,128,128]{5,4,3,2,1,0:T(8,128)(2,1)S(1)}, bf16[2,2,2,2,128,128]{5,4,3,2,1,0:T(8,128)(2,1)S(1)}, u32[]{:S(2)}, u32[]{:S(2)}) collective-permute-start(bf16[2,2,2,2,128,128]{5,4,3,2,1,0:T(8,128)(2,1)S(1)} %get-tuple-element.87), channel_id=1, source_target_pairs={{0,16},{16,32},{32,48},{48,0},{64,80},{80,96},{96,112},{112,64},{1... | collective-permute-start | bytes 1572872 | tf_op jit(solution)/shard_map/ppermute | solution.py:240
  48.3 11.7 %attend_blocks.3 = (bf16[2,128,128]{2,1,0:T(8,128)(2,1)S(1)}, bf16[2,128,128]{2,1,0:T(8,128)(2,1)S(1)}, bf16[2,8,2,2,128,128]{5,4,3,2,1,0:T(8,128)(2,1)S(1)}, f3...) custom-call(s32[2,16]{1,0:T(2,128)S(1)} %fusion.41.refs_0_, ...), custom_call_target="tpu_custom_call", output_to_operand_aliasing={{3}: (13, {})} | custom-call | flops 10000000000 | bytes 25165824 | tf_op jit(solution)/shard_map/attend_blocks/pallas_call | solution.py:184
  60.0 2.0 %collective-permute-start.18 = (bf16[2,2,2,128,128]{4,3,2,1,0:T(8,128)(2,1)S(1)}, bf16[2,2,2,128,128]{4,3,2,1,0:T(8,128)(2,1)S(1)}, u32[]{:S(2)}, u32[]{:S(2)}) collective-permute-start(bf16[2,2,2,128,128]{4,3,2,1,0:T(8,128)(2,1)S(1)} %get-tuple-element.90), channel_id=1, source_target_pairs={{0,16},{16,32},{32,48},{48,0},{64,80},{80,96},{96,112},{112,64},{1... | collective-permute-start | bytes 786440 | tf_op jit(solution)/shard_map/ppermute | solution.py:240
  62.0 1.9 %collective-permute-start.19 = (bf16[2,2,2,128,128]{4,3,2,1,0:T(8,128)(2,1)S(1)}, bf16[2,2,2,128,128]{4,3,2,1,0:T(8,128)(2,1)S(1)}, u32[]{:S(2)}, u32[]{:S(2)}) collective-permute-start(bf16[2,2,2,128,128]{4,3,2,1,0:T(8,128)(2,1)S(1)} %get-tuple-element.92), channel_id=1, source_target_pairs={{0,32},{16,48},{32,0},{48,16},{64,96},{80,112},{96,64},{112,80},{1... | collective-permute-start | bytes 786440 | tf_op jit(solution)/shard_map/ppermute | solution.py:240
  63.9 2.4 %collective-permute-start.20 = (bf16[2,2,2,128,128]{4,3,2,1,0:T(8,128)(2,1)S(1)}, bf16[2,2,2,128,128]{4,3,2,1,0:T(8,128)(2,1)S(1)}, u32[]{:S(2)}, u32[]{:S(2)}) collective-permute-start(bf16[2,2,2,128,128]{4,3,2,1,0:T(8,128)(2,1)S(1)} %get-tuple-element.91), channel_id=1, source_target_pairs={{0,48},{16,0},{32,16},{48,32},{64,112},{80,64},{96,80},{112,96},{1... | collective-permute-start | bytes 786440 | tf_op jit(solution)/shard_map/ppermute | solution.py:240
  69.7 2.7 %collective-permute-start.22 = (bf16[4,2,2,128,128]{4,3,2,1,0:T(8,128)(2,1)S(1)}, bf16[4,2,2,128,128]{4,3,2,1,0:T(8,128)(2,1)S(1)}, u32[]{:S(2)}, u32[]{:S(2)}) collective-permute-start(bf16[4,2,2,128,128]{4,3,2,1,0:T(8,128)(2,1)S(1)} %slice_bitcast_fusion), channel_id=1, source_target_pairs={{0,64},{16,80},{32,96},{48,112},{64,0},{80,16},{96,32},{112,48},{1... | collective-permute-start | bytes 1572872 | tf_op jit(solution)/shard_map/ppermute | solution.py:240
  72.4 4.3 %collective-permute-done.19 = bf16[2,2,2,128,128]{4,3,2,1,0:T(8,128)(2,1)S(1)} collective-permute-done((bf16[2,2,2,128,128]{4,3,2,1,0:T(8,128)(2,1)S(1)}, bf16[2,2,2,128,128]{4,3,2,1,0:T(8,128)(2,1)S(1)}, u32[]{:S(2)}, u32[]{:S(2)}) %collective-permute-start.19) | collective-permute-done | bytes 262176 | tf_op jit(solution)/shard_map/ppermute | solution.py:240
  76.7 5.1 %collective-permute-start.12 = (bf16[8,2,128,128]{3,2,1,0:T(8,128)(2,1)S(1)}, bf16[8,2,128,128]{3,2,1,0:T(8,128)(2,1)S(1)}, u32[]{:S(2)}, u32[]{:S(2)}) collective-permute-start(bf16[8,2,128,128]{3,2,1,0:T(8,128)(2,1)S(1)} %get-tuple-element.65), channel_id=1, source_target_pairs={{0,4},{1,5},{2,6},{3,7},{4,8},{5,9},{6,10},{7,11},{8,12},{9,13},{1... | collective-permute-start | bytes 1572872 | tf_op jit(solution)/shard_map/ppermute | solution.py:235
  81.9 7.6 %collective-permute-done.15 = bf16[4,2,128,128]{3,2,1,0:T(8,128)(2,1)S(1)} collective-permute-done((bf16[4,2,128,128]{3,2,1,0:T(8,128)(2,1)S(1)}, bf16[4,2,128,128]{3,2,1,0:T(8,128)(2,1)S(1)}, u32[]{:S(2)}, u32[]{:S(2)}) %collective-permute-start.15) | collective-permute-done | bytes 262176 | tf_op jit(solution)/shard_map/ppermute | solution.py:235
  90.9 5.1 %collective-permute-done.21 = bf16[2,2,128,128]{3,2,1,0:T(8,128)(2,1)S(1)} collective-permute-done((bf16[2,2,128,128]{3,2,1,0:T(8,128)(2,1)S(1)}, bf16[2,2,128,128]{3,2,1,0:T(8,128)(2,1)S(1)}, u32[]{:S(2)}, u32[]{:S(2)}) %collective-permute-start.21) | collective-permute-done | bytes 131104 | tf_op jit(solution)/shard_map/ppermute | solution.py:240
  96.0 3.3 %collective-permute-start.13 = (bf16[8,2,128,128]{3,2,1,0:T(8,128)(2,1)S(1)}, bf16[8,2,128,128]{3,2,1,0:T(8,128)(2,1)S(1)}, u32[]{:S(2)}, u32[]{:S(2)}) collective-permute-start(bf16[8,2,128,128]{3,2,1,0:T(8,128)(2,1)S(1)} %get-tuple-element.66), channel_id=1, source_target_pairs={{0,12},{1,13},{2,14},{3,15},{4,0},{5,1},{6,2},{7,3},{8,4},{9,5},{1... | collective-permute-start | bytes 1572872 | tf_op jit(solution)/shard_map/ppermute | solution.py:235
  99.3 2.1 %collective-permute-start.28 = (bf16[2,2,2,2,128,128]{5,4,3,2,1,0:T(8,128)(2,1)S(1)}, bf16[2,2,2,2,128,128]{5,4,3,2,1,0:T(8,128)(2,1)S(1)}, u32[]{:S(2)}, u32[]{:S(2)}) collective-permute-start(bf16[2,2,2,2,128,128]{5,4,3,2,1,0:T(8,128)(2,1)S(1)} %get-tuple-element.88), channel_id=1, source_target_pairs={{0,48},{16,0},{32,16},{48,32},{64,112},{80,64},{96,80},{112,96},{1... | collective-permute-start | bytes 1572872 | tf_op jit(solution)/shard_map/ppermute | solution.py:240
  101.6 3.9 %collective-permute-start.16 = (bf16[4,2,128,128]{3,2,1,0:T(8,128)(2,1)S(1)}, bf16[4,2,128,128]{3,2,1,0:T(8,128)(2,1)S(1)}, u32[]{:S(2)}, u32[]{:S(2)}) collective-permute-start(bf16[4,2,128,128]{3,2,1,0:T(8,128)(2,1)S(1)} %add_convert_fusion.2), channel_id=1, source_target_pairs={{0,8},{1,9},{2,10},{3,11},{4,12},{5,13},{6,14},{7,15},{8,0},{9,1},... | collective-permute-start | bytes 786440 | tf_op jit(solution)/shard_map/ppermute | solution.py:235
  105.5 8.3 %collective-permute-done.13 = bf16[8,2,128,128]{3,2,1,0:T(8,128)(2,1)S(1)} collective-permute-done((bf16[8,2,128,128]{3,2,1,0:T(8,128)(2,1)S(1)}, bf16[8,2,128,128]{3,2,1,0:T(8,128)(2,1)S(1)}, u32[]{:S(2)}, u32[]{:S(2)}) %collective-permute-start.13) | collective-permute-done | bytes 524320 | tf_op jit(solution)/shard_map/ppermute | solution.py:235
  113.8 7.6 %collective-permute-start.23 = (bf16[2,2,128,128]{3,2,1,0:T(8,128)(2,1)S(1)}, bf16[2,2,128,128]{3,2,1,0:T(8,128)(2,1)S(1)}, u32[]{:S(2)}, u32[]{:S(2)}) collective-permute-start(bf16[2,2,128,128]{3,2,1,0:T(8,128)(2,1)S(1)} %get-tuple-element.97), channel_id=1, source_target_pairs={{0,16},{16,32},{32,48},{48,0},{64,80},{80,96},{96,112},{112,64},{1... | collective-permute-start | bytes 393224 | tf_op jit(solution)/shard_map/ppermute | solution.py:240
  121.5 11.6 %collective-permute-start.24 = (bf16[2,2,128,128]{3,2,1,0:T(8,128)(2,1)S(1)}, bf16[2,2,128,128]{3,2,1,0:T(8,128)(2,1)S(1)}, u32[]{:S(2)}, u32[]{:S(2)}) collective-permute-start(bf16[2,2,128,128]{3,2,1,0:T(8,128)(2,1)S(1)} %get-tuple-element.99), channel_id=1, source_target_pairs={{0,32},{16,48},{32,0},{48,16},{64,96},{80,112},{96,64},{112,80},{1... | collective-permute-start | bytes 393224 | tf_op jit(solution)/shard_map/ppermute | solution.py:240
  133.1 2.6 %collective-permute-start.25 = (bf16[2,2,128,128]{3,2,1,0:T(8,128)(2,1)S(1)}, bf16[2,2,128,128]{3,2,1,0:T(8,128)(2,1)S(1)}, u32[]{:S(2)}, u32[]{:S(2)}) collective-permute-start(bf16[2,2,128,128]{3,2,1,0:T(8,128)(2,1)S(1)} %get-tuple-element.98), channel_id=1, source_target_pairs={{0,48},{16,0},{32,16},{48,32},{64,112},{80,64},{96,80},{112,96},{1... | collective-permute-start | bytes 393224 | tf_op jit(solution)/shard_map/ppermute | solution.py:240
  138.4 5.5 %collective-permute-done.14 = bf16[4,2,128,128]{3,2,1,0:T(8,128)(2,1)S(1)} collective-permute-done((bf16[4,2,128,128]{3,2,1,0:T(8,128)(2,1)S(1)}, bf16[4,2,128,128]{3,2,1,0:T(8,128)(2,1)S(1)}, u32[]{:S(2)}, u32[]{:S(2)}) %collective-permute-start.14) | collective-permute-done | bytes 262176 | tf_op jit(solution)/shard_map/ppermute | solution.py:235
  144.2 3.2 %collective-permute-done.30 = bf16[2,2,2,128,128]{4,3,2,1,0:T(8,128)(2,1)S(1)} collective-permute-done((bf16[2,2,2,128,128]{4,3,2,1,0:T(8,128)(2,1)S(1)}, bf16[2,2,2,128,128]{4,3,2,1,0:T(8,128)(2,1)S(1)}, u32[]{:S(2)}, u32[]{:S(2)}) %collective-permute-start.30) | collective-permute-done | bytes 262176 | tf_op jit(solution)/shard_map/ppermute | solution.py:248
  147.6 1.3 copy.29
  (96 shorter events, 20.1 us)
Async XLA Ops:
  3.0 3.2 %collective-permute-start.2 = (bf16[2,2,128,128]{3,2,1,0:T(8,128)(2,1)S(1)}, bf16[2,2,128,128]{3,2,1,0:T(8,128)(2,1)S(1)}, u32[]{:S(2)}, u32[]{:S(2)}) collective-permute-start(bf16[2,2,128,128]{3,2,1,0:T(8,128)(2,1)S(1)} %pad_maximum_fusion.5), channel_id=1, source_target_pairs={{0,1},{1,0},{2,3},{3,2},{4,5},{5,4},{6,7},{7,6},{8,9},{9,8},{10,11... | collective-permute-start | bytes 393224 | tf_op jit(solution)/shard_map/ppermute | solution.py:235
  4.6 13.8 %collective-permute-start = (s32[2,17]{1,0:T(2,128)S(1)}, s32[2,17]{1,0:T(2,128)S(1)}, u32[]{:S(2)}, u32[]{:S(2)}) collective-permute-start(s32[2,17]{1,0:T(2,128)S(1)} %pad_add_fusion), channel_id=1, source_target_pairs={{0,1},{1,0},{2,3},{3,2},{4,5},{5,4},{6,7},{7,6},{8,9},{9,8},{10,11... | collective-permute-start | bytes 416 | tf_op jit(solution)/shard_map/ppermute | solution.py:235
  11.3 7.3 %copy-start.3 = (s32[2,16]{1,0:T(2,128)S(1)}, s32[2,16]{1,0:T(2,128)}, u32[]{:S(2)}) copy-start(s32[2,16]{1,0:T(2,128)} %param.14) | copy-start | bytes 388
  11.3 26.4 %collective-permute-start.3 = (bf16[2,2,16,128,128]{4,3,2,1,0:T(8,128)(2,1)}, bf16[2,2,16,128,128]{4,3,2,1,0:T(8,128)(2,1)}, u32[]{:S(2)}, u32[]{:S(2)}) collective-permute-start(bf16[2,2,16,128,128]{4,3,2,1,0:T(8,128)(2,1)} %get-tuple-element.85), channel_id=1, source_target_pairs={{0,1},{1,0},{2,3},{3,2},{4,5},{5,4},{6,7},{7,6},{8,9},{9,8},{10,11... | collective-permute-start | bytes 6291464 | tf_op jit(solution)/shard_map/ppermute | solution.py:235
  12.5 8.8 %collective-permute-start.4 = (bf16[4,2,128,128]{3,2,1,0:T(8,128)(2,1)S(1)}, bf16[4,2,128,128]{3,2,1,0:T(8,128)(2,1)S(1)}, u32[]{:S(2)}, u32[]{:S(2)}) collective-permute-start(bf16[4,2,128,128]{3,2,1,0:T(8,128)(2,1)S(1)} %pad_maximum_fusion.refs_5_), channel_id=1, source_target_pairs={{0,2},{1,3},{2,0},{3,1},{4,6},{5,7},{6,4},{7,5},{8,10},{9,11},{10,... | collective-permute-start | bytes 786440 | tf_op jit(solution)/shard_map/ppermute | solution.py:235
  14.2 10.7 %collective-permute-start.7 = (bf16[4,2,128,128]{3,2,1,0:T(8,128)(2,1)S(1)}, bf16[4,2,128,128]{3,2,1,0:T(8,128)(2,1)S(1)}, u32[]{:S(2)}, u32[]{:S(2)}) collective-permute-start(bf16[4,2,128,128]{3,2,1,0:T(8,128)(2,1)S(1)} %pad_maximum_fusion.refs_5_), channel_id=1, source_target_pairs={{0,8},{1,9},{2,10},{3,11},{4,12},{5,13},{6,14},{7,15},{8,0},{9,1},... | collective-permute-start | bytes 786440 | tf_op jit(solution)/shard_map/ppermute | solution.py:235
  17.4 13.5 %collective-permute-start.5 = (bf16[4,2,128,128]{3,2,1,0:T(8,128)(2,1)S(1)}, bf16[4,2,128,128]{3,2,1,0:T(8,128)(2,1)S(1)}, u32[]{:S(2)}, u32[]{:S(2)}) collective-permute-start(bf16[4,2,128,128]{3,2,1,0:T(8,128)(2,1)S(1)} %pad_maximum_fusion.refs_5_), channel_id=1, source_target_pairs={{0,12},{1,13},{2,14},{3,15},{4,0},{5,1},{6,2},{7,3},{8,4},{9,5},{1... | collective-permute-start | bytes 786440 | tf_op jit(solution)/shard_map/ppermute | solution.py:235
  18.5 1.7 %collective-permute-start.1 = (bf16[3,2,128,128]{3,2,1,0:T(8,128)(2,1)}, bf16[3,2,128,128]{3,2,1,0:T(8,128)(2,1)S(1)}, u32[]{:S(2)}, u32[]{:S(2)}) collective-permute-start(bf16[3,2,128,128]{3,2,1,0:T(8,128)(2,1)} %pad_maximum_fusion.3), channel_id=1, source_target_pairs={{0,1},{1,0},{2,3},{3,2},{4,5},{5,4},{6,7},{7,6},{8,9},{9,8},{10,11... | collective-permute-start | bytes 589832 | tf_op jit(solution)/shard_map/ppermute | solution.py:235
  20.2 11.4 %collective-permute-start.9 = (bf16[4,2,128,128]{3,2,1,0:T(8,128)(2,1)S(1)}, bf16[4,2,128,128]{3,2,1,0:T(8,128)(2,1)S(1)}, u32[]{:S(2)}, u32[]{:S(2)}) collective-permute-start(bf16[4,2,128,128]{3,2,1,0:T(8,128)(2,1)S(1)} %pad_maximum_fusion.refs_5_), channel_id=1, source_target_pairs={{0,4},{1,5},{2,6},{3,7},{4,8},{5,9},{6,10},{7,11},{8,12},{9,13},{1... | collective-permute-start | bytes 786440 | tf_op jit(solution)/shard_map/ppermute | solution.py:235
  21.3 14.4 %collective-permute-start.10 = (bf16[4,2,128,128]{3,2,1,0:T(8,128)(2,1)S(1)}, bf16[4,2,128,128]{3,2,1,0:T(8,128)(2,1)S(1)}, u32[]{:S(2)}, u32[]{:S(2)}) collective-permute-start(bf16[4,2,128,128]{3,2,1,0:T(8,128)(2,1)S(1)} %collective-permute-done.4.refs_6_), channel_id=1, source_target_pairs={{0,4},{1,5},{2,6},{3,7},{4,8},{5,9},{6,10},{7,11},{8,12},{9,13},{1... | collective-permute-start | bytes 786440 | tf_op jit(solution)/shard_map/ppermute | solution.py:235
  24.9 10.9 %collective-permute-start.6 = (bf16[4,2,128,128]{3,2,1,0:T(8,128)(2,1)S(1)}, bf16[4,2,128,128]{3,2,1,0:T(8,128)(2,1)S(1)}, u32[]{:S(2)}, u32[]{:S(2)}) collective-permute-start(bf16[4,2,128,128]{3,2,1,0:T(8,128)(2,1)S(1)} %collective-permute-done.4.refs_6_), channel_id=1, source_target_pairs={{0,12},{1,13},{2,14},{3,15},{4,0},{5,1},{6,2},{7,3},{8,4},{9,5},{1... | collective-permute-start | bytes 786440 | tf_op jit(solution)/shard_map/ppermute | solution.py:235
  30.9 6.8 %collective-permute-start.8 = (bf16[4,2,128,128]{3,2,1,0:T(8,128)(2,1)S(1)}, bf16[4,2,128,128]{3,2,1,0:T(8,128)(2,1)S(1)}, u32[]{:S(2)}, u32[]{:S(2)}) collective-permute-start(bf16[4,2,128,128]{3,2,1,0:T(8,128)(2,1)S(1)} %collective-permute-done.7.refs_9_), channel_id=1, source_target_pairs={{0,2},{1,3},{2,0},{3,1},{4,6},{5,7},{6,4},{7,5},{8,10},{9,11},{10,... | collective-permute-start | bytes 786440 | tf_op jit(solution)/shard_map/ppermute | solution.py:235
  46.1 75.4 %collective-permute-start.26 = (bf16[2,2,2,2,128,128]{5,4,3,2,1,0:T(8,128)(2,1)S(1)}, bf16[2,2,2,2,128,128]{5,4,3,2,1,0:T(8,128)(2,1)S(1)}, u32[]{:S(2)}, u32[]{:S(2)}) collective-permute-start(bf16[2,2,2,2,128,128]{5,4,3,2,1,0:T(8,128)(2,1)S(1)} %get-tuple-element.87), channel_id=1, source_target_pairs={{0,16},{16,32},{32,48},{48,0},{64,80},{80,96},{96,112},{112,64},{1... | collective-permute-start | bytes 1572872 | tf_op jit(solution)/shard_map/ppermute | solution.py:240
  60.0 9.6 %collective-permute-start.18 = (bf16[2,2,2,128,128]{4,3,2,1,0:T(8,128)(2,1)S(1)}, bf16[2,2,2,128,128]{4,3,2,1,0:T(8,128)(2,1)S(1)}, u32[]{:S(2)}, u32[]{:S(2)}) collective-permute-start(bf16[2,2,2,128,128]{4,3,2,1,0:T(8,128)(2,1)S(1)} %get-tuple-element.90), channel_id=1, source_target_pairs={{0,16},{16,32},{32,48},{48,0},{64,80},{80,96},{96,112},{112,64},{1... | collective-permute-start | bytes 786440 | tf_op jit(solution)/shard_map/ppermute | solution.py:240
  62.0 14.6 %collective-permute-start.19 = (bf16[2,2,2,128,128]{4,3,2,1,0:T(8,128)(2,1)S(1)}, bf16[2,2,2,128,128]{4,3,2,1,0:T(8,128)(2,1)S(1)}, u32[]{:S(2)}, u32[]{:S(2)}) collective-permute-start(bf16[2,2,2,128,128]{4,3,2,1,0:T(8,128)(2,1)S(1)} %get-tuple-element.92), channel_id=1, source_target_pairs={{0,32},{16,48},{32,0},{48,16},{64,96},{80,112},{96,64},{112,80},{1... | collective-permute-start | bytes 786440 | tf_op jit(solution)/shard_map/ppermute | solution.py:240
  63.9 17.8 %collective-permute-start.20 = (bf16[2,2,2,128,128]{4,3,2,1,0:T(8,128)(2,1)S(1)}, bf16[2,2,2,128,128]{4,3,2,1,0:T(8,128)(2,1)S(1)}, u32[]{:S(2)}, u32[]{:S(2)}) collective-permute-start(bf16[2,2,2,128,128]{4,3,2,1,0:T(8,128)(2,1)S(1)} %get-tuple-element.91), channel_id=1, source_target_pairs={{0,48},{16,0},{32,16},{48,32},{64,112},{80,64},{96,80},{112,96},{1... | collective-permute-start | bytes 786440 | tf_op jit(solution)/shard_map/ppermute | solution.py:240
  66.3 1.4 collective-permute-start.11
  67.8 65.4 %collective-permute-start.27 = (bf16[2,2,2,2,128,128]{5,4,3,2,1,0:T(8,128)(2,1)S(1)}, bf16[2,2,2,2,128,128]{5,4,3,2,1,0:T(8,128)(2,1)S(1)}, u32[]{:S(2)}, u32[]{:S(2)}) collective-permute-start(bf16[2,2,2,2,128,128]{5,4,3,2,1,0:T(8,128)(2,1)S(1)} %get-tuple-element.89), channel_id=1, source_target_pairs={{0,32},{16,48},{32,0},{48,16},{64,96},{80,112},{96,64},{112,80},{1... | collective-permute-start | bytes 1572872 | tf_op jit(solution)/shard_map/ppermute | solution.py:240
  69.7 29.6 %collective-permute-start.22 = (bf16[4,2,2,128,128]{4,3,2,1,0:T(8,128)(2,1)S(1)}, bf16[4,2,2,128,128]{4,3,2,1,0:T(8,128)(2,1)S(1)}, u32[]{:S(2)}, u32[]{:S(2)}) collective-permute-start(bf16[4,2,2,128,128]{4,3,2,1,0:T(8,128)(2,1)S(1)} %slice_bitcast_fusion), channel_id=1, source_target_pairs={{0,64},{16,80},{32,96},{48,112},{64,0},{80,16},{96,32},{112,48},{1... | collective-permute-start | bytes 1572872 | tf_op jit(solution)/shard_map/ppermute | solution.py:240
  76.7 24.9 %collective-permute-start.12 = (bf16[8,2,128,128]{3,2,1,0:T(8,128)(2,1)S(1)}, bf16[8,2,128,128]{3,2,1,0:T(8,128)(2,1)S(1)}, u32[]{:S(2)}, u32[]{:S(2)}) collective-permute-start(bf16[8,2,128,128]{3,2,1,0:T(8,128)(2,1)S(1)} %get-tuple-element.65), channel_id=1, source_target_pairs={{0,4},{1,5},{2,6},{3,7},{4,8},{5,9},{6,10},{7,11},{8,12},{9,13},{1... | collective-permute-start | bytes 1572872 | tf_op jit(solution)/shard_map/ppermute | solution.py:235
  81.7 7.8 %collective-permute-start.15 = (bf16[4,2,128,128]{3,2,1,0:T(8,128)(2,1)S(1)}, bf16[4,2,128,128]{3,2,1,0:T(8,128)(2,1)S(1)}, u32[]{:S(2)}, u32[]{:S(2)}) collective-permute-start(bf16[4,2,128,128]{3,2,1,0:T(8,128)(2,1)S(1)} %get-tuple-element.69), channel_id=1, source_target_pairs={{0,2},{1,3},{2,0},{3,1},{4,6},{5,7},{6,4},{7,5},{8,10},{9,11},{10,... | collective-permute-start | bytes 786440 | tf_op jit(solution)/shard_map/ppermute | solution.py:235
  89.5 6.5 %collective-permute-start.21 = (bf16[2,2,128,128]{3,2,1,0:T(8,128)(2,1)S(1)}, bf16[2,2,128,128]{3,2,1,0:T(8,128)(2,1)S(1)}, u32[]{:S(2)}, u32[]{:S(2)}) collective-permute-start(bf16[2,2,128,128]{3,2,1,0:T(8,128)(2,1)S(1)} %slice_bitcast_fusion.10), channel_id=1, source_target_pairs={{0,64},{16,80},{32,96},{48,112},{64,0},{80,16},{96,32},{112,48},{1... | collective-permute-start | bytes 393224 | tf_op jit(solution)/shard_map/ppermute | solution.py:240
  96.0 17.8 %collective-permute-start.13 = (bf16[8,2,128,128]{3,2,1,0:T(8,128)(2,1)S(1)}, bf16[8,2,128,128]{3,2,1,0:T(8,128)(2,1)S(1)}, u32[]{:S(2)}, u32[]{:S(2)}) collective-permute-start(bf16[8,2,128,128]{3,2,1,0:T(8,128)(2,1)S(1)} %get-tuple-element.66), channel_id=1, source_target_pairs={{0,12},{1,13},{2,14},{3,15},{4,0},{5,1},{6,2},{7,3},{8,4},{9,5},{1... | collective-permute-start | bytes 1572872 | tf_op jit(solution)/shard_map/ppermute | solution.py:235
  99.3 36.4 %collective-permute-start.28 = (bf16[2,2,2,2,128,128]{5,4,3,2,1,0:T(8,128)(2,1)S(1)}, bf16[2,2,2,2,128,128]{5,4,3,2,1,0:T(8,128)(2,1)S(1)}, u32[]{:S(2)}, u32[]{:S(2)}) collective-permute-start(bf16[2,2,2,2,128,128]{5,4,3,2,1,0:T(8,128)(2,1)S(1)} %get-tuple-element.88), channel_id=1, source_target_pairs={{0,48},{16,0},{32,16},{48,32},{64,112},{80,64},{96,80},{112,96},{1... | collective-permute-start | bytes 1572872 | tf_op jit(solution)/shard_map/ppermute | solution.py:240
  101.6 36.8 %collective-permute-start.16 = (bf16[4,2,128,128]{3,2,1,0:T(8,128)(2,1)S(1)}, bf16[4,2,128,128]{3,2,1,0:T(8,128)(2,1)S(1)}, u32[]{:S(2)}, u32[]{:S(2)}) collective-permute-start(bf16[4,2,128,128]{3,2,1,0:T(8,128)(2,1)S(1)} %add_convert_fusion.2), channel_id=1, source_target_pairs={{0,8},{1,9},{2,10},{3,11},{4,12},{5,13},{6,14},{7,15},{8,0},{9,1},... | collective-permute-start | bytes 786440 | tf_op jit(solution)/shard_map/ppermute | solution.py:235
  113.8 22.3 %collective-permute-start.23 = (bf16[2,2,128,128]{3,2,1,0:T(8,128)(2,1)S(1)}, bf16[2,2,128,128]{3,2,1,0:T(8,128)(2,1)S(1)}, u32[]{:S(2)}, u32[]{:S(2)}) collective-permute-start(bf16[2,2,128,128]{3,2,1,0:T(8,128)(2,1)S(1)} %get-tuple-element.97), channel_id=1, source_target_pairs={{0,16},{16,32},{32,48},{48,0},{64,80},{80,96},{96,112},{112,64},{1... | collective-permute-start | bytes 393224 | tf_op jit(solution)/shard_map/ppermute | solution.py:240
  121.5 15.8 %collective-permute-start.24 = (bf16[2,2,128,128]{3,2,1,0:T(8,128)(2,1)S(1)}, bf16[2,2,128,128]{3,2,1,0:T(8,128)(2,1)S(1)}, u32[]{:S(2)}, u32[]{:S(2)}) collective-permute-start(bf16[2,2,128,128]{3,2,1,0:T(8,128)(2,1)S(1)} %get-tuple-element.99), channel_id=1, source_target_pairs={{0,32},{16,48},{32,0},{48,16},{64,96},{80,112},{96,64},{112,80},{1... | collective-permute-start | bytes 393224 | tf_op jit(solution)/shard_map/ppermute | solution.py:240
  133.1 5.2 %collective-permute-start.25 = (bf16[2,2,128,128]{3,2,1,0:T(8,128)(2,1)S(1)}, bf16[2,2,128,128]{3,2,1,0:T(8,128)(2,1)S(1)}, u32[]{:S(2)}, u32[]{:S(2)}) collective-permute-start(bf16[2,2,128,128]{3,2,1,0:T(8,128)(2,1)S(1)} %get-tuple-element.98), channel_id=1, source_target_pairs={{0,48},{16,0},{32,16},{48,32},{64,112},{80,64},{96,80},{112,96},{1... | collective-permute-start | bytes 393224 | tf_op jit(solution)/shard_map/ppermute | solution.py:240
  135.8 8.1 %collective-permute-start.14 = (bf16[4,2,128,128]{3,2,1,0:T(8,128)(2,1)S(1)}, bf16[4,2,128,128]{3,2,1,0:T(8,128)(2,1)S(1)}, u32[]{:S(2)}, u32[]{:S(2)}) collective-permute-start(bf16[4,2,128,128]{3,2,1,0:T(8,128)(2,1)S(1)} %add_convert_fusion.3), channel_id=1, source_target_pairs={{0,2},{1,3},{2,0},{3,1},{4,6},{5,7},{6,4},{7,5},{8,10},{9,11},{10,... | collective-permute-start | bytes 786440 | tf_op jit(solution)/shard_map/ppermute | solution.py:235
  136.2 8.0 %collective-permute-start.29 = (bf16[2,2,2,128,128]{4,3,2,1,0:T(8,128)(2,1)S(1)}, bf16[2,2,2,128,128]{4,3,2,1,0:T(8,128)(2,1)S(1)}, u32[]{:S(2)}, u32[]{:S(2)}) collective-permute-start(bf16[2,2,2,128,128]{4,3,2,1,0:T(8,128)(2,1)S(1)} %get-tuple-element.95), channel_id=1, source_target_pairs={{0,1},{1,0},{2,3},{3,2},{4,5},{5,4},{6,7},{7,6},{8,9},{9,8},{10,11... | collective-permute-start | bytes 786440 | tf_op jit(solution)/shard_map/ppermute | solution.py:235
  137.3 10.1 %collective-permute-start.30 = (bf16[2,2,2,128,128]{4,3,2,1,0:T(8,128)(2,1)S(1)}, bf16[2,2,2,128,128]{4,3,2,1,0:T(8,128)(2,1)S(1)}, u32[]{:S(2)}, u32[]{:S(2)}) collective-permute-start(bf16[2,2,2,128,128]{4,3,2,1,0:T(8,128)(2,1)S(1)} %get-tuple-element.96), channel_id=1, source_target_pairs={{0,65},{1,64},{2,67},{3,66},{4,69},{5,68},{6,71},{7,70},{8,73},{9,... | collective-permute-start | bytes 786440 | tf_op jit(solution)/shard_map/ppermute | solution.py:248
  144.1 4.8 %collective-permute-start.17 = (bf16[2,2,128,128]{3,2,1,0:T(8,128)(2,1)S(1)}, bf16[2,2,128,128]{3,2,1,0:T(8,128)(2,1)S(1)}, u32[]{:S(2)}, u32[]{:S(2)}) collective-permute-start(bf16[2,2,128,128]{3,2,1,0:T(8,128)(2,1)S(1)} %get-tuple-element.100), channel_id=1, source_target_pairs={{0,1},{1,0},{2,3},{3,2},{4,5},{5,4},{6,7},{7,6},{8,9},{9,8},{10,11... | collective-permute-start | bytes 393224 | tf_op jit(solution)/shard_map/ppermute | solution.py:235
  (3 other events, 6.0 us)
